TPU v7x, 128 devices: a whole 4x4x4 slice. The times are simulated.
128 devices in a mesh: seq: 32 (over y, x, core), exp: 4 (over z).
Axes of the slice: x: 4, y: 4, z: 4, core: 2. Of those that a mesh axis runs over, the one named last changes fastest.
Arguments:
- qk_proj: bfloat16 [4096, 2, 2048], P('seq', None, 'exp'), may hold values from -6 to 6
- v_proj: bfloat16 [4096, 4096], P('seq', 'exp'), may hold values from -6 to 6
- z_proj: bfloat16 [4096, 4096], P('seq', 'exp'), may hold values from -6 to 6
- conv_qk: float32 [4, 2, 2048], P(None, None, 'exp'), may hold values from -3 to 3
- conv_v: float32 [4, 4096], P(None, 'exp'), may hold values from -3 to 3
- decay_log: float32 [32, 4096], P('exp', 'seq'), may hold values from -2 to 0
- beta_gate: float32 [32, 4096], P('exp', 'seq'), may hold values from 0.05 to 0.95
- doc_ids: int32 [4096], replicated, may hold values from 0 to 31, never falling along the last dimension, each value on 1 to 1024 neighbouring positions
- head_gain: float32 [128], replicated, may hold values from 0.1 to 1.9
- out_weight: bfloat16 [4096, 2048], P('exp'), may hold values from -0.09375 to 0.09375
- residual: bfloat16 [4096, 2048], P(('seq', 'exp')), may hold values from -6 to 6
- post_gain: float32 [2048], replicated, may hold values from 0.1 to 1.9
- route_ids: int32 [4096, 10], P(('seq', 'exp')), may hold values from 0 to 255, all different within a row; in each aligned block of 32 rows (0 to 31, 32 to 63, ...) at most 2 rows name the same one
- route_weight: float32 [4096, 10], P(('seq', 'exp')), may hold values from 0.02 to 0.3
- expert_gate_up: bfloat16 [256, 2, 2048, 512], P(('seq', 'exp')), may hold values from -0.125 to 0.125
- expert_down: bfloat16 [256, 512, 2048], P(('seq', 'exp')), may hold values from -0.25 to 0.25
- shared_gate_up: bfloat16 [2, 2048, 512], replicated, may hold values from -0.125 to 0.125
- shared_down: bfloat16 [512, 2048], replicated, may hold values from -0.25 to 0.25
- shared_gate: float32 [2048], replicated, may hold values from -0.125 to 0.125
Outputs:
- hidden_mid: bfloat16 [4096, 2048], P(('seq', 'exp'))
- moe_out: bfloat16 [4096, 2048], P(('seq', 'exp'))
Inputs may be any that keep to these rules, and one draw needn't show every extreme that they name: `route_ids`: each row names 10 different experts. In each aligned block of 32 rows (the rows of one device) no expert is named by more than 2 rows, and in some blocks an expert is named by exactly 2 rows. `doc_ids`: document numbers never fall along the stream; each document covers 1 to 1024 tokens, and one covers exactly 1024.
All inputs are finite; a program needn't handle non-finite values.
Results may differ from a plain program's by a relative error of at most 0.0075.
Values may be sent and summed in bfloat16 or wider, within the bound.
No kernel may reach another device: no remote copies, remote signals or barrier semaphores. Data moves between devices by JAX's collectives and lax.ppermute only.
A program may use at most 128 MiB of HBM per device.

v0:
```python
import jax
import jax.numpy as jnp
from jax import lax
from jax.sharding import PartitionSpec as P

GROUP = 64


exact_result = lax.Precision.HIGHEST


def shifted(value, axis, by):
    peers = lax.axis_size(axis)
    pairs = [(i, i + by) for i in range(peers) if 0 <= i + by < peers]
    return lax.ppermute(value, axis, pairs)


def causal_conv(extended, weight, doc_window):
    kernel_len = weight.shape[0]
    length = extended.shape[0] - kernel_len + 1
    own_doc = doc_window[kernel_len - 1 :]
    summed = jnp.zeros((length,) + extended.shape[1:], jnp.float32)
    for tap_index in range(kernel_len):
        same_doc = (doc_window[tap_index : tap_index + length] == own_doc).astype(jnp.float32)
        same_doc = same_doc.reshape((length,) + (1,) * (extended.ndim - 1))
        summed = summed + weight[tap_index] * (
            extended[tap_index : tap_index + length].astype(jnp.float32) * same_doc
        )
    return jax.nn.silu(summed)


def prepare(qk_conv, v_conv, decay_log, beta_gate, doc_window, block_len):
    length = v_conv.shape[0]
    head_count = decay_log.shape[0]
    key_heads = head_count // 2
    key_dim = qk_conv.shape[2] // key_heads
    value_dim = v_conv.shape[1] // head_count
    split_qk = qk_conv.reshape(length, 2, key_heads, key_dim)
    unit_qk = split_qk * lax.rsqrt(jnp.sum(split_qk * split_qk, axis=-1, keepdims=True) + 1e-06)
    blocks = length // block_len

    def heads_first(tensor):
        return jnp.transpose(tensor, (1, 0, 2)).reshape(
            head_count, blocks, block_len, tensor.shape[2]
        )

    queries = heads_first(jnp.repeat(unit_qk[:, 0], 2, axis=1) * key_dim ** (-0.5))
    key_vecs = heads_first(jnp.repeat(unit_qk[:, 1], 2, axis=1))
    values = heads_first(v_conv.reshape(length, head_count, value_dim))
    decays = decay_log.reshape(head_count, blocks, block_len)
    rates = beta_gate.reshape(head_count, blocks, block_len)
    kernel_len = doc_window.shape[0] - length + 1
    seg_block = doc_window[kernel_len - 1 :].reshape(blocks, block_len)
    seg_before = doc_window[kernel_len - 2 : kernel_len - 2 + length : block_len]
    return (queries, key_vecs, values, decays, rates, seg_block, seg_before)


def delta_blocks(queries, key_vecs, values, decays, rates, seg_block, seg_before):
    block_len = key_vecs.shape[2]
    value_dim = values.shape[3]
    cum_decay = jnp.cumsum(decays, axis=-1)
    lower_incl = jnp.tril(jnp.ones((block_len, block_len), dtype=bool))
    strict_lower = jnp.tril(jnp.ones((block_len, block_len), dtype=bool), -1)
    same_doc = seg_block[:, :, None] == seg_block[:, None, :]
    keep_mask = same_doc & lower_incl
    spread = cum_decay[..., :, None] - cum_decay[..., None, :]
    within = jnp.exp(jnp.where(keep_mask, spread, 0.0)) * keep_mask
    carried = jnp.exp(cum_decay) * (seg_block == seg_before[:, None])
    key_dots = jnp.einsum("hnik,hnjk->hnij", key_vecs, key_vecs, precision=exact_result)
    system = (
        jnp.eye(block_len, dtype=jnp.float32)
        + rates[..., :, None] * within * key_dots * strict_lower
    )
    right_sides = jnp.concatenate(
        [rates[..., None] * values, (rates * carried)[..., None] * key_vecs], axis=-1
    )
    solved = jax.scipy.linalg.solve_triangular(system, right_sides, lower=True, unit_diagonal=True)
    new_values = solved[..., :value_dim]
    key_weights = solved[..., value_dim:]
    scores = jnp.einsum("hnik,hnjk->hnij", queries, key_vecs, precision=exact_result) * within
    out_local = jnp.einsum("hnij,hnjv->hniv", scores, new_values, precision=exact_result)
    query_eff = carried[..., None] * queries - jnp.einsum(
        "hnij,hnjk->hnik", scores, key_weights, precision=exact_result
    )
    end_keys = within[..., -1, :][..., None] * key_vecs
    transit = carried[..., -1][..., None, None] * jnp.eye(
        key_vecs.shape[3], dtype=jnp.float32
    ) - jnp.einsum("hnjk,hnjl->hnkl", end_keys, key_weights, precision=exact_result)
    offset = jnp.einsum("hnjk,hnjv->hnkv", end_keys, new_values, precision=exact_result)
    return (out_local, query_eff, transit, offset)


def run_blocks(query_eff, out_local, transit, offset, start_state):

    def advance(current_state, pieces):
        effective_query, local_output, permute_matrix, beta_matrix = pieces
        layer_output = (
            jnp.einsum("mjw,mwq->mjq", effective_query, current_state, precision=exact_result)
            + local_output
        )
        following_state = (
            jnp.einsum("jyu,jug->jyg", permute_matrix, current_state, precision=exact_result)
            + beta_matrix
        )
        return (following_state, layer_output)

    stacked = (
        jnp.moveaxis(query_eff, 1, 0),
        jnp.moveaxis(out_local, 1, 0),
        jnp.moveaxis(transit, 1, 0),
        jnp.moveaxis(offset, 1, 0),
    )
    last_state, outputs = lax.scan(advance, start_state, stacked)
    return outputs


def gated_norm(outputs, z_proj, head_gain):
    blocks, head_count, block_len, value_dim = outputs.shape
    attn_heads = jnp.transpose(outputs, (0, 2, 1, 3)).reshape(
        blocks * block_len, head_count, value_dim
    )
    gate_z = z_proj.reshape(blocks * block_len, head_count, value_dim).astype(jnp.float32)
    scaled = (
        attn_heads
        * lax.rsqrt(jnp.mean(attn_heads * attn_heads, axis=-1, keepdims=True) + 1e-06)
        * head_gain
        * jax.nn.silu(gate_z)
    )
    return scaled.reshape(blocks * block_len, head_count * value_dim).astype(jnp.bfloat16)


def rms_scale(hidden, gain):
    return (
        hidden * lax.rsqrt(jnp.mean(hidden * hidden, axis=-1, keepdims=True) + 1e-06) * gain
    ).astype(jnp.bfloat16)


def compose(initial_mapping, secondary_mapping):
    return (
        jnp.einsum(
            "hkl,hlm->hkm", secondary_mapping[0], initial_mapping[0], precision=exact_result
        ),
        jnp.einsum("jyu,jug->jyg", secondary_mapping[0], initial_mapping[1], precision=exact_result)
        + secondary_mapping[1],
    )


def experts_apply(received, expert_gate_up, expert_down):
    gate_up = jnp.einsum(
        "secd,ezdf->zsecf", received, expert_gate_up, preferred_element_type=jnp.float32
    )
    activated = (jax.nn.silu(gate_up[0]) * gate_up[1]).astype(jnp.bfloat16)
    return jnp.einsum(
        "secf,efd->secd", activated, expert_down, preferred_element_type=jnp.float32
    ).astype(jnp.bfloat16)


def shards(
    qk_proj,
    v_proj,
    z_proj,
    conv_qk,
    conv_v,
    decay_log,
    beta_gate,
    doc_ids,
    head_gain,
    out_weight,
    residual,
    post_gain,
    route_ids,
    route_weight,
    expert_gate_up,
    expert_down,
    shared_gate_up,
    shared_down,
    shared_gate,
):
    kernel_len = conv_qk.shape[0]
    length = qk_proj.shape[0]
    key_cols = qk_proj.shape[2]
    flat_qk = qk_proj.reshape(length, 2 * key_cols)
    rim_send = jnp.concatenate(
        [flat_qk[length - kernel_len + 1 :], v_proj[length - kernel_len + 1 :]], axis=1
    )
    rim_recv = shifted(rim_send, "seq", 1)
    doc_pad = jnp.concatenate([jnp.full((kernel_len - 1,), -1, jnp.int32), doc_ids])
    doc_window = lax.dynamic_slice_in_dim(
        doc_pad, lax.axis_index("seq") * length, length + kernel_len - 1
    )
    qk_ext = jnp.concatenate(
        [rim_recv[:, : 2 * key_cols].reshape(kernel_len - 1, 2, key_cols), qk_proj], axis=0
    )
    v_ext = jnp.concatenate([rim_recv[:, 2 * key_cols :], v_proj], axis=0)
    qk_conv = causal_conv(qk_ext, conv_qk, doc_window)
    v_conv = causal_conv(v_ext, conv_v, doc_window)
    queries, key_vecs, values, decays, rates, seg_block, seg_before = prepare(
        qk_conv, v_conv, decay_log, beta_gate, doc_window, GROUP
    )
    out_local, query_eff, transit, offset = delta_blocks(
        queries, key_vecs, values, decays, rates, seg_block, seg_before
    )
    head_count = transit.shape[0]
    key_dim = transit.shape[2]
    identity = jnp.broadcast_to(jnp.eye(key_dim, dtype=jnp.float32), (head_count, key_dim, key_dim))
    zero_state = jnp.zeros((head_count, key_dim, offset.shape[3]), jnp.float32)

    def fold_block(carried_map, pieces):
        return (compose(carried_map, pieces), None)

    device_map, unused = lax.scan(
        fold_block,
        (identity, zero_state),
        (jnp.moveaxis(transit, 1, 0), jnp.moveaxis(offset, 1, 0)),
    )
    device_transfer, device_offset = device_map

    def relay_step(turn_index, arriving_rows):
        advanced_state = (
            jnp.einsum("jyu,jug->jyg", device_transfer, arriving_rows, precision=exact_result)
            + device_offset
        )
        return shifted(advanced_state, "seq", 1)

    start_state = lax.fori_loop(0, lax.axis_size("seq") - 1, relay_step, zero_state)
    outputs = run_blocks(query_eff, out_local, transit, offset, start_state)
    gated = gated_norm(outputs, z_proj, head_gain)
    attn_part = lax.psum_scatter(
        jnp.dot(gated, out_weight, preferred_element_type=jnp.float32),
        "exp",
        scatter_dimension=0,
        tiled=True,
    )
    hidden = residual.astype(jnp.float32) + attn_part
    normed = rms_scale(hidden, post_gain)
    row_count = normed.shape[0]
    model_width = normed.shape[1]
    top_count = route_ids.shape[1]
    exp_dev = expert_down.shape[0]
    seq_count = lax.axis_size("seq")
    exp_count = lax.axis_size("exp")
    experts_all = exp_dev * seq_count * exp_count
    capacity = max(2, (row_count * top_count * 8 + 5 * experts_all - 1) // (5 * experts_all))
    pair_total = row_count * top_count
    flat_ids = route_ids.reshape(-1)
    pair_index = jnp.arange(pair_total, dtype=jnp.int32)
    earlier = (flat_ids[:, None] == flat_ids[None, :]) & (pair_index[None, :] < pair_index[:, None])
    slot_rank = jnp.sum(earlier.astype(jnp.int32), axis=1)
    dest_slot = flat_ids * capacity + slot_rank
    send_rows = (
        jnp.zeros((experts_all * capacity, model_width), jnp.bfloat16)
        .at[dest_slot]
        .set(jnp.repeat(normed, top_count, axis=0))
    )
    send_four = send_rows.reshape(seq_count * exp_count, exp_dev, capacity, model_width)
    returned = lax.all_to_all(
        experts_apply(
            lax.all_to_all(send_four, ("seq", "exp"), split_axis=0, concat_axis=0, tiled=True),
            expert_gate_up,
            expert_down,
        ),
        ("seq", "exp"),
        split_axis=0,
        concat_axis=0,
        tiled=True,
    )
    picked = returned.reshape(experts_all * capacity, model_width)[dest_slot].reshape(
        row_count, top_count, model_width
    )
    weighted = jnp.sum(route_weight[..., None] * picked.astype(jnp.float32), axis=1)
    shared_both = jnp.einsum(
        "rd,zdf->zrf", normed, shared_gate_up, preferred_element_type=jnp.float32
    )
    shared_act = (jax.nn.silu(shared_both[0]) * shared_both[1]).astype(jnp.bfloat16)
    shared_branch = jnp.dot(shared_act, shared_down, preferred_element_type=jnp.float32)
    shared_scale = jax.nn.sigmoid(
        jnp.dot(normed.astype(jnp.float32), shared_gate, precision=exact_result)
    )
    moe_sum = weighted + shared_scale[:, None] * shared_branch
    return (hidden.astype(jnp.bfloat16), moe_sum.astype(jnp.bfloat16))


def solution(mesh):
    placed = (
        P("seq", None, "exp"),
        P("seq", "exp"),
        P("seq", "exp"),
        P(None, None, "exp"),
        P(None, "exp"),
        P("exp", "seq"),
        P("exp", "seq"),
        P(),
        P(),
        P("exp", None),
        P(("seq", "exp"), None),
        P(),
        P(("seq", "exp"), None),
        P(("seq", "exp"), None),
        P(("seq", "exp"), None, None, None),
        P(("seq", "exp"), None, None),
        P(),
        P(),
        P(),
    )
    return jax.shard_map(
        shards,
        mesh=mesh,
        in_specs=placed,
        out_specs=(P(("seq", "exp"), None), P(("seq", "exp"), None)),
        check_vma=False,
    )
```

profile of v0, /device:TPU:1, one launch (start us, length us, event | category | flops | bytes accessed | tf_op | source)
XLA Modules:
  0.0 788.0 jit_solution(1686956589357551504)
XLA Ops:
  33.3 80.0 %custom-call.4 = f32[8,2,1,64,64]{3,4,2,1,0:T(8,128)} custom-call(f32[8,2,1,64,64]{4,3,2,1,0:T(8,128)} %fusion.43), custom_call_target="InvertDiagBlocksLowerTriangular" | custom-call | tf_op jit(solution)/shard_map/jit(_solve_triangular)/vmap(vmap())/triangular_solve | solution.py:77
  125.7 10.2 %while.37 = (s32[]{:T(128)}, f32[8,128,128]{2,1,0:T(8,128)}, f32[8,128,128]{2,1,0:T(8,128)}, f32[2,8,128,128]{3,2,1,0:T(8,128)S(1)}, f32[2,8,128,128]{3,2,1,0:T(8,128)}, /*index=5*/s32[]{:T(128)}, s32[]{:T(128)}) while((s32[]{:T(128)}, f32[8,128,128]{2,1,0:T(8,128)}, f32[8,128,128]{2,1,0:T(8,128)}, ...), condition=%wide.region_3.4_spmd.clone, body=%wide.region_2.3_spmd.clone.sunk | while | flops 402915328 | bytes 7865463 | solution.py:211
  136.8 445.4 %while.35 = (s32[]{:T(128)}, f32[8,128,128]{2,1,0:T(8,128)}, f32[8,128,128]{2,1,0:T(8,128)}, f32[8,128,128]{2,1,0:T(8,128)}, s32[]{:T(128)}) while((s32[]{:T(128)}, f32[8,128,128]{2,1,0:T(8,128)}, f32[8,128,128]{2,1,0:T(8,128)}, f32[8,128,128]{2,1,0:T(8,128)}, s32[]{:T(128)}) %tuple.81), condition=%wide.region_5.6_spmd, body=%wide.region_4.5_spmd.sunk | while | flops 201457664 | bytes 4194405 | solution.py:225
  168.7 6.4 collective-permute-done
  182.3 6.4 collective-permute-done
  209.4 6.4 collective-permute-done
  236.6 6.4 collective-permute-done
  277.4 6.4 collective-permute-done
  304.6 6.4 collective-permute-done
  331.8 6.4 collective-permute-done
  358.9 6.4 collective-permute-done
  372.5 6.4 collective-permute-done
  387.4 6.4 collective-permute-done
  396.6 6.5 collective-permute-start
  412.3 6.5 collective-permute-start
  428.0 6.5 collective-permute-start
  443.7 6.5 collective-permute-start
  459.4 6.5 collective-permute-start
  465.9 6.4 collective-permute-done
  475.1 6.5 collective-permute-start
  481.6 6.4 collective-permute-done
  490.8 6.5 collective-permute-start
  506.5 6.5 collective-permute-start
  522.2 6.5 collective-permute-start
  537.9 6.5 collective-permute-start
  553.6 6.5 collective-permute-start
  569.3 6.5 collective-permute-start
  582.2 9.8 %while.36 = (s32[]{:T(128)}, f32[8,128,128]{2,1,0:T(8,128)}, f32[2,8,64,128]{3,2,1,0:T(8,128)}, f32[2,8,128,128]{3,2,1,0:T(8,128)S(1)}, f32[2,8,128,128]{3,2,1,0...) while((s32[]{:T(128)}, f32[8,128,128]{2,1,0:T(8,128)}, ...), condition=%wide.region_7.8_spmd, body=%wide.region_6.7_spmd.sunk | while | flops 302186496 | bytes 8652913 | solution.py:113
  599.8 61.4 %reduce-scatter.2.cloned.1.call-done = f32[32,2048]{1,0:T(8,128)} async-done(((f32[128,2048]{1,0:T(8,128)}), f32[32,2048]{1,0:T(8,128)}) %reduce-scatter.2.cloned.1.call-update) | async-done | bytes 262160 | tf_op jit(solution)/shard_map/reduce_scatter | solution.py:228
  676.6 39.9 %all_to_all.10 = bf16[128,2,2,2048]{3,2,1,0:T(2,128)(2,1)S(1)} all-to-all(bf16[128,2,2,2048]{3,2,1,0:T(2,128)(2,1)} %reshape.235), channel_id=1, replica_groups=mesh['seq'=32,'exp'=4] {'seq','exp'}, dimensions={0} | all-to-all | bytes 4194304 | tf_op jit(solution)/shard_map/all_to_all | solution.py:258
  716.5 7.3 fusion.32
  738.9 25.0 %all-to-all-done.1 = bf16[128,2,2,2048]{3,2,1,0:T(2,128)(2,1)} async-done(((bf16[128,2,2,2048]{3,2,1,0:T(2,128)(2,1)}), bf16[128,2,2,2048]{3,2,1,0:T(2,128)(2,1)}, u32[]{:S(2)}, u32[]{:S(2)}) %all-to-all-start.1) | async-done | bytes 2097184 | tf_op jit(solution)/shard_map/all_to_all | solution.py:256
  (249 shorter events, 404.5 us)
Async XLA Ops:
  7.2 654.1 %reduce-scatter.2.cloned.1.call-start = ((), (), s32[]{:S(2)}) async-start(), calls=%async_computation.3 | async-start | bytes 1310720 | tf_op jit(solution)/shard_map/reduce_scatter | solution.py:228
  8.8 14.9 %collective-permute-start.1 = (bf16[3,2048]{1,0:T(4,128)(2,1)S(1)}, bf16[3,2048]{1,0:T(4,128)(2,1)S(1)}, u32[]{:S(2)}, u32[]{:S(2)}) collective-permute-start(bf16[3,2048]{1,0:T(4,128)(2,1)S(1)} %pad_maximum_fusion.1), channel_id=1, source_target_pairs={{0,4},{4,8},{8,12},{12,16},{16,20},{20,24},{24,28},{28,32},{32,36}... | collective-permute-start | bytes 36872 | tf_op jit(solution)/shard_map/ppermute | solution.py:15
  150.7 10.8 %collective-permute-start = (f32[8,128,128]{2,1,0:T(8,128)}, f32[8,128,128]{2,1,0:T(8,128)}, u32[]{:S(2)}, u32[]{:S(2)}) collective-permute-start(f32[8,128,128]{2,1,0:T(8,128)} %convolution_add_fusion.7), channel_id=1, source_target_pairs={{0,4},{4,8},{8,12},{12,16},{16,20},{20,24},{24,28},{28,32},{32,36}... | collective-permute-start | bytes 1572872 | tf_op jit(solution)/shard_map/while/body/eval_jaxpr/ppermute | solution.py:15
  164.3 10.8 %collective-permute-start = (f32[8,128,128]{2,1,0:T(8,128)}, f32[8,128,128]{2,1,0:T(8,128)}, u32[]{:S(2)}, u32[]{:S(2)}) collective-permute-start(f32[8,128,128]{2,1,0:T(8,128)} %convolution_add_fusion.7), channel_id=1, source_target_pairs={{0,4},{4,8},{8,12},{12,16},{16,20},{20,24},{24,28},{28,32},{32,36}... | collective-permute-start | bytes 1572872 | tf_op jit(solution)/shard_map/while/body/eval_jaxpr/ppermute | solution.py:15
  177.9 10.8 %collective-permute-start = (f32[8,128,128]{2,1,0:T(8,128)}, f32[8,128,128]{2,1,0:T(8,128)}, u32[]{:S(2)}, u32[]{:S(2)}) collective-permute-start(f32[8,128,128]{2,1,0:T(8,128)} %convolution_add_fusion.7), channel_id=1, source_target_pairs={{0,4},{4,8},{8,12},{12,16},{16,20},{20,24},{24,28},{28,32},{32,36}... | collective-permute-start | bytes 1572872 | tf_op jit(solution)/shard_map/while/body/eval_jaxpr/ppermute | solution.py:15
  191.5 10.8 %collective-permute-start = (f32[8,128,128]{2,1,0:T(8,128)}, f32[8,128,128]{2,1,0:T(8,128)}, u32[]{:S(2)}, u32[]{:S(2)}) collective-permute-start(f32[8,128,128]{2,1,0:T(8,128)} %convolution_add_fusion.7), channel_id=1, source_target_pairs={{0,4},{4,8},{8,12},{12,16},{16,20},{20,24},{24,28},{28,32},{32,36}... | collective-permute-start | bytes 1572872 | tf_op jit(solution)/shard_map/while/body/eval_jaxpr/ppermute | solution.py:15
  205.0 10.8 %collective-permute-start = (f32[8,128,128]{2,1,0:T(8,128)}, f32[8,128,128]{2,1,0:T(8,128)}, u32[]{:S(2)}, u32[]{:S(2)}) collective-permute-start(f32[8,128,128]{2,1,0:T(8,128)} %convolution_add_fusion.7), channel_id=1, source_target_pairs={{0,4},{4,8},{8,12},{12,16},{16,20},{20,24},{24,28},{28,32},{32,36}... | collective-permute-start | bytes 1572872 | tf_op jit(solution)/shard_map/while/body/eval_jaxpr/ppermute | solution.py:15
  218.6 10.8 %collective-permute-start = (f32[8,128,128]{2,1,0:T(8,128)}, f32[8,128,128]{2,1,0:T(8,128)}, u32[]{:S(2)}, u32[]{:S(2)}) collective-permute-start(f32[8,128,128]{2,1,0:T(8,128)} %convolution_add_fusion.7), channel_id=1, source_target_pairs={{0,4},{4,8},{8,12},{12,16},{16,20},{20,24},{24,28},{28,32},{32,36}... | collective-permute-start | bytes 1572872 | tf_op jit(solution)/shard_map/while/body/eval_jaxpr/ppermute | solution.py:15
  232.2 10.8 %collective-permute-start = (f32[8,128,128]{2,1,0:T(8,128)}, f32[8,128,128]{2,1,0:T(8,128)}, u32[]{:S(2)}, u32[]{:S(2)}) collective-permute-start(f32[8,128,128]{2,1,0:T(8,128)} %convolution_add_fusion.7), channel_id=1, source_target_pairs={{0,4},{4,8},{8,12},{12,16},{16,20},{20,24},{24,28},{28,32},{32,36}... | collective-permute-start | bytes 1572872 | tf_op jit(solution)/shard_map/while/body/eval_jaxpr/ppermute | solution.py:15
  245.8 10.8 %collective-permute-start = (f32[8,128,128]{2,1,0:T(8,128)}, f32[8,128,128]{2,1,0:T(8,128)}, u32[]{:S(2)}, u32[]{:S(2)}) collective-permute-start(f32[8,128,128]{2,1,0:T(8,128)} %convolution_add_fusion.7), channel_id=1, source_target_pairs={{0,4},{4,8},{8,12},{12,16},{16,20},{20,24},{24,28},{28,32},{32,36}... | collective-permute-start | bytes 1572872 | tf_op jit(solution)/shard_map/while/body/eval_jaxpr/ppermute | solution.py:15
  259.4 10.8 %collective-permute-start = (f32[8,128,128]{2,1,0:T(8,128)}, f32[8,128,128]{2,1,0:T(8,128)}, u32[]{:S(2)}, u32[]{:S(2)}) collective-permute-start(f32[8,128,128]{2,1,0:T(8,128)} %convolution_add_fusion.7), channel_id=1, source_target_pairs={{0,4},{4,8},{8,12},{12,16},{16,20},{20,24},{24,28},{28,32},{32,36}... | collective-permute-start | bytes 1572872 | tf_op jit(solution)/shard_map/while/body/eval_jaxpr/ppermute | solution.py:15
  273.0 10.8 %collective-permute-start = (f32[8,128,128]{2,1,0:T(8,128)}, f32[8,128,128]{2,1,0:T(8,128)}, u32[]{:S(2)}, u32[]{:S(2)}) collective-permute-start(f32[8,128,128]{2,1,0:T(8,128)} %convolution_add_fusion.7), channel_id=1, source_target_pairs={{0,4},{4,8},{8,12},{12,16},{16,20},{20,24},{24,28},{28,32},{32,36}... | collective-permute-start | bytes 1572872 | tf_op jit(solution)/shard_map/while/body/eval_jaxpr/ppermute | solution.py:15
  286.6 10.8 %collective-permute-start = (f32[8,128,128]{2,1,0:T(8,128)}, f32[8,128,128]{2,1,0:T(8,128)}, u32[]{:S(2)}, u32[]{:S(2)}) collective-permute-start(f32[8,128,128]{2,1,0:T(8,128)} %convolution_add_fusion.7), channel_id=1, source_target_pairs={{0,4},{4,8},{8,12},{12,16},{16,20},{20,24},{24,28},{28,32},{32,36}... | collective-permute-start | bytes 1572872 | tf_op jit(solution)/shard_map/while/body/eval_jaxpr/ppermute | solution.py:15
  300.2 10.8 %collective-permute-start = (f32[8,128,128]{2,1,0:T(8,128)}, f32[8,128,128]{2,1,0:T(8,128)}, u32[]{:S(2)}, u32[]{:S(2)}) collective-permute-start(f32[8,128,128]{2,1,0:T(8,128)} %convolution_add_fusion.7), channel_id=1, source_target_pairs={{0,4},{4,8},{8,12},{12,16},{16,20},{20,24},{24,28},{28,32},{32,36}... | collective-permute-start | bytes 1572872 | tf_op jit(solution)/shard_map/while/body/eval_jaxpr/ppermute | solution.py:15
  313.8 10.8 %collective-permute-start = (f32[8,128,128]{2,1,0:T(8,128)}, f32[8,128,128]{2,1,0:T(8,128)}, u32[]{:S(2)}, u32[]{:S(2)}) collective-permute-start(f32[8,128,128]{2,1,0:T(8,128)} %convolution_add_fusion.7), channel_id=1, source_target_pairs={{0,4},{4,8},{8,12},{12,16},{16,20},{20,24},{24,28},{28,32},{32,36}... | collective-permute-start | bytes 1572872 | tf_op jit(solution)/shard_map/while/body/eval_jaxpr/ppermute | solution.py:15
  327.4 10.8 %collective-permute-start = (f32[8,128,128]{2,1,0:T(8,128)}, f32[8,128,128]{2,1,0:T(8,128)}, u32[]{:S(2)}, u32[]{:S(2)}) collective-permute-start(f32[8,128,128]{2,1,0:T(8,128)} %convolution_add_fusion.7), channel_id=1, source_target_pairs={{0,4},{4,8},{8,12},{12,16},{16,20},{20,24},{24,28},{28,32},{32,36}... | collective-permute-start | bytes 1572872 | tf_op jit(solution)/shard_map/while/body/eval_jaxpr/ppermute | solution.py:15
  341.0 10.8 %collective-permute-start = (f32[8,128,128]{2,1,0:T(8,128)}, f32[8,128,128]{2,1,0:T(8,128)}, u32[]{:S(2)}, u32[]{:S(2)}) collective-permute-start(f32[8,128,128]{2,1,0:T(8,128)} %convolution_add_fusion.7), channel_id=1, source_target_pairs={{0,4},{4,8},{8,12},{12,16},{16,20},{20,24},{24,28},{28,32},{32,36}... | collective-permute-start | bytes 1572872 | tf_op jit(solution)/shard_map/while/body/eval_jaxpr/ppermute | solution.py:15
  354.5 10.8 %collective-permute-start = (f32[8,128,128]{2,1,0:T(8,128)}, f32[8,128,128]{2,1,0:T(8,128)}, u32[]{:S(2)}, u32[]{:S(2)}) collective-permute-start(f32[8,128,128]{2,1,0:T(8,128)} %convolution_add_fusion.7), channel_id=1, source_target_pairs={{0,4},{4,8},{8,12},{12,16},{16,20},{20,24},{24,28},{28,32},{32,36}... | collective-permute-start | bytes 1572872 | tf_op jit(solution)/shard_map/while/body/eval_jaxpr/ppermute | solution.py:15
  381.7 12.1 %collective-permute-start = (f32[8,128,128]{2,1,0:T(8,128)}, f32[8,128,128]{2,1,0:T(8,128)}, u32[]{:S(2)}, u32[]{:S(2)}) collective-permute-start(f32[8,128,128]{2,1,0:T(8,128)} %convolution_add_fusion.7), channel_id=1, source_target_pairs={{0,4},{4,8},{8,12},{12,16},{16,20},{20,24},{24,28},{28,32},{32,36}... | collective-permute-start | bytes 1572872 | tf_op jit(solution)/shard_map/while/body/eval_jaxpr/ppermute | solution.py:15
  396.6 12.9 %collective-permute-start = (f32[8,128,128]{2,1,0:T(8,128)}, f32[8,128,128]{2,1,0:T(8,128)}, u32[]{:S(2)}, u32[]{:S(2)}) collective-permute-start(f32[8,128,128]{2,1,0:T(8,128)} %convolution_add_fusion.7), channel_id=1, source_target_pairs={{0,4},{4,8},{8,12},{12,16},{16,20},{20,24},{24,28},{28,32},{32,36}... | collective-permute-start | bytes 1572872 | tf_op jit(solution)/shard_map/while/body/eval_jaxpr/ppermute | solution.py:15
  412.3 12.9 %collective-permute-start = (f32[8,128,128]{2,1,0:T(8,128)}, f32[8,128,128]{2,1,0:T(8,128)}, u32[]{:S(2)}, u32[]{:S(2)}) collective-permute-start(f32[8,128,128]{2,1,0:T(8,128)} %convolution_add_fusion.7), channel_id=1, source_target_pairs={{0,4},{4,8},{8,12},{12,16},{16,20},{20,24},{24,28},{28,32},{32,36}... | collective-permute-start | bytes 1572872 | tf_op jit(solution)/shard_map/while/body/eval_jaxpr/ppermute | solution.py:15
  428.0 12.9 %collective-permute-start = (f32[8,128,128]{2,1,0:T(8,128)}, f32[8,128,128]{2,1,0:T(8,128)}, u32[]{:S(2)}, u32[]{:S(2)}) collective-permute-start(f32[8,128,128]{2,1,0:T(8,128)} %convolution_add_fusion.7), channel_id=1, source_target_pairs={{0,4},{4,8},{8,12},{12,16},{16,20},{20,24},{24,28},{28,32},{32,36}... | collective-permute-start | bytes 1572872 | tf_op jit(solution)/shard_map/while/body/eval_jaxpr/ppermute | solution.py:15
  443.7 12.9 %collective-permute-start = (f32[8,128,128]{2,1,0:T(8,128)}, f32[8,128,128]{2,1,0:T(8,128)}, u32[]{:S(2)}, u32[]{:S(2)}) collective-permute-start(f32[8,128,128]{2,1,0:T(8,128)} %convolution_add_fusion.7), channel_id=1, source_target_pairs={{0,4},{4,8},{8,12},{12,16},{16,20},{20,24},{24,28},{28,32},{32,36}... | collective-permute-start | bytes 1572872 | tf_op jit(solution)/shard_map/while/body/eval_jaxpr/ppermute | solution.py:15
  459.4 12.9 %collective-permute-start = (f32[8,128,128]{2,1,0:T(8,128)}, f32[8,128,128]{2,1,0:T(8,128)}, u32[]{:S(2)}, u32[]{:S(2)}) collective-permute-start(f32[8,128,128]{2,1,0:T(8,128)} %convolution_add_fusion.7), channel_id=1, source_target_pairs={{0,4},{4,8},{8,12},{12,16},{16,20},{20,24},{24,28},{28,32},{32,36}... | collective-permute-start | bytes 1572872 | tf_op jit(solution)/shard_map/while/body/eval_jaxpr/ppermute | solution.py:15
  475.1 12.9 %collective-permute-start = (f32[8,128,128]{2,1,0:T(8,128)}, f32[8,128,128]{2,1,0:T(8,128)}, u32[]{:S(2)}, u32[]{:S(2)}) collective-permute-start(f32[8,128,128]{2,1,0:T(8,128)} %convolution_add_fusion.7), channel_id=1, source_target_pairs={{0,4},{4,8},{8,12},{12,16},{16,20},{20,24},{24,28},{28,32},{32,36}... | collective-permute-start | bytes 1572872 | tf_op jit(solution)/shard_map/while/body/eval_jaxpr/ppermute | solution.py:15
  490.8 12.9 %collective-permute-start = (f32[8,128,128]{2,1,0:T(8,128)}, f32[8,128,128]{2,1,0:T(8,128)}, u32[]{:S(2)}, u32[]{:S(2)}) collective-permute-start(f32[8,128,128]{2,1,0:T(8,128)} %convolution_add_fusion.7), channel_id=1, source_target_pairs={{0,4},{4,8},{8,12},{12,16},{16,20},{20,24},{24,28},{28,32},{32,36}... | collective-permute-start | bytes 1572872 | tf_op jit(solution)/shard_map/while/body/eval_jaxpr/ppermute | solution.py:15
  506.5 12.9 %collective-permute-start = (f32[8,128,128]{2,1,0:T(8,128)}, f32[8,128,128]{2,1,0:T(8,128)}, u32[]{:S(2)}, u32[]{:S(2)}) collective-permute-start(f32[8,128,128]{2,1,0:T(8,128)} %convolution_add_fusion.7), channel_id=1, source_target_pairs={{0,4},{4,8},{8,12},{12,16},{16,20},{20,24},{24,28},{28,32},{32,36}... | collective-permute-start | bytes 1572872 | tf_op jit(solution)/shard_map/while/body/eval_jaxpr/ppermute | solution.py:15
  522.2 12.9 %collective-permute-start = (f32[8,128,128]{2,1,0:T(8,128)}, f32[8,128,128]{2,1,0:T(8,128)}, u32[]{:S(2)}, u32[]{:S(2)}) collective-permute-start(f32[8,128,128]{2,1,0:T(8,128)} %convolution_add_fusion.7), channel_id=1, source_target_pairs={{0,4},{4,8},{8,12},{12,16},{16,20},{20,24},{24,28},{28,32},{32,36}... | collective-permute-start | bytes 1572872 | tf_op jit(solution)/shard_map/while/body/eval_jaxpr/ppermute | solution.py:15
  537.9 12.9 %collective-permute-start = (f32[8,128,128]{2,1,0:T(8,128)}, f32[8,128,128]{2,1,0:T(8,128)}, u32[]{:S(2)}, u32[]{:S(2)}) collective-permute-start(f32[8,128,128]{2,1,0:T(8,128)} %convolution_add_fusion.7), channel_id=1, source_target_pairs={{0,4},{4,8},{8,12},{12,16},{16,20},{20,24},{24,28},{28,32},{32,36}... | collective-permute-start | bytes 1572872 | tf_op jit(solution)/shard_map/while/body/eval_jaxpr/ppermute | solution.py:15
  553.6 12.9 %collective-permute-start = (f32[8,128,128]{2,1,0:T(8,128)}, f32[8,128,128]{2,1,0:T(8,128)}, u32[]{:S(2)}, u32[]{:S(2)}) collective-permute-start(f32[8,128,128]{2,1,0:T(8,128)} %convolution_add_fusion.7), channel_id=1, source_target_pairs={{0,4},{4,8},{8,12},{12,16},{16,20},{20,24},{24,28},{28,32},{32,36}... | collective-permute-start | bytes 1572872 | tf_op jit(solution)/shard_map/while/body/eval_jaxpr/ppermute | solution.py:15
  569.3 12.9 %collective-permute-start = (f32[8,128,128]{2,1,0:T(8,128)}, f32[8,128,128]{2,1,0:T(8,128)}, u32[]{:S(2)}, u32[]{:S(2)}) collective-permute-start(f32[8,128,128]{2,1,0:T(8,128)} %convolution_add_fusion.7), channel_id=1, source_target_pairs={{0,4},{4,8},{8,12},{12,16},{16,20},{20,24},{24,28},{28,32},{32,36}... | collective-permute-start | bytes 1572872 | tf_op jit(solution)/shard_map/while/body/eval_jaxpr/ppermute | solution.py:15
  728.7 35.2 %all-to-all-start.1 = ((bf16[128,2,2,2048]{3,2,1,0:T(2,128)(2,1)}), bf16[128,2,2,2048]{3,2,1,0:T(2,128)(2,1)}, u32[]{:S(2)}, u32[]{:S(2)}) async-start(bf16[128,2,2,2048]{3,2,1,0:T(2,128)(2,1)} %copy.140), calls=%async_computation.2 | async-start | bytes 4194304 | tf_op jit(solution)/shard_map/all_to_all | solution.py:256
  (37 other events, 1246.7 us)
Sparse Core Ops, SparseCore 0:
  599.3 61.9 reduce-scatter.1
where the time goes:
time: 791 us; the launch traced here: 788 us
  waiting for transfers between devices  285 us (36%)
  starting transfers between devices  170 us (21%)
  matrix products  131 us (17%)
  other arithmetic  96.5 us (12%)
  local copies, waits for them, and re-layouts  51 us (6%)
  blocking collectives  39.9 us (5%)
  between operations  14.6 us (2%)
    ppermute x32, waiting for transfers between devices, shifted(): return lax.ppermute(value, axis, pairs)  199 us
    ppermute x32, starting transfers between devices, shifted(): return lax.ppermute(value, axis, pairs)  164 us
    dot_general x31, matrix products, relay_step(): jnp.einsum('jyu,jug->jyg', device_transfer, arriving_rows, precision=exac...  86.3 us
    another operation x4, other arithmetic, delta_blocks(): jax.scipy.linalg.solve_triangular(system, right_sides, lower=True, unit_d...  81.4 us
    reduce_scatter x1, waiting for transfers between devices, shards(): lax.psum_scatter(jnp.dot(gated, out_weight, preferred_element_type=jnp.fl...  61.4 us
    all_to_all x1, blocking collectives, shards(): lax.all_to_all(send_four, ('seq', 'exp'), split_axis=0, concat_axis=0, ti...  39.9 us
    all_to_all x1, waiting for transfers between devices, shards(): lax.all_to_all(experts_apply(lax.all_to_all(send_four, ('seq', 'exp'), sp...  25 us
  transfers between devices with their start and end apart: 34, of which 33 were waited for; matrix products, arithmetic and copies ran while one was open for 2% of the time, Pallas kernels for 0%

commit v1 on v0

v1 whole, which is shorter than its diff:
```python
import functools

import jax
import jax.numpy as jnp
from jax import lax
from jax.experimental import pallas as pl
from jax.experimental.pallas import tpu as pltpu
from jax.sharding import PartitionSpec as P

F32 = jnp.float32
BF16 = jnp.bfloat16
HIGH = lax.Precision.HIGHEST
L = 128
HD = 128
HEADS = 8
RUN = 8
VMEM_CAP = 40 * 1024 * 1024


def dotf(a, b, ca=1, cb=0):
    return lax.dot_general(a, b, (((ca,), (cb,)), ((), ())), precision=HIGH, preferred_element_type=F32)


def dotb(a, b, ca=1, cb=0):
    return lax.dot_general(a, b, (((ca,), (cb,)), ((), ())), preferred_element_type=F32)


def split(x):
    hi = x.astype(BF16)
    return hi, (x - hi.astype(F32)).astype(BF16)


def silu(x):
    return x * jax.nn.sigmoid(x)


def call(body, outs, *args, scratch=(), specs=None, flops=0, name=None):
    vmem = pl.BlockSpec(memory_space=pltpu.VMEM)
    size = sum(a.size * a.dtype.itemsize for a in args)
    return pl.pallas_call(
        body,
        out_shape=outs,
        in_specs=specs or [vmem] * len(args),
        out_specs=jax.tree.map(lambda _: vmem, outs),
        scratch_shapes=list(scratch),
        compiler_params=pltpu.CompilerParams(vmem_limit_bytes=VMEM_CAP),
        cost_estimate=pl.CostEstimate(flops=flops, bytes_accessed=size, transcendentals=0),
        name=name,
    )(*args)


def sds(shape, dtype):
    return jax.ShapeDtypeStruct(shape, dtype)


def iota(shape, dim):
    return lax.broadcasted_iota(jnp.int32, shape, dim)


def conv(x_ref, halo, taps, same_cols):
    x = x_ref[...].astype(F32)
    width = x.shape[1]
    row8 = iota((8, width), 0)
    total = taps(3) * x
    for s in (1, 2, 3):
        moved = pltpu.roll(x, s, 0)
        first = jnp.where(row8 < s, pltpu.roll(halo, s, 0), moved[:8])
        moved = jnp.concatenate([first, moved[8:]], axis=0)
        total = total + taps(3 - s) * (moved * same_cols[s - 1])
    return silu(total)


def maps_kernel(q_ref, k_ref, v_ref, halo_ref, cqk_ref, cv_ref, decay_ref, beta_ref, doc_ref, maps_ref, sc_ref, uw_ref, cq_ref):
    me = lax.axis_index("seq")
    cur = doc_ref[pl.ds(me, 1), :]
    prev = doc_ref[pl.ds(jnp.maximum(me - 1, 0), 1), :]
    prev = jnp.where(me == 0, -1, prev)
    cur8 = jnp.broadcast_to(cur, (8, L)).astype(F32)
    prev8 = jnp.broadcast_to(prev, (8, L)).astype(F32)
    lane8 = iota((8, L), 1)
    row8 = iota((8, L), 0)
    cum = decay_ref[...]
    for step in (1, 2, 4, 8, 16, 32, 64):
        cum = cum + jnp.where(lane8 >= step, pltpu.roll(cum, step, 1), 0.0)
    flags = (cur8 == prev8[:, L - 1 :]).astype(F32)
    for s in (1, 2, 3):
        shifted = jnp.where(lane8 < s, pltpu.roll(prev8, s, 1), pltpu.roll(cur8, s, 1))
        flags = jnp.where(row8 == s, (shifted == cur8).astype(F32), flags)
    flags = jnp.where(row8 == 4, cur8, flags)
    rows = jnp.concatenate([cum, beta_ref[...], flags, jnp.zeros((L - 24, L), F32)], axis=0)
    cols = rows.T
    carry_col = cols[:, 16:17]
    same_cols = [cols[:, 17:18], cols[:, 18:19], cols[:, 19:20]]
    doc_col = cols[:, 20:21]
    doc_row = cur8[:1]

    halo = halo_ref[...].astype(F32)
    kw = q_ref.shape[1]
    q = conv(q_ref, halo[:, :kw], lambda i: cqk_ref[i, 0:1, :], same_cols)
    k = conv(k_ref, halo[:, kw : 2 * kw], lambda i: cqk_ref[i, 1:2, :], same_cols)
    v = conv(v_ref, halo[:, 2 * kw :], lambda i: cv_ref[i : i + 1, :], same_cols)

    ri, ci = iota((L, L), 0), iota((L, L), 1)
    same = doc_col == doc_row
    keep = same & (ri >= ci)
    strict = ri > ci
    eye = (ri == ci).astype(F32)
    end_same = doc_col == doc_row[:, L - 1 :]
    q_heads, k_heads, kk, qk = [], [], [], []
    for j in range(HEADS // 2):
        qj, kj = q[:, j * HD : (j + 1) * HD], k[:, j * HD : (j + 1) * HD]
        qj = qj * lax.rsqrt(jnp.sum(qj * qj, axis=1, keepdims=True) + 1e-06) * (HD ** -0.5)
        kj = kj * lax.rsqrt(jnp.sum(kj * kj, axis=1, keepdims=True) + 1e-06)
        q_heads.append(qj)
        k_heads.append(kj)
        kk.append(dotf(kj, kj, 1, 1))
        qk.append(dotf(qj, kj, 1, 1))
    systems, inverses = [], []
    for h in range(HEADS):
        c_col, c_row = cols[:, h : h + 1], cum[h : h + 1]
        within = jnp.where(keep, jnp.exp(jnp.where(keep, c_col - c_row, 0.0)), 0.0)
        sc_ref[h] = qk[h // 2] * within
        systems.append(jnp.where(strict, cols[:, 8 + h : 9 + h] * within * kk[h // 2], 0.0))
    one = (ri // 2 == ci // 2)
    inverses = [eye - jnp.where(one, a, 0.0) for a in systems]
    size = 2
    while size < L:
        pick = (ri // (2 * size) == ci // (2 * size)) & (ri // size != ci // size)
        inner = [dotf(jnp.where(pick, a, 0.0), x) for a, x in zip(systems, inverses)]
        inverses = [x - dotf(x, y) for x, y in zip(inverses, inner)]
        size *= 2
    for h in range(HEADS):
        kj = k_heads[h // 2]
        c_col = cols[:, h : h + 1]
        b_col = cols[:, 8 + h : 9 + h]
        carried = jnp.exp(c_col) * carry_col
        right = jnp.concatenate([b_col * v[:, h * HD : (h + 1) * HD], (b_col * carried) * kj], axis=1)
        uw = dotf(inverses[h], right)
        uw_ref[h] = uw
        cq_ref[h] = carried * q_heads[h // 2]
        c_last = cum[h : h + 1, L - 1 :]
        end_w = jnp.where(end_same, jnp.exp(jnp.where(end_same, c_last - c_col, 0.0)), 0.0)
        ends = dotf(end_w * kj, uw, 0, 0)
        maps_ref[h, :L] = (carried[L - 1 :] * eye - ends[:, HD:]).astype(BF16)
        maps_ref[h, L:] = ends[:, :HD].astype(BF16)


def local_kernel(sc_ref, uw_ref, cq_ref, out_ref, qe_ref):
    for h in range(HEADS):
        both = dotf(sc_ref[h], uw_ref[h])
        out_ref[h] = both[:, :HD]
        hi, lo = split(cq_ref[h] - both[:, HD:])
        qe_ref[h, :, :HD] = hi
        qe_ref[h, :, HD:] = lo


def chain_kernel(maps_ref, pq_ref, end_ref):
    ri, ci = iota((HD, HD), 0), iota((HD, HD), 1)
    state = jnp.concatenate([jnp.zeros((HD, HD), F32), (ri == ci).astype(F32)], axis=1)
    for i in range(RUN):
        pq_ref[i] = state
        trans = maps_ref[i, :HD]
        offset = maps_ref[i, HD:].astype(F32)
        if i == 0:
            state = jnp.concatenate([offset, trans.astype(F32)], axis=1)
            continue
        hi, lo = split(state)
        moved = dotb(jnp.concatenate([trans, trans], axis=1), jnp.concatenate([hi, lo], axis=0))
        state = jnp.concatenate([moved[:, :HD] + offset, moved[:, HD:]], axis=1)
    end_ref[...] = state[:, :HD].astype(BF16)


def starts_kernel(pq_ref, end_ref, start_ref):
    end = end_ref[...]
    ends = jnp.concatenate([end, end], axis=0)
    for i in range(RUN):
        hi, lo = split(pq_ref[i, :, HD:])
        moved = dotb(jnp.concatenate([hi, lo], axis=1), ends)
        start_ref[i] = (pq_ref[i, :, :HD] + moved).astype(BF16)


def project_kernel(out_ref, qe_ref, start_ref, z_ref, gain_ref, w_hbm, own_ref, s1_ref, s2_ref, s3_ref, w_ref, part_ref, sem):
    pieces = 4
    rows = w_ref.shape[0] // pieces
    copies = [
        pltpu.make_async_copy(w_hbm.at[pl.ds(p * rows, rows)], w_ref.at[pl.ds(p * rows, rows)], sem.at[p])
        for p in range(pieces)
    ]
    for copy in copies:
        copy.start()
    gain = gain_ref[...]
    gated = []
    for h in range(HEADS):
        start = start_ref[h]
        attn = out_ref[h] + dotb(qe_ref[h], jnp.concatenate([start, start], axis=0))
        z = z_ref[:, h * HD : (h + 1) * HD].astype(F32)
        scale = lax.rsqrt(jnp.mean(attn * attn, axis=1, keepdims=True) + 1e-06)
        gated.append((attn * scale * gain * silu(z)).astype(BF16))
    per = HEADS // pieces
    total = None
    for p in range(pieces):
        copies[p].wait()
        left = jnp.concatenate(gated[p * per : (p + 1) * per], axis=1)
        term = dotb(left, w_ref[pl.ds(p * rows, rows)])
        total = term if total is None else total + term
    part_ref[...] = total
    me = lax.axis_index("exp")
    n = own_ref.shape[0]
    own_ref[...] = part_ref[pl.ds(pl.multiple_of(me * n, n), n)]
    for s, ref in ((1, s1_ref), (2, s2_ref), (3, s3_ref)):
        to = lax.rem(me + s, 4)
        ref[...] = part_ref[pl.ds(pl.multiple_of(to * n, n), n)].astype(BF16)


def route_kernel(own_ref, r1_ref, r2_ref, r3_ref, res_ref, gain_ref, ids_ref, wt_ref, mid_ref, norm_ref, send_ref, pick_ref):
    hidden = own_ref[...] + r1_ref[...].astype(F32) + r2_ref[...].astype(F32) + r3_ref[...].astype(F32)
    hidden = res_ref[...].astype(F32) + hidden
    mid_ref[...] = hidden.astype(BF16)
    normed = hidden * lax.rsqrt(jnp.mean(hidden * hidden, axis=1, keepdims=True) + 1e-06) * gain_ref[...]
    normed = normed.astype(BF16)
    norm_ref[...] = normed
    tokens, width = normed.shape
    half = width // 2
    slots = send_ref.shape[0]
    col = iota((tokens, slots), 1)
    expert = col // 4
    rank = (col // 2) % 2
    named = jnp.zeros((tokens, slots), F32)
    weight = jnp.zeros((tokens, slots), F32)
    for k in range(ids_ref.shape[1]):
        hit = expert == ids_ref[:, k : k + 1]
        named = jnp.where(hit, 1.0, named)
        weight = jnp.where(hit, wt_ref[:, k : k + 1], weight)
    before = (iota((tokens, tokens), 0) > iota((tokens, tokens), 1)).astype(BF16)
    earlier = dotb(before, named.astype(BF16))
    chosen = jnp.where(earlier == rank.astype(F32), named, 0.0)
    weight = chosen * weight
    low = col % 2 == 0
    pick = jnp.concatenate([jnp.where(low, chosen, 0.0), jnp.where(low, 0.0, chosen)], axis=0).astype(BF16)
    send_ref[...] = dotb(pick, jnp.concatenate([normed[:, :half], normed[:, half:]], axis=0), 0, 0).astype(BF16)
    both = jnp.concatenate([jnp.where(low, weight, 0.0), jnp.where(low, 0.0, weight)], axis=0)
    hi, lo = split(both)
    pick_ref[: 2 * tokens] = hi
    pick_ref[2 * tokens :] = lo


def shared_kernel(norm_ref, gu_ref, down_ref, gate_ref, out_ref):
    normed = norm_ref[...]
    act = (silu(dotb(normed, gu_ref[0])) * dotb(normed, gu_ref[1])).astype(BF16)
    branch = dotb(act, down_ref[...])
    score = jnp.sum(normed.astype(F32) * gate_ref[...], axis=1, keepdims=True)
    out_ref[...] = jax.nn.sigmoid(score) * branch


def expert_kernel(recv_ref, gu_hbm, down_hbm, out_ref, gu_ref, down_ref, flat_ref, x_ref, sem):
    copies = []
    for e in range(2):
        for z in range(2):
            copies.append(pltpu.make_async_copy(gu_hbm.at[e, z], gu_ref.at[e, z], sem.at[3 * e + z]))
        copies.append(pltpu.make_async_copy(down_hbm.at[e], down_ref.at[e], sem.at[3 * e + 2]))
    for copy in copies:
        copy.start()
    rows, half = recv_ref.shape
    srcs = rows // 8
    flat = functools.partial(pl.ds, size=srcs, stride=8)
    lanes = 128
    for c in range(half // lanes):
        at = slice(c * lanes, (c + 1) * lanes)
        flat_ref[c] = recv_ref[:, at].astype(F32)
        for e in range(2):
            for r in range(2):
                for b in range(2):
                    x_ref[e, r * srcs : (r + 1) * srcs, b * half + c * lanes : b * half + (c + 1) * lanes] = flat_ref[
                        c, flat(4 * e + 2 * r + b), :
                    ].astype(BF16)
    for e in range(2):
        x = x_ref[e]
        copies[3 * e].wait()
        gate = dotb(x, gu_ref[e, 0])
        copies[3 * e + 1].wait()
        act = (silu(gate) * dotb(x, gu_ref[e, 1])).astype(BF16)
        copies[3 * e + 2].wait()
        for b in range(2):
            y = dotb(act, down_ref[e, :, b * half : (b + 1) * half])
            for r in range(2):
                for c in range(half // lanes):
                    flat_ref[c, flat(4 * e + 2 * r + b), :] = y[r * srcs : (r + 1) * srcs, c * lanes : (c + 1) * lanes]
    for c in range(half // lanes):
        out_ref[:, c * lanes : (c + 1) * lanes] = flat_ref[c].astype(BF16)


def combine_kernel(back_ref, pick_ref, shared_ref, out_ref):
    got = dotb(pick_ref[...], back_ref[...])
    n = got.shape[0] // 4
    half = got.shape[1]
    got = got[: 2 * n] + got[2 * n :]
    out_ref[:, :half] = (got[:n] + shared_ref[:, :half]).astype(BF16)
    out_ref[:, half:] = (got[n:] + shared_ref[:, half:]).astype(BF16)


def shards(
    qk_proj,
    v_proj,
    z_proj,
    conv_qk,
    conv_v,
    decay_log,
    beta_gate,
    doc_ids,
    head_gain,
    out_weight,
    residual,
    post_gain,
    route_ids,
    route_weight,
    expert_gate_up,
    expert_down,
    shared_gate_up,
    shared_down,
    shared_gate,
):
    seq_n, exp_n = lax.axis_size("seq"), lax.axis_size("exp")
    runs = [[g * RUN + i for i in range(RUN)] for g in range(seq_n // RUN)]
    q, k = qk_proj[:, 0], qk_proj[:, 1]
    rim = jnp.concatenate([q[L - 8 :], k[L - 8 :], v_proj[L - 8 :]], axis=1)
    halo = lax.ppermute(rim, "seq", [(i, i + 1) for i in range(seq_n - 1)])

    maps, scores, uw, cq = call(
        maps_kernel,
        (
            sds((HEADS, 2 * HD, HD), BF16),
            sds((HEADS, L, L), F32),
            sds((HEADS, L, 2 * HD), F32),
            sds((HEADS, L, HD), F32),
        ),
        q, k, v_proj, halo, conv_qk, conv_v, decay_log, beta_gate, doc_ids.reshape(seq_n, L),
        flops=2 * 10**9,
        name="maps",
    )
    maps = lax.all_to_all(maps, "seq", split_axis=0, concat_axis=0, tiled=True, axis_index_groups=runs)
    local_out, query_eff = call(
        local_kernel,
        (sds((HEADS, L, HD), F32), sds((HEADS, L, 2 * HD), BF16)),
        scores, uw, cq,
        flops=10**8,
        name="local_out",
    )
    pq, end = call(
        chain_kernel,
        (sds((RUN, HD, 2 * HD), F32), sds((HD, HD), BF16)),
        maps,
        flops=10**8,
        name="chain",
    )
    end = lax.ppermute(end, "seq", [(i, i + RUN) for i in range(seq_n - RUN)])
    starts = call(starts_kernel, sds((RUN, HD, HD), BF16), pq, end, flops=10**8, name="starts")
    starts = lax.all_to_all(starts, "seq", split_axis=0, concat_axis=0, tiled=True, axis_index_groups=runs)

    model = out_weight.shape[1]
    rows = residual.shape[0]
    vmem, anyw = pl.BlockSpec(memory_space=pltpu.VMEM), pl.BlockSpec(memory_space=pl.ANY)
    piece = sds((rows, model), BF16)
    own, *sends = call(
        project_kernel,
        (sds((rows, model), F32), piece, piece, piece),
        local_out, query_eff, starts, z_proj, head_gain.reshape(1, HD), out_weight,
        specs=[vmem] * 5 + [anyw],
        scratch=[pltpu.VMEM(out_weight.shape, BF16), pltpu.VMEM((L, model), F32), pltpu.SemaphoreType.DMA((4,))],
        flops=6 * 10**8,
        name="project",
    )
    got = {}
    for s in (2, 1, 3):
        got[s] = lax.ppermute(sends[s - 1], "exp", [(i, (i + s) % exp_n) for i in range(exp_n)])
    devices = seq_n * exp_n
    slots = devices * 8
    half = model // 2
    hidden_mid, normed, send, pick = call(
        route_kernel,
        (piece, piece, sds((slots, half), BF16), sds((4 * rows, slots), BF16)),
        own, got[1], got[2], got[3], residual, post_gain.reshape(1, model), route_ids, route_weight,
        flops=2 * 10**8,
        name="route",
    )
    axes = ("seq", "exp")
    recv = lax.all_to_all(send.reshape(devices, 8, half), axes, split_axis=0, concat_axis=0, tiled=True)
    shared = call(
        shared_kernel,
        sds((rows, model), F32),
        normed, shared_gate_up, shared_down, shared_gate.reshape(1, model),
        flops=2 * 10**8,
        name="shared",
    )
    made = call(
        expert_kernel,
        sds((slots, half), BF16),
        recv.reshape(slots, half), expert_gate_up, expert_down,
        specs=[vmem, anyw, anyw],
        scratch=[
            pltpu.VMEM(expert_gate_up.shape, BF16),
            pltpu.VMEM(expert_down.shape, BF16),
            pltpu.VMEM((half // 128, slots, 128), F32),
            pltpu.VMEM((2, 2 * devices, model), BF16),
            pltpu.SemaphoreType.DMA((6,)),
        ],
        flops=4 * 10**9,
        name="experts",
    )
    back = lax.all_to_all(made.reshape(devices, 8, half), axes, split_axis=0, concat_axis=0, tiled=True)
    moe_out = call(
        combine_kernel,
        piece,
        back.reshape(slots, half), pick, shared,
        flops=3 * 10**8,
        name="combine",
    )
    return hidden_mid, moe_out


def solution(mesh):
    placed = (
        P("seq", None, "exp"),
        P("seq", "exp"),
        P("seq", "exp"),
        P(None, None, "exp"),
        P(None, "exp"),
        P("exp", "seq"),
        P("exp", "seq"),
        P(),
        P(),
        P("exp", None),
        P(("seq", "exp"), None),
        P(),
        P(("seq", "exp"), None),
        P(("seq", "exp"), None),
        P(("seq", "exp"), None, None, None),
        P(("seq", "exp"), None, None),
        P(),
        P(),
        P(),
    )
    return jax.shard_map(
        shards,
        mesh=mesh,
        in_specs=placed,
        out_specs=(P(("seq", "exp"), None), P(("seq", "exp"), None)),
        check_vma=False,
    )
```

time: 791 us -> 156 us (0.20)
  waiting for transfers between devices: 285 us -> 36.5 us
  starting transfers between devices: 170 us -> 22.9 us
  matrix products: 131 us -> 0 us
  other arithmetic: 96.5 us -> 0.01 us
  local copies, waits for them, and re-layouts: 51 us -> 16 us
  Pallas kernels: 0 us -> 25.2 us
  between operations: 14.6 us -> 0.81 us
  blocking collectives: 39.9 us -> 53.5 us
    ppermute x32 -> x5, waiting for transfers between devices: 199 us -> 5.4 us  [the longest x3 4.4 us: shards(): lax.ppermute(sends[s - 1], 'exp', [(i, (i + s) % exp_n) for i in range(ex...]
    ppermute x32 -> x5, starting transfers between devices: 164 us -> 13.9 us  [the longest x3 5.74 us: shards(): lax.ppermute(sends[s - 1], 'exp', [(i, (i + s) % exp_n) for i in range(ex...]
    dot_general x51 -> x0, matrix products: 130 us -> none  [the longest x31 86.3 us: relay_step(): jnp.einsum('jyu,jug->jyg', device_transfer, arriving_rows, precision=exac...]
    another operation x5 -> x0, other arithmetic: 81.8 us -> none  [the longest x4 81.4 us: delta_blocks(): jax.scipy.linalg.solve_triangular(system, right_sides, lower=True, unit_d...]
    reduce_scatter x1 -> x0, waiting for transfers between devices: 61.4 us -> none  [shards(): lax.psum_scatter(jnp.dot(gated, out_weight, preferred_element_type=jnp.fl...]
    pallas_call x0 -> x9, Pallas kernels: none -> 25.2 us  [call(): pl.pallas_call(body, out_shape=outs, in_specs=specs or [vmem] * len(args)...]
    all_to_all x1 -> x2, blocking collectives: 39.9 us -> 53.5 us  [the longest x1 39.4 us: shards(): lax.all_to_all(send.reshape(devices, 8, half), axes, split_axis=0, concat...]
    reshape x8 -> x0, local copies, waits for them, and re-layouts: 12.4 us -> none  [the longest x1 4.38 us: shards(): send_rows.reshape(seq_count * exp_count, exp_dev, capacity, model_width)]
  transfers between devices with their start and end apart: 34 -> 7, of which waited for: 33 -> 6; matrix products, arithmetic and copies ran while one was open for 2% -> 1% of each run, Pallas kernels for 0% -> 1%
where the time goes in v1:
time: 156 us; the launch traced here: 155 us
  blocking collectives  53.5 us (34%)
  waiting for transfers between devices  36.5 us (23%)
  Pallas kernels  25.2 us (16%)
  starting transfers between devices  22.9 us (15%)
  local copies, waits for them, and re-layouts  16 us (10%)
    all_to_all x1, blocking collectives, shards(): lax.all_to_all(send.reshape(devices, 8, half), axes, split_axis=0, concat...  39.4 us
    all_to_all x1, waiting for transfers between devices, shards(): lax.all_to_all(made.reshape(devices, 8, half), axes, split_axis=0, concat...  25.6 us
    pallas_call x9, Pallas kernels, call(): pl.pallas_call(body, out_shape=outs, in_specs=specs or [vmem] * len(args)...  25.2 us
    all_to_all x1, blocking collectives, shards(): lax.all_to_all(maps, 'seq', split_axis=0, concat_axis=0, tiled=True, axis...  14.1 us
    unnamed x38, local copies, waits for them, and re-layouts  12.9 us
    ppermute x3, starting transfers between devices, shards(): lax.ppermute(sends[s - 1], 'exp', [(i, (i + s) % exp_n) for i in range(ex...  5.74 us
    all_to_all x1, waiting for transfers between devices, shards(): lax.all_to_all(starts, 'seq', split_axis=0, concat_axis=0, tiled=True, ax...  5.48 us
    all_to_all x1, starting transfers between devices, shards(): lax.all_to_all(starts, 'seq', split_axis=0, concat_axis=0, tiled=True, ax...  5.2 us
  transfers between devices with their start and end apart: 7, of which 6 were waited for; matrix products, arithmetic and copies ran while one was open for 1% of the time, Pallas kernels for 1%

profile of v1, /device:TPU:1, one launch (start us, length us, event | category | flops | bytes accessed | tf_op | source)
XLA Modules:
  0.0 154.8 jit_solution(6877547949550958380)
XLA Ops:
  0.6 0.7 slice.29
  1.4 0.8 fusion
  2.2 4.5 %collective-permute-start = (bf16[8,2048]{1,0:T(8,128)(2,1)S(1)}, bf16[8,2048]{1,0:T(8,128)(2,1)S(1)}, u32[]{:S(2)}, u32[]{:S(2)}) collective-permute-start(bf16[8,2048]{1,0:T(8,128)(2,1)S(1)} %pad_maximum_fusion), channel_id=1, source_target_pairs={{0,4},{4,8},{8,12},{12,16},{16,20},{20,24},{24,28},{28,32},{32,36}... | collective-permute-start | bytes 98312 | tf_op jit(solution)/shard_map/ppermute | solution.py:326
  6.7 1.5 fusion.1
  8.3 0.9 copy-done.9
  12.7 9.9 %maps.1 = (bf16[8,256,128]{2,1,0:T(8,128)(2,1)S(1)}, f32[8,128,128]{2,1,0:T(8,128)S(1)}, f32[8,128,256]{2,1,0:T(8,128)S(1)}, f32[8,128,128]{2,1,0:T(8,128)S(1)}) custom-call(bf16[128,512]{1,0:T(8,128)(2,1)S(1)} %get-tuple-element.39.q_ref, bf16[128,512]{1,0:T(8,128)(2,1)S(1)} %get-tuple-element.38.k_ref, bf16[128,1024]{1,0:T(8,128)(2,1)S(1)} %copy-done.9, ...), custom_call_target="tpu_custom_call" | custom-call | flops 2000000000 | bytes 614400 | tf_op jit(solution)/shard_map/maps/pallas_call | solution.py:40
  22.7 14.1 %all_to_all.20.maps_ref = bf16[8,256,128]{2,1,0:T(8,128)(2,1)S(1)} all-to-all(bf16[8,256,128]{2,1,0:T(8,128)(2,1)S(1)} %get-tuple-element.23), channel_id=1, replica_groups={{0,4,8,12,16,20,24,28},{32,36,40,44,48,52,56,60},{64,68,72,76,80,84,88,..., dimensions={0} | all-to-all | bytes 1048576 | tf_op jit(solution)/shard_map/all_to_all | solution.py:340
  36.8 1.2 chain.1
  38.0 3.6 %collective-permute-start.1 = (bf16[128,128]{1,0:T(8,128)(2,1)S(1)}, bf16[128,128]{1,0:T(8,128)(2,1)S(1)}, u32[]{:S(2)}, u32[]{:S(2)}) collective-permute-start(bf16[128,128]{1,0:T(8,128)(2,1)S(1)} %get-tuple-element.25), channel_id=1, source_target_pairs={{0,32},{4,36},{8,40},{12,44},{16,48},{20,52},{24,56},{28,60},{32,6... | collective-permute-start | bytes 98312 | tf_op jit(solution)/shard_map/ppermute | solution.py:355
  41.6 1.0 collective-permute-done.1.end_ref
  42.6 1.0 starts.1
  43.6 5.2 %all-to-all-start.1 = ((bf16[8,128,128]{2,1,0:T(8,128)(2,1)}), bf16[8,128,128]{2,1,0:T(8,128)(2,1)S(1)}, u32[]{:S(2)}, u32[]{:S(2)}) async-start(bf16[8,128,128]{2,1,0:T(8,128)(2,1)} %starts.1), calls=%async_computation.1 | async-start | bytes 524288 | tf_op jit(solution)/shard_map/all_to_all | solution.py:357
  48.8 1.0 local_out.1
  49.8 5.5 %all-to-all-done.1.start_ref = bf16[8,128,128]{2,1,0:T(8,128)(2,1)S(1)} async-done(((bf16[8,128,128]{2,1,0:T(8,128)(2,1)}), bf16[8,128,128]{2,1,0:T(8,128)(2,1)S(1)}, u32[]{:S(2)}, u32[]{:S(2)}) %all-to-all-start.1) | async-done | bytes 262176 | tf_op jit(solution)/shard_map/all_to_all | solution.py:357
  55.3 2.2 %copy-done.2 = bf16[1024,2048]{1,0:T(8,128)(2,1)S(1)} copy-done((bf16[1024,2048]{1,0:T(8,128)(2,1)S(1)}, bf16[1024,2048]{1,0:T(8,128)(2,1)}, u32[]{:S(2)}) %copy-start.2) | copy-done | bytes 4194328
  57.5 0.9 copy-done.5
  58.4 1.7 %project.1 = (f32[32,2048]{1,0:T(8,128)S(1)}, bf16[32,2048]{1,0:T(8,128)(2,1)S(1)}, bf16[32,2048]{1,0:T(8,128)(2,1)S(1)}, bf16[32,2048]{1,0:T(8,128)(2,1)S(1)}) custom-call(f32[8,128,128]{2,1,0:T(8,128)S(1)} %get-tuple-element.21.out_ref, bf16[8,128,256]{2,1,0:T(8,128)(2,1)S(1)} %get-tuple-element.22.qe_ref, ...), custom_call_target="tpu_custom_call" | custom-call | flops 600000000 | bytes 5767680 | tf_op jit(solution)/shard_map/project/pallas_call | solution.py:40
  60.2 1.7 %collective-permute-start.2 = (bf16[32,2048]{1,0:T(8,128)(2,1)S(1)}, bf16[32,2048]{1,0:T(8,128)(2,1)S(1)}, u32[]{:S(2)}, u32[]{:S(2)}) collective-permute-start(bf16[32,2048]{1,0:T(8,128)(2,1)S(1)} %get-tuple-element.27), channel_id=1, source_target_pairs={{0,1},{1,2},{2,3},{3,0},{4,5},{5,6},{6,7},{7,4},{8,9},{9,10},{10,1... | collective-permute-start | bytes 393224 | tf_op jit(solution)/shard_map/ppermute | solution.py:374
  61.9 3.3 %collective-permute-start.3 = (bf16[32,2048]{1,0:T(8,128)(2,1)S(1)}, bf16[32,2048]{1,0:T(8,128)(2,1)S(1)}, u32[]{:S(2)}, u32[]{:S(2)}) collective-permute-start(bf16[32,2048]{1,0:T(8,128)(2,1)S(1)} %get-tuple-element.28), channel_id=1, source_target_pairs={{0,2},{1,3},{2,0},{3,1},{4,6},{5,7},{6,4},{7,5},{8,10},{9,11},{10,... | collective-permute-start | bytes 393224 | tf_op jit(solution)/shard_map/ppermute | solution.py:374
  65.2 0.7 collective-permute-start.4
  66.1 0.7 collective-permute-done.2.r1_ref
  66.8 3.4 %collective-permute-done.3.r2_ref = bf16[32,2048]{1,0:T(8,128)(2,1)S(1)} collective-permute-done((bf16[32,2048]{1,0:T(8,128)(2,1)S(1)}, bf16[32,2048]{1,0:T(8,128)(2,1)S(1)}, u32[]{:S(2)}, u32[]{:S(2)}) %collective-permute-start.3) | collective-permute-done | bytes 131104 | tf_op jit(solution)/shard_map/ppermute | solution.py:374
  70.5 1.1 route.1
  71.7 39.4 %all_to_all.21 = bf16[128,8,1024]{2,1,0:T(8,128)(2,1)S(1)} all-to-all(bf16[128,8,1024]{2,1,0:T(8,128)(2,1)S(1)} %bitcast.19), channel_id=1, replica_groups=mesh['seq'=32,'exp'=4] {'seq','exp'}, dimensions={0} | all-to-all | bytes 4194304 | tf_op jit(solution)/shard_map/all_to_all | solution.py:386
  111.0 6.8 %experts.1 = bf16[1024,1024]{1,0:T(8,128)(2,1)S(1)} custom-call(bf16[1024,1024]{1,0:T(8,128)(2,1)S(1)} %bitcast.18, bf16[2,2,2048,512]{3,2,1,0:T(8,128)(2,1)} %gu_hbm.1, bf16[2,512,2048]{2,1,0:T(8,128)(2,1)S(1)} %copy-done.3), custom_call_target="tpu_custom_call" | custom-call | flops 4000000000 | bytes 14680064 | tf_op jit(solution)/shard_map/experts/pallas_call | solution.py:40
  117.9 1.3 copy-done
  119.2 3.8 %all-to-all-start.3 = ((bf16[128,8,1024]{2,1,0:T(8,128)(2,1)}), bf16[128,8,1024]{2,1,0:T(8,128)(2,1)S(1)}, u32[]{:S(2)}, u32[]{:S(2)}) async-start(bf16[128,8,1024]{2,1,0:T(8,128)(2,1)} %bitcast.17), calls=%async_computation.3 | async-start | bytes 4194304 | tf_op jit(solution)/shard_map/all_to_all | solution.py:409
  123.1 2.2 %copy-done.1 = bf16[2,2048,512]{2,1,0:T(8,128)(2,1)S(1)} copy-done((bf16[2,2048,512]{2,1,0:T(8,128)(2,1)S(1)}, bf16[2,2048,512]{2,1,0:T(8,128)(2,1)}, u32[]{:S(2)}) %copy-start.1) | copy-done | bytes 4194328
  125.3 1.6 %copy-done.4 = bf16[512,2048]{1,0:T(8,128)(2,1)S(1)} copy-done((bf16[512,2048]{1,0:T(8,128)(2,1)S(1)}, bf16[512,2048]{1,0:T(8,128)(2,1)}, u32[]{:S(2)}) %copy-start.4) | copy-done | bytes 2097176
  126.9 1.2 shared.1.shared_ref
  128.1 25.6 %all-to-all-done.3 = bf16[128,8,1024]{2,1,0:T(8,128)(2,1)S(1)} async-done(((bf16[128,8,1024]{2,1,0:T(8,128)(2,1)}), bf16[128,8,1024]{2,1,0:T(8,128)(2,1)S(1)}, u32[]{:S(2)}, u32[]{:S(2)}) %all-to-all-start.3) | async-done | bytes 2097184 | tf_op jit(solution)/shard_map/all_to_all | solution.py:409
  153.7 1.1 combine.1
  (37 shorter events, 4.0 us)
Async XLA Ops:
  2.2 6.0 %collective-permute-start = (bf16[8,2048]{1,0:T(8,128)(2,1)S(1)}, bf16[8,2048]{1,0:T(8,128)(2,1)S(1)}, u32[]{:S(2)}, u32[]{:S(2)}) collective-permute-start(bf16[8,2048]{1,0:T(8,128)(2,1)S(1)} %pad_maximum_fusion), channel_id=1, source_target_pairs={{0,4},{4,8},{8,12},{12,16},{16,20},{20,24},{24,28},{28,32},{32,36}... | collective-permute-start | bytes 98312 | tf_op jit(solution)/shard_map/ppermute | solution.py:326
  8.3 1.0 copy-start.9
  9.2 0.7 copy-start.11
  9.9 0.7 copy-start.12
  10.6 0.7 copy-start.13
  11.4 0.7 copy-start.14
  12.0 0.7 copy-start.15
  37.9 17.3 %copy-start.10 = (f32[128]{0:T(128)S(1)}, f32[128]{0:T(128)}, u32[]{:S(2)}) copy-start(f32[128]{0:T(128)} %param.27) | copy-start | bytes 1540
  38.0 4.6 %collective-permute-start.1 = (bf16[128,128]{1,0:T(8,128)(2,1)S(1)}, bf16[128,128]{1,0:T(8,128)(2,1)S(1)}, u32[]{:S(2)}, u32[]{:S(2)}) collective-permute-start(bf16[128,128]{1,0:T(8,128)(2,1)S(1)} %get-tuple-element.25), channel_id=1, source_target_pairs={{0,32},{4,36},{8,40},{12,44},{16,48},{20,52},{24,56},{28,60},{32,6... | collective-permute-start | bytes 98312 | tf_op jit(solution)/shard_map/ppermute | solution.py:355
  43.6 11.7 %all-to-all-start.1 = ((bf16[8,128,128]{2,1,0:T(8,128)(2,1)}), bf16[8,128,128]{2,1,0:T(8,128)(2,1)S(1)}, u32[]{:S(2)}, u32[]{:S(2)}) async-start(bf16[8,128,128]{2,1,0:T(8,128)(2,1)} %starts.1), calls=%async_computation.1 | async-start | bytes 524288 | tf_op jit(solution)/shard_map/all_to_all | solution.py:357
  55.3 2.2 %copy-start.2 = (bf16[1024,2048]{1,0:T(8,128)(2,1)S(1)}, bf16[1024,2048]{1,0:T(8,128)(2,1)}, u32[]{:S(2)}) copy-start(bf16[1024,2048]{1,0:T(8,128)(2,1)} %w_hbm.1) | copy-start | bytes 12582916
  57.5 0.9 copy-start.5
  58.4 7.5 %copy-start.16 = (s32[32,10]{0,1:T(8,128)S(1)}, s32[32,10]{0,1:T(8,128)}, u32[]{:S(2)}) copy-start(s32[32,10]{0,1:T(8,128)} %param.31) | copy-start | bytes 3844
  58.4 7.6 %copy-start.17 = (f32[32,10]{0,1:T(8,128)S(1)}, f32[32,10]{0,1:T(8,128)}, u32[]{:S(2)}) copy-start(f32[32,10]{0,1:T(8,128)} %param.32) | copy-start | bytes 3844
  58.4 12.1 %copy-start.6 = (bf16[32,2048]{1,0:T(8,128)(2,1)S(1)}, bf16[32,2048]{1,0:T(8,128)(2,1)}, u32[]{:S(2)}) copy-start(bf16[32,2048]{1,0:T(8,128)(2,1)} %res_ref.1) | copy-start | bytes 393220
  58.4 12.1 %copy-start.7 = (f32[2048]{0:T(1024)S(1)}, f32[2048]{0:T(1024)}, u32[]{:S(2)}) copy-start(f32[2048]{0:T(1024)} %param.30) | copy-start | bytes 24580
  60.2 6.7 %collective-permute-start.2 = (bf16[32,2048]{1,0:T(8,128)(2,1)S(1)}, bf16[32,2048]{1,0:T(8,128)(2,1)S(1)}, u32[]{:S(2)}, u32[]{:S(2)}) collective-permute-start(bf16[32,2048]{1,0:T(8,128)(2,1)S(1)} %get-tuple-element.27), channel_id=1, source_target_pairs={{0,1},{1,2},{2,3},{3,0},{4,5},{5,6},{6,7},{7,4},{8,9},{9,10},{10,1... | collective-permute-start | bytes 393224 | tf_op jit(solution)/shard_map/ppermute | solution.py:374
  61.9 8.4 %collective-permute-start.3 = (bf16[32,2048]{1,0:T(8,128)(2,1)S(1)}, bf16[32,2048]{1,0:T(8,128)(2,1)S(1)}, u32[]{:S(2)}, u32[]{:S(2)}) collective-permute-start(bf16[32,2048]{1,0:T(8,128)(2,1)S(1)} %get-tuple-element.28), channel_id=1, source_target_pairs={{0,2},{1,3},{2,0},{3,1},{4,6},{5,7},{6,4},{7,5},{8,10},{9,11},{10,... | collective-permute-start | bytes 393224 | tf_op jit(solution)/shard_map/ppermute | solution.py:374
  65.2 5.3 %collective-permute-start.4 = (bf16[32,2048]{1,0:T(8,128)(2,1)S(1)}, bf16[32,2048]{1,0:T(8,128)(2,1)S(1)}, u32[]{:S(2)}, u32[]{:S(2)}) collective-permute-start(bf16[32,2048]{1,0:T(8,128)(2,1)S(1)} %get-tuple-element.29), channel_id=1, source_target_pairs={{0,3},{1,0},{2,1},{3,2},{4,7},{5,4},{6,5},{7,6},{8,11},{9,8},{10,9... | collective-permute-start | bytes 393224 | tf_op jit(solution)/shard_map/ppermute | solution.py:374
  71.7 39.4 %copy-start.3 = (bf16[2,512,2048]{2,1,0:T(8,128)(2,1)S(1)}, bf16[2,512,2048]{2,1,0:T(8,128)(2,1)}, u32[]{:S(2)}) copy-start(bf16[2,512,2048]{2,1,0:T(8,128)(2,1)} %down_hbm.1) | copy-start | bytes 12582916
  117.9 1.3 copy-start
  119.2 3.8 %copy-start.8 = (f32[2048]{0:T(1024)S(1)}, f32[2048]{0:T(1024)}, u32[]{:S(2)}) copy-start(f32[2048]{0:T(1024)} %param.37) | copy-start | bytes 24580
  119.2 34.5 %all-to-all-start.3 = ((bf16[128,8,1024]{2,1,0:T(8,128)(2,1)}), bf16[128,8,1024]{2,1,0:T(8,128)(2,1)S(1)}, u32[]{:S(2)}, u32[]{:S(2)}) async-start(bf16[128,8,1024]{2,1,0:T(8,128)(2,1)} %bitcast.17), calls=%async_computation.3 | async-start | bytes 4194304 | tf_op jit(solution)/shard_map/all_to_all | solution.py:409
  123.1 2.2 %copy-start.1 = (bf16[2,2048,512]{2,1,0:T(8,128)(2,1)S(1)}, bf16[2,2048,512]{2,1,0:T(8,128)(2,1)}, u32[]{:S(2)}) copy-start(bf16[2,2048,512]{2,1,0:T(8,128)(2,1)} %gu_ref.1) | copy-start | bytes 12582916
  125.3 1.6 %copy-start.4 = (bf16[512,2048]{1,0:T(8,128)(2,1)S(1)}, bf16[512,2048]{1,0:T(8,128)(2,1)}, u32[]{:S(2)}) copy-start(bf16[512,2048]{1,0:T(8,128)(2,1)} %down_ref.1) | copy-start | bytes 6291460

commit v2 on v1

v2 whole, which is shorter than its diff:
```python
import functools

import jax
import jax.numpy as jnp
from jax import lax
from jax.experimental import pallas as pl
from jax.experimental.pallas import tpu as pltpu
from jax.sharding import PartitionSpec as P

F32 = jnp.float32
BF16 = jnp.bfloat16
HIGH = lax.Precision.HIGHEST
L = 128
HD = 128
HEADS = 8
RUN = 8
VMEM_CAP = 28 * 1024 * 1024


def dotf(a, b, ca=1, cb=0):
    return lax.dot_general(a, b, (((ca,), (cb,)), ((), ())), precision=HIGH, preferred_element_type=F32)


def dotb(a, b, ca=1, cb=0):
    return lax.dot_general(a, b, (((ca,), (cb,)), ((), ())), preferred_element_type=F32)


def split(x):
    hi = x.astype(BF16)
    return hi, (x - hi.astype(F32)).astype(BF16)


def silu(x):
    return x * jax.nn.sigmoid(x)


def call(body, outs, *args, scratch=(), hbm=(), vmem=(), flops=0, name=None):
    here, far_spec = pl.BlockSpec(memory_space=pltpu.VMEM), pl.BlockSpec(memory_space=pltpu.HBM)
    size = sum(a.size * a.dtype.itemsize for a in args)
    held = {i: pltpu.HBM for i in hbm} | {i: pltpu.VMEM for i in vmem}
    args = [pltpu.with_memory_space_constraint(a, held[i]) if i in held else a for i, a in enumerate(args)]
    made = pl.pallas_call(
        body,
        out_shape=[place(o.shape, o.dtype) if place else o for o, place in outs],
        in_specs=[far_spec if i in hbm else here for i in range(len(args))],
        out_specs=[far_spec if place is pltpu.HBM else here for _, place in outs],
        scratch_shapes=list(scratch),
        compiler_params=pltpu.CompilerParams(vmem_limit_bytes=VMEM_CAP),
        cost_estimate=pl.CostEstimate(flops=flops, bytes_accessed=size, transcendentals=0),
        name=name,
    )(*args)
    return made[0] if len(outs) == 1 else made


def near(shape, dtype):
    return jax.ShapeDtypeStruct(shape, dtype), pltpu.VMEM


def far(shape, dtype):
    return jax.ShapeDtypeStruct(shape, dtype), pltpu.HBM


def free(shape, dtype):
    return jax.ShapeDtypeStruct(shape, dtype), None


def iota(shape, dim):
    return lax.broadcasted_iota(jnp.int32, shape, dim)


def dot3(a, b, ca=1, cb=0):
    ah, al = split(a)
    bh, bl = split(b)
    return dotb(jnp.concatenate([ah, al, ah], axis=ca), jnp.concatenate([bh, bh, bl], axis=cb), ca, cb)


def prep_kernel(q_hbm, k_hbm, v_hbm, cqk_hbm, cv_hbm, decay_hbm, beta_hbm, doc_hbm, conv_ref, edge_ref, within_ref, sys_ref, cols_ref, x_ref, cqk_ref, cv_ref, db_ref, doc_ref, sem):
    kw = q_hbm.shape[1]
    vw = v_hbm.shape[1]
    pairs = (
        (doc_hbm, doc_ref),
        (decay_hbm, db_ref.at[0]),
        (beta_hbm, db_ref.at[1]),
        (cqk_hbm, cqk_ref),
        (cv_hbm, cv_ref),
        (q_hbm, x_ref.at[:, :kw]),
        (k_hbm, x_ref.at[:, kw : 2 * kw]),
        (v_hbm, x_ref.at[:, 2 * kw :]),
    )
    copies = [pltpu.make_async_copy(src, dst, sem.at[i]) for i, (src, dst) in enumerate(pairs)]
    for copy in copies:
        copy.start()
    for copy in copies[:3]:
        copy.wait()
    me = lax.axis_index("seq")
    cur = doc_ref[pl.ds(me, 1), :]
    prev = doc_ref[pl.ds(jnp.maximum(me - 1, 0), 1), :]
    prev = jnp.where(me == 0, -1, prev)
    cur8 = jnp.broadcast_to(cur, (8, L)).astype(F32)
    prev8 = jnp.broadcast_to(prev, (8, L)).astype(F32)
    lane8 = iota((8, L), 1)
    row8 = iota((8, L), 0)
    cum = db_ref[0]
    for step in (1, 2, 4, 8, 16, 32, 64):
        cum = cum + jnp.where(lane8 >= step, pltpu.roll(cum, step, 1), 0.0)
    flags = (cur8 == prev8[:, L - 1 :]).astype(F32)
    for s in (1, 2, 3):
        shifted = jnp.where(lane8 < s, pltpu.roll(prev8, s, 1), pltpu.roll(cur8, s, 1))
        flags = jnp.where(row8 == s, (shifted == cur8).astype(F32), flags)
    flags = jnp.where(row8 == 4, cur8, flags)
    last = L - 1
    doc_row = cur8[:1]
    end_same = cur8 == cur8[:, last:]
    carried = jnp.exp(cum) * (cur8 == prev8[:, last:]).astype(F32)
    ends = jnp.where(end_same, jnp.exp(jnp.where(end_same, cum[:, last:] - cum, 0.0)), 0.0)
    rows = jnp.concatenate([cum, db_ref[1], flags, carried, ends, jnp.zeros((L - 40, L), F32)], axis=0)
    cols = rows.T
    cols_ref[...] = cols
    doc_col = cols[:, 20:21]
    ri, ci = iota((L, L), 0), iota((L, L), 1)
    keep = (doc_col == doc_row) & (ri >= ci)
    strict = ri > ci
    for h in range(HEADS):
        spread = cols[:, h : h + 1] - cum[h : h + 1]
        within = jnp.where(keep, jnp.exp(jnp.where(keep, spread, 0.0)), 0.0)
        within_ref[h] = within
        sys_ref[h] = jnp.where(strict, cols[:, 8 + h : 9 + h] * within, 0.0)
    for copy in copies[3:]:
        copy.wait()

    def taps(i, at, half):
        if half is None:
            return cv_ref[i : i + 1, at]
        return cqk_ref[i, half : half + 1, at]

    step = 256
    for start in range(0, 2 * kw + vw, step):
        if start < 2 * kw:
            half, off = start // kw, start % kw
        else:
            half, off = None, start - 2 * kw
        at, here = slice(off, off + step), slice(start, start + step)
        x = x_ref[:, here].astype(F32)
        row = iota((8, step), 0)
        total = taps(3, at, half) * x
        for s in (1, 2, 3):
            moved = pltpu.roll(x, s, 0)
            moved = jnp.concatenate([jnp.where(row < s, 0.0, moved[:8]), moved[8:]], axis=0)
            total = total + taps(3 - s, at, half) * (moved * cols[:, 16 + s : 17 + s])
            edge_ref[8 + s : 9 + s, here] = taps(3 - s, at, half)
        edge_ref[:8, here] = total[:8]
        conv_ref[:, here] = silu(total)


def maps_kernel(conv_ref, edge_ref, halo_ref, within_ref, sys_ref, cols_ref, maps_ref, sc_ref, uw_ref, cq_ref):
    cols = cols_ref[...]
    halo = halo_ref[...].astype(F32)
    row8 = iota(halo.shape, 0)
    first = edge_ref[:8]
    for s in (1, 2, 3):
        moved = jnp.where(row8 < s, pltpu.roll(halo, s, 0), 0.0)
        first = first + edge_ref[8 + s : 9 + s] * (moved * cols[:8, 16 + s : 17 + s])
    first = silu(first)

    def feature(j):
        at = slice(j * HD, (j + 1) * HD)
        return jnp.concatenate([first[:, at], conv_ref[8:, at]], axis=0)

    ri, ci = iota((L, L), 0), iota((L, L), 1)
    eye = (ri == ci).astype(F32)
    pairs = HEADS // 2
    q_heads, k_heads, kk, qk = [], [], [], []
    for j in range(pairs):
        qj, kj = feature(j), feature(pairs + j)
        qj = qj * lax.rsqrt(jnp.sum(qj * qj, axis=1, keepdims=True) + 1e-06) * (HD ** -0.5)
        kj = kj * lax.rsqrt(jnp.sum(kj * kj, axis=1, keepdims=True) + 1e-06)
        q_heads.append(qj)
        k_heads.append(kj)
        dots = dot3(jnp.concatenate([qj, kj], axis=0), kj, 1, 1)
        qk.append(dots[:L])
        kk.append(dots[L:])
    systems = [sys_ref[h] * kk[h // 2] for h in range(HEADS)]
    narrow = [a.astype(BF16) for a in systems]
    zero = jnp.zeros((L, L), BF16)
    one = ri // 2 == ci // 2
    inverses = [eye - jnp.where(one, a, 0.0) for a in systems]
    size = 2
    while size < L:
        pick = (ri // (2 * size) == ci // (2 * size)) & (ri // size != ci // size)
        low = [x.astype(BF16) for x in inverses]
        inner = [dotb(jnp.where(pick, a, zero), x) for a, x in zip(narrow, low)]
        inverses = [x - dotb(b, y.astype(BF16)) for x, b, y in zip(inverses, low, inner)]
        size *= 2
    rests = [eye - x - dot3(a, x) for a, x in zip(systems, inverses)]
    inverses = [x + dotb(x.astype(BF16), r.astype(BF16)) for x, r in zip(inverses, rests)]
    for h in range(HEADS):
        kj = k_heads[h // 2]
        b_col = cols[:, 8 + h : 9 + h]
        carried = cols[:, 24 + h : 25 + h]
        right = jnp.concatenate([b_col * feature(2 * pairs + h), (b_col * carried) * kj], axis=1)
        uw = dot3(inverses[h], right)
        uw_ref[h] = uw
        sc_ref[h] = qk[h // 2] * within_ref[h]
        cq_ref[h] = carried * q_heads[h // 2]
        ends = dot3(cols[:, 32 + h : 33 + h] * kj, uw, 0, 0)
        maps_ref[h, :L] = (carried[L - 1 :] * eye - ends[:, HD:]).astype(BF16)
        maps_ref[h, L:] = ends[:, :HD].astype(BF16)


def local_kernel(sc_ref, uw_ref, cq_ref, out_ref, qe_ref):
    for h in range(HEADS):
        both = dot3(sc_ref[h], uw_ref[h])
        out_ref[h] = both[:, :HD]
        hi, lo = split(cq_ref[h] - both[:, HD:])
        qe_ref[h, :, :HD] = hi
        qe_ref[h, :, HD:] = lo


def chain_kernel(maps_ref, pq_ref, end_ref):
    ri, ci = iota((HD, HD), 0), iota((HD, HD), 1)
    state = jnp.concatenate([jnp.zeros((HD, HD), F32), (ri == ci).astype(F32)], axis=1)
    for i in range(RUN):
        pq_ref[i] = state
        trans = maps_ref[i, :HD]
        offset = maps_ref[i, HD:].astype(F32)
        if i == 0:
            state = jnp.concatenate([offset, trans.astype(F32)], axis=1)
            continue
        hi, lo = split(state)
        moved = dotb(jnp.concatenate([trans, trans], axis=1), jnp.concatenate([hi, lo], axis=0))
        state = jnp.concatenate([moved[:, :HD] + offset, moved[:, HD:]], axis=1)
    end_ref[...] = state[:, :HD].astype(BF16)


def starts_kernel(pq_ref, end_ref, start_ref):
    end = end_ref[...]
    ends = jnp.concatenate([end, end], axis=0)
    for i in range(RUN):
        hi, lo = split(pq_ref[i, :, HD:])
        moved = dotb(jnp.concatenate([hi, lo], axis=1), ends)
        start_ref[i] = (pq_ref[i, :, :HD] + moved).astype(BF16)


def project_kernel(out_ref, qe_ref, start_ref, z_ref, gain_ref, w_ref, own_ref, s1_ref, s2_ref, s3_ref, part_ref):
    gain = gain_ref[...]
    gated = []
    for h in range(HEADS):
        start = start_ref[h]
        attn = out_ref[h] + dotb(qe_ref[h], jnp.concatenate([start, start], axis=0))
        z = z_ref[:, h * HD : (h + 1) * HD].astype(F32)
        scale = lax.rsqrt(jnp.mean(attn * attn, axis=1, keepdims=True) + 1e-06)
        gated.append((attn * scale * gain * silu(z)).astype(BF16))
    part_ref[...] = dotb(jnp.concatenate(gated, axis=1), w_ref[...])
    me = lax.axis_index("exp")
    n = own_ref.shape[0]
    own_ref[...] = part_ref[pl.ds(pl.multiple_of(me * n, n), n)]
    for s, ref in ((1, s1_ref), (2, s2_ref), (3, s3_ref)):
        to = lax.rem(me + s, 4)
        ref[...] = part_ref[pl.ds(pl.multiple_of(to * n, n), n)].astype(BF16)


def route_kernel(own_ref, r1_ref, r2_ref, r3_ref, res_ref, gain_ref, ids_ref, wt_ref, mid_ref, norm_ref, send_ref, pick_ref):
    hidden = own_ref[...] + r1_ref[...].astype(F32) + r2_ref[...].astype(F32) + r3_ref[...].astype(F32)
    hidden = res_ref[...].astype(F32) + hidden
    mid_ref[...] = hidden.astype(BF16)
    normed = hidden * lax.rsqrt(jnp.mean(hidden * hidden, axis=1, keepdims=True) + 1e-06) * gain_ref[...]
    normed = normed.astype(BF16)
    norm_ref[...] = normed
    tokens, width = normed.shape
    half = width // 2
    slots = send_ref.shape[0]
    col = iota((tokens, slots), 1)
    expert = col // 4
    rank = (col // 2) % 2
    named = jnp.zeros((tokens, slots), F32)
    weight = jnp.zeros((tokens, slots), F32)
    for k in range(ids_ref.shape[1]):
        hit = expert == ids_ref[:, k : k + 1]
        named = jnp.where(hit, 1.0, named)
        weight = jnp.where(hit, wt_ref[:, k : k + 1], weight)
    before = (iota((tokens, tokens), 0) > iota((tokens, tokens), 1)).astype(BF16)
    earlier = dotb(before, named.astype(BF16))
    chosen = jnp.where(earlier == rank.astype(F32), named, 0.0)
    weight = chosen * weight
    low = col % 2 == 0
    pick = jnp.concatenate([jnp.where(low, chosen, 0.0), jnp.where(low, 0.0, chosen)], axis=0).astype(BF16)
    send_ref[...] = dotb(pick, jnp.concatenate([normed[:, :half], normed[:, half:]], axis=0), 0, 0).astype(BF16)
    both = jnp.concatenate([jnp.where(low, weight, 0.0), jnp.where(low, 0.0, weight)], axis=0)
    hi, lo = split(both)
    pick_ref[: 2 * tokens] = hi
    pick_ref[2 * tokens :] = lo


def shared_kernel(norm_ref, gate_ref, sgu_hbm, sdown_hbm, out_ref, sgu_ref, sdown_ref, sem):
    pairs = ((sgu_hbm, sgu_ref), (sdown_hbm, sdown_ref))
    copies = [pltpu.make_async_copy(src, dst, sem.at[i]) for i, (src, dst) in enumerate(pairs)]
    for copy in copies:
        copy.start()
    normed = norm_ref[...]
    score = jnp.sum(normed.astype(F32) * gate_ref[...], axis=1, keepdims=True)
    copies[0].wait()
    act = (silu(dotb(normed, sgu_ref[0])) * dotb(normed, sgu_ref[1])).astype(BF16)
    copies[1].wait()
    out_ref[...] = jax.nn.sigmoid(score) * dotb(act, sdown_ref[...])


def expert_kernel(recv_ref, gu_hbm, down_ref, out_hbm, gu_ref, flat_ref, x_ref, out_ref, gu_sem, sem):
    loads = [pltpu.make_async_copy(gu_hbm.at[e, z], gu_ref.at[e, z], gu_sem.at[2 * e + z]) for e in range(2) for z in range(2)]
    for load in loads:
        load.start()
    rows, half = recv_ref.shape
    srcs = rows // 8
    flat = functools.partial(pl.ds, size=srcs, stride=8)
    lanes = 128
    for c in range(half // lanes):
        at = slice(c * lanes, (c + 1) * lanes)
        flat_ref[c] = recv_ref[:, at].astype(F32)
        for e in range(2):
            for r in range(2):
                for b in range(2):
                    x_ref[e, r * srcs : (r + 1) * srcs, b * half + c * lanes : b * half + (c + 1) * lanes] = flat_ref[
                        c, flat(4 * e + 2 * r + b), :
                    ].astype(BF16)
    acts = []
    for e in range(2):
        x = x_ref[e]
        loads[2 * e].wait()
        gate = silu(dotb(x, gu_ref[e, 0]))
        loads[2 * e + 1].wait()
        acts.append((gate * dotb(x, gu_ref[e, 1])).astype(BF16))
    wide = 2 * lanes
    copies = []
    for p in range(half // wide):
        for e in range(2):
            for b in range(2):
                y = dotb(acts[e], down_ref[e, :, b * half + p * wide : b * half + (p + 1) * wide])
                for r in range(2):
                    for c in range(2):
                        flat_ref[2 * p + c, flat(4 * e + 2 * r + b), :] = y[
                            r * srcs : (r + 1) * srcs, c * lanes : (c + 1) * lanes
                        ]
        for c in (2 * p, 2 * p + 1):
            out_ref[:, c * lanes : (c + 1) * lanes] = flat_ref[c].astype(BF16)
        at = slice(p * wide, (p + 1) * wide)
        copies.append(pltpu.make_async_copy(out_ref.at[:, at], out_hbm.at[:, at], sem.at[p]))
        copies[-1].start()
    for copy in copies:
        copy.wait()


def combine_kernel(back_ref, pick_ref, shared_ref, out_ref):
    got = dotb(pick_ref[...], back_ref[...])
    n = got.shape[0] // 4
    half = got.shape[1]
    got = got[: 2 * n] + got[2 * n :]
    out_ref[:, :half] = (got[:n] + shared_ref[:, :half]).astype(BF16)
    out_ref[:, half:] = (got[n:] + shared_ref[:, half:]).astype(BF16)


def shards(
    qk_proj,
    v_proj,
    z_proj,
    conv_qk,
    conv_v,
    decay_log,
    beta_gate,
    doc_ids,
    head_gain,
    out_weight,
    residual,
    post_gain,
    route_ids,
    route_weight,
    expert_gate_up,
    expert_down,
    shared_gate_up,
    shared_down,
    shared_gate,
):
    seq_n, exp_n = lax.axis_size("seq"), lax.axis_size("exp")
    runs = [[g * RUN + i for i in range(RUN)] for g in range(seq_n // RUN)]
    q, k = qk_proj[:, 0], qk_proj[:, 1]
    rim = jnp.concatenate([q[L - 8 :], k[L - 8 :], v_proj[L - 8 :]], axis=1)
    halo = lax.ppermute(rim, "seq", [(i, i + 1) for i in range(seq_n - 1)])

    wide = 2 * q.shape[1] + v_proj.shape[1]
    conv, edge, within, system, cols = call(
        prep_kernel,
        (
            near((L, wide), F32),
            near((16, wide), F32),
            near((HEADS, L, L), F32),
            near((HEADS, L, L), F32),
            near((L, L), F32),
        ),
        q, k, v_proj, conv_qk, conv_v, decay_log, beta_gate, doc_ids.reshape(seq_n, L),
        hbm=range(8),
        scratch=[
            pltpu.VMEM((L, wide), BF16),
            pltpu.VMEM(conv_qk.shape, F32),
            pltpu.VMEM(conv_v.shape, F32),
            pltpu.VMEM((2, HEADS, L), F32),
            pltpu.VMEM((seq_n, L), jnp.int32),
            pltpu.SemaphoreType.DMA((8,)),
        ],
        flops=10**8,
        name="prep",
    )
    maps, scores, uw, cq = call(
        maps_kernel,
        (
            near((HEADS, 2 * HD, HD), BF16),
            near((HEADS, L, L), F32),
            near((HEADS, L, 2 * HD), F32),
            near((HEADS, L, HD), F32),
        ),
        conv, edge, halo, within, system, cols,
        flops=2 * 10**9,
        name="maps",
    )
    maps = lax.all_to_all(maps, "seq", split_axis=0, concat_axis=0, tiled=True, axis_index_groups=runs)
    local_out, query_eff = call(
        local_kernel,
        (near((HEADS, L, HD), F32), near((HEADS, L, 2 * HD), BF16)),
        scores, uw, cq,
        flops=10**8,
        name="local_out",
    )
    pq, end = call(
        chain_kernel,
        (near((RUN, HD, 2 * HD), F32), near((HD, HD), BF16)),
        maps,
        flops=10**8,
        name="chain",
    )
    end = lax.ppermute(end, "seq", [(i, i + RUN) for i in range(seq_n - RUN)])
    end, local_out, query_eff = lax.optimization_barrier((end, local_out, query_eff))
    starts = call(starts_kernel, (near((RUN, HD, HD), BF16),), pq, end, flops=10**8, name="starts")
    starts = lax.all_to_all(starts, "seq", split_axis=0, concat_axis=0, tiled=True, axis_index_groups=runs)

    model = out_weight.shape[1]
    rows = residual.shape[0]
    piece = near((rows, model), BF16)
    own, *sends = call(
        project_kernel,
        (near((rows, model), F32), piece, piece, piece),
        local_out, query_eff, starts, z_proj, head_gain.reshape(1, HD), out_weight,
        vmem=(3, 5),
        scratch=[pltpu.VMEM((L, model), F32)],
        flops=6 * 10**8,
        name="project",
    )
    got = {}
    for s in (2, 1, 3):
        got[s] = lax.ppermute(sends[s - 1], "exp", [(i, (i + s) % exp_n) for i in range(exp_n)])
    devices = seq_n * exp_n
    slots = devices * 8
    half = model // 2
    hidden_mid, normed, send, pick = call(
        route_kernel,
        (free((rows, model), BF16), piece, near((slots, half), BF16), near((4 * rows, slots), BF16)),
        own, got[1], got[2], got[3], residual, post_gain.reshape(1, model), route_ids, route_weight,
        flops=2 * 10**8,
        name="route",
    )
    axes = ("seq", "exp")
    recv = lax.all_to_all(send.reshape(devices, 8, half), axes, split_axis=0, concat_axis=0, tiled=True)
    made = call(
        expert_kernel,
        (far((slots, half), BF16),),
        recv.reshape(slots, half), expert_gate_up, expert_down,
        hbm=(1,),
        vmem=(2,),
        scratch=[
            pltpu.VMEM(expert_gate_up.shape, BF16),
            pltpu.VMEM((half // 128, slots, 128), F32),
            pltpu.VMEM((2, 2 * devices, model), BF16),
            pltpu.VMEM((slots, half), BF16),
            pltpu.SemaphoreType.DMA((4,)),
            pltpu.SemaphoreType.DMA((half // 256,)),
        ],
        flops=4 * 10**9,
        name="experts",
    )
    made, normed = lax.optimization_barrier((made, normed))
    shared = call(
        shared_kernel,
        (near((rows, model), F32),),
        normed, shared_gate.reshape(1, model), shared_gate_up, shared_down,
        hbm=(2, 3),
        scratch=[
            pltpu.VMEM(shared_gate_up.shape, BF16),
            pltpu.VMEM(shared_down.shape, BF16),
            pltpu.SemaphoreType.DMA((2,)),
        ],
        flops=2 * 10**8,
        name="shared",
    )
    back = lax.all_to_all(made.reshape(devices, 8, half), axes, split_axis=0, concat_axis=0, tiled=True)
    moe_out = call(
        combine_kernel,
        (free((rows, model), BF16),),
        back.reshape(slots, half), pick, shared,
        flops=3 * 10**8,
        name="combine",
    )
    return hidden_mid, moe_out


def solution(mesh):
    placed = (
        P("seq", None, "exp"),
        P("seq", "exp"),
        P("seq", "exp"),
        P(None, None, "exp"),
        P(None, "exp"),
        P("exp", "seq"),
        P("exp", "seq"),
        P(),
        P(),
        P("exp", None),
        P(("seq", "exp"), None),
        P(),
        P(("seq", "exp"), None),
        P(("seq", "exp"), None),
        P(("seq", "exp"), None, None, None),
        P(("seq", "exp"), None, None),
        P(),
        P(),
        P(),
    )
    return jax.shard_map(
        shards,
        mesh=mesh,
        in_specs=placed,
        out_specs=(P(("seq", "exp"), None), P(("seq", "exp"), None)),
        check_vma=False,
    )
```

time: 156 us -> 141 us (0.904)
  local copies, waits for them, and re-layouts: 16 us -> 4 us
  blocking collectives: 53.5 us -> 63.4 us
  starting transfers between devices: 22.9 us -> 17.3 us
  waiting for transfers between devices: 36.5 us -> 32 us
  Pallas kernels: 25.2 us -> 22.3 us
    unnamed x38 -> x20, local copies, waits for them, and re-layouts: 12.9 us -> 0.22 us
    all_to_all x0 -> x1, blocking collectives: none -> 10.8 us  [shards(): lax.all_to_all(starts, 'seq', split_axis=0, concat_axis=0, tiled=True, ax...]
    all_to_all x1 -> x0, waiting for transfers between devices: 5.48 us -> none  [shards(): lax.all_to_all(starts, 'seq', split_axis=0, concat_axis=0, tiled=True, ax...]
    all_to_all x1 -> x0, starting transfers between devices: 5.2 us -> none  [shards(): lax.all_to_all(starts, 'seq', split_axis=0, concat_axis=0, tiled=True, ax...]
    pallas_call x9 -> x10, Pallas kernels: 25.2 us -> 22.3 us  [call(): pl.pallas_call(body, out_shape=[place(o.shape, o.dtype) if place else o f...]
  transfers between devices with their start and end apart: 7 -> 6, of which waited for: 6 -> 5; matrix products, arithmetic and copies ran while one was open for 1% -> 2% of each run, Pallas kernels for 1% -> 5%
where the time goes in v2:
time: 141 us; the launch traced here: 140 us
  blocking collectives  63.4 us (45%)
  waiting for transfers between devices  32 us (23%)
  Pallas kernels  22.3 us (16%)
  starting transfers between devices  17.3 us (12%)
  local copies, waits for them, and re-layouts  4 us (3%)
    all_to_all x1, blocking collectives, shards(): lax.all_to_all(send.reshape(devices, 8, half), axes, split_axis=0, concat...  39.3 us
    all_to_all x1, waiting for transfers between devices, shards(): lax.all_to_all(made.reshape(devices, 8, half), axes, split_axis=0, concat...  27.1 us
    pallas_call x10, Pallas kernels, call(): pl.pallas_call(body, out_shape=[place(o.shape, o.dtype) if place else o f...  22.3 us
    all_to_all x1, blocking collectives, shards(): lax.all_to_all(maps, 'seq', split_axis=0, concat_axis=0, tiled=True, axis...  13.2 us
    all_to_all x1, blocking collectives, shards(): lax.all_to_all(starts, 'seq', split_axis=0, concat_axis=0, tiled=True, ax...  10.8 us
    ppermute x3, starting transfers between devices, shards(): lax.ppermute(sends[s - 1], 'exp', [(i, (i + s) % exp_n) for i in range(ex...  5.77 us
    ppermute x1, starting transfers between devices, shards(): halo = lax.ppermute(rim, 'seq', [(i, i + 1) for i in range(seq_n - 1)])  4.5 us
    ppermute x3, waiting for transfers between devices, shards(): lax.ppermute(sends[s - 1], 'exp', [(i, (i + s) % exp_n) for i in range(ex...  4.38 us
  transfers between devices with their start and end apart: 6, of which 5 were waited for; matrix products, arithmetic and copies ran while one was open for 2% of the time, Pallas kernels for 5%

profile of v2, /device:TPU:1, one launch (start us, length us, event | category | flops | bytes accessed | tf_op | source)
XLA Modules:
  0.0 139.8 jit_solution(9393426827383906690)
XLA Ops:
  0.6 0.8 fusion
  1.5 0.7 slice.29
  2.2 4.5 %collective-permute-start = (bf16[8,2048]{1,0:T(8,128)(2,1)S(1)}, bf16[8,2048]{1,0:T(8,128)(2,1)S(1)}, u32[]{:S(2)}, u32[]{:S(2)}) collective-permute-start(bf16[8,2048]{1,0:T(8,128)(2,1)S(1)} %pad_maximum_fusion), channel_id=1, source_target_pairs={{0,4},{4,8},{8,12},{12,16},{16,20},{20,24},{24,28},{28,32},{32,36}... | collective-permute-start | bytes 98312 | tf_op jit(solution)/shard_map/ppermute | solution.py:385
  6.7 1.5 %fusion.1 = (bf16[128,1,512]{2,1,0:T(2,128)(2,1)S(1)}, bf16[128,1,512]{2,1,0:T(2,128)(2,1)S(1)}) fusion(bf16[128,2,512]{2,1,0:T(2,128)(2,1)} %param.19), kind=kLoop, calls=%fused_computation.6 | loop fusion | bytes 524288 | tf_op jit(solution)/shard_map/slice | solution.py:383
  8.2 0.7 copy_bitcast_fusion
  8.9 2.7 %prep.1 = (f32[128,2048]{1,0:T(8,128)S(1)}, f32[16,2048]{1,0:T(8,128)S(1)}, f32[8,128,128]{2,1,0:T(8,128)S(1)}, f32[8,128,128]{2,1,0:T(8,128)S(1)}, f32[128,128]{1,0:T(8,128)S(1)}) custom-call(bf16[128,512]{1,0:T(8,128)(2,1)} %get-tuple-element.59.q_hbm, bf16[128,512]{1,0:T(8,128)(2,1)} %get-tuple-element.58.k_hbm, bf16[128,1024]{1,0:T(8,128)(2,1)} %v_hbm.1, ...), custom_call_target="tpu_custom_call" | custom-call | flops 100000000 | bytes 581632 | tf_op jit(solution)/shard_map/prep/pallas_call | solution.py:42
  11.6 3.7 %maps.1 = (bf16[8,256,128]{2,1,0:T(8,128)(2,1)S(1)}, f32[8,128,128]{2,1,0:T(8,128)S(1)}, f32[8,128,256]{2,1,0:T(8,128)S(1)}, f32[8,128,128]{2,1,0:T(8,128)S(1)}) custom-call(f32[128,2048]{1,0:T(8,128)S(1)} %get-tuple-element.28.conv_ref, f32[16,2048]{1,0:T(8,128)S(1)} %get-tuple-element.29.edge_ref, bf16[8,2048]{1,0:T(8,128)(2,1)S(1)} %collective-permute-done.halo_ref, ...), custom_call_target="tpu_custom_call" | custom-call | flops 2000000000 | bytes 2326528 | tf_op jit(solution)/shard_map/maps/pallas_call | solution.py:42
  15.3 13.2 %all_to_all.20.maps_ref = bf16[8,256,128]{2,1,0:T(8,128)(2,1)S(1)} all-to-all(bf16[8,256,128]{2,1,0:T(8,128)(2,1)S(1)} %get-tuple-element.33), channel_id=1, replica_groups={{0,4,8,12,16,20,24,28},{32,36,40,44,48,52,56,60},{64,68,72,76,80,84,88,..., dimensions={0} | all-to-all | bytes 1048576 | tf_op jit(solution)/shard_map/all_to_all | solution.py:422
  28.6 1.2 chain.1
  29.8 0.0 copy-start.2
  29.8 3.3 %collective-permute-start.1 = (bf16[128,128]{1,0:T(8,128)(2,1)S(1)}, bf16[128,128]{1,0:T(8,128)(2,1)S(1)}, u32[]{:S(2)}, u32[]{:S(2)}) collective-permute-start(bf16[128,128]{1,0:T(8,128)(2,1)S(1)} %get-tuple-element.34), channel_id=1, source_target_pairs={{0,32},{4,36},{8,40},{12,44},{16,48},{20,52},{24,56},{28,60},{32,6... | collective-permute-start | bytes 98312 | tf_op jit(solution)/shard_map/ppermute | solution.py:437
  33.1 0.5 local_out.1
  33.6 0.5 collective-permute-done.1.end_ref
  34.1 0.3 starts.1
  34.4 10.8 %all_to_all.21.start_ref = bf16[8,128,128]{2,1,0:T(8,128)(2,1)S(1)} all-to-all(bf16[8,128,128]{2,1,0:T(8,128)(2,1)S(1)} %starts.1), channel_id=1, replica_groups={{0,4,8,12,16,20,24,28},{32,36,40,44,48,52,56,60},{64,68,72,76,80,84,88,..., dimensions={0} | all-to-all | bytes 524288 | tf_op jit(solution)/shard_map/all_to_all | solution.py:440
  45.2 0.0 copy-start.3
  45.3 1.1 project.1
  46.4 1.7 %collective-permute-start.2 = (bf16[32,2048]{1,0:T(8,128)(2,1)S(1)}, bf16[32,2048]{1,0:T(8,128)(2,1)S(1)}, u32[]{:S(2)}, u32[]{:S(2)}) collective-permute-start(bf16[32,2048]{1,0:T(8,128)(2,1)S(1)} %get-tuple-element.45), channel_id=1, source_target_pairs={{0,1},{1,2},{2,3},{3,0},{4,5},{5,6},{6,7},{7,4},{8,9},{9,10},{10,1... | collective-permute-start | bytes 393224 | tf_op jit(solution)/shard_map/ppermute | solution.py:456
  48.1 3.3 %collective-permute-start.3 = (bf16[32,2048]{1,0:T(8,128)(2,1)S(1)}, bf16[32,2048]{1,0:T(8,128)(2,1)S(1)}, u32[]{:S(2)}, u32[]{:S(2)}) collective-permute-start(bf16[32,2048]{1,0:T(8,128)(2,1)S(1)} %get-tuple-element.46), channel_id=1, source_target_pairs={{0,2},{1,3},{2,0},{3,1},{4,6},{5,7},{6,4},{7,5},{8,10},{9,11},{10,... | collective-permute-start | bytes 393224 | tf_op jit(solution)/shard_map/ppermute | solution.py:456
  51.4 0.7 collective-permute-start.4
  52.2 0.1 copy.25.ids_ref
  52.3 0.1 copy.26.wt_ref
  52.3 0.7 collective-permute-done.2.r1_ref
  53.1 3.4 %collective-permute-done.3.r2_ref = bf16[32,2048]{1,0:T(8,128)(2,1)S(1)} collective-permute-done((bf16[32,2048]{1,0:T(8,128)(2,1)S(1)}, bf16[32,2048]{1,0:T(8,128)(2,1)S(1)}, u32[]{:S(2)}, u32[]{:S(2)}) %collective-permute-start.3) | collective-permute-done | bytes 131104 | tf_op jit(solution)/shard_map/ppermute | solution.py:456
  56.5 0.2 collective-permute-done.4.r3_ref
  56.7 1.2 route.1
  57.9 39.3 %all_to_all.22 = bf16[128,8,1024]{2,1,0:T(8,128)(2,1)S(1)} all-to-all(bf16[128,8,1024]{2,1,0:T(8,128)(2,1)S(1)} %bitcast.18), channel_id=1, replica_groups=mesh['seq'=32,'exp'=4] {'seq','exp'}, dimensions={0} | all-to-all | bytes 4194304 | tf_op jit(solution)/shard_map/all_to_all | solution.py:468
  97.2 7.1 %experts.1 = bf16[1024,1024]{1,0:T(8,128)(2,1)} custom-call(bf16[1024,1024]{1,0:T(8,128)(2,1)S(1)} %bitcast.17, bf16[2,2,2048,512]{3,2,1,0:T(8,128)(2,1)} %gu_hbm.1, bf16[2,512,2048]{2,1,0:T(8,128)(2,1)S(1)} %copy-done.1), custom_call_target="tpu_custom_call" | custom-call | flops 4000000000 | bytes 14680064 | tf_op jit(solution)/shard_map/experts/pallas_call | solution.py:42
  104.3 3.7 %all-to-all-start.3 = ((bf16[128,8,1024]{2,1,0:T(8,128)(2,1)}), bf16[128,8,1024]{2,1,0:T(8,128)(2,1)S(1)}, u32[]{:S(2)}, u32[]{:S(2)}) async-start(bf16[128,8,1024]{2,1,0:T(8,128)(2,1)} %bitcast.22), calls=%async_computation.3 | async-start | bytes 4194304 | tf_op jit(solution)/shard_map/all_to_all | solution.py:500
  108.0 3.5 %shared.1.shared_ref = f32[32,2048]{1,0:T(8,128)S(1)} custom-call(bf16[32,2048]{1,0:T(8,128)(2,1)S(1)} %get-tuple-element.53.norm_ref, f32[1,2048]{1,0:T(1,128)S(1)} %bitcast.20, bf16[2,2048,512]{2,1,0:T(8,128)(2,1)} %sgu_hbm.1, bf16[512,2048]{1,0:T(8,128)(2,1)} %sdown_hbm.1), custom_call_target="tpu_custom_call" | custom-call | flops 200000000 | bytes 6430720 | tf_op jit(solution)/shard_map/shared/pallas_call | solution.py:42
  111.6 27.1 %all-to-all-done.3 = bf16[128,8,1024]{2,1,0:T(8,128)(2,1)S(1)} async-done(((bf16[128,8,1024]{2,1,0:T(8,128)(2,1)}), bf16[128,8,1024]{2,1,0:T(8,128)(2,1)S(1)}, u32[]{:S(2)}, u32[]{:S(2)}) %all-to-all-start.3) | async-done | bytes 2097184 | tf_op jit(solution)/shard_map/all_to_all | solution.py:500
  138.7 1.1 combine.1
  (19 shorter events, 0.1 us)
Async XLA Ops:
  2.2 9.4 %collective-permute-start = (bf16[8,2048]{1,0:T(8,128)(2,1)S(1)}, bf16[8,2048]{1,0:T(8,128)(2,1)S(1)}, u32[]{:S(2)}, u32[]{:S(2)}) collective-permute-start(bf16[8,2048]{1,0:T(8,128)(2,1)S(1)} %pad_maximum_fusion), channel_id=1, source_target_pairs={{0,4},{4,8},{8,12},{12,16},{16,20},{20,24},{24,28},{28,32},{32,36}... | collective-permute-start | bytes 98312 | tf_op jit(solution)/shard_map/ppermute | solution.py:385
  28.6 16.6 %copy-start = (bf16[1024,2048]{1,0:T(8,128)(2,1)S(1)}, bf16[1024,2048]{1,0:T(8,128)(2,1)}, u32[]{:S(2)}) copy-start(bf16[1024,2048]{1,0:T(8,128)(2,1)} %w_ref.1) | copy-start | bytes 12582916
  29.8 15.4 %copy-start.2 = (bf16[128,1024]{1,0:T(8,128)(2,1)S(1)}, bf16[128,1024]{1,0:T(8,128)(2,1)}, u32[]{:S(2)}) copy-start(bf16[128,1024]{1,0:T(8,128)(2,1)} %z_ref.1) | copy-start | bytes 786436
  29.8 15.4 %copy-start.6 = (f32[128]{0:T(128)S(1)}, f32[128]{0:T(128)}, u32[]{:S(2)}) copy-start(f32[128]{0:T(128)} %param.27) | copy-start | bytes 1540
  29.8 4.3 %collective-permute-start.1 = (bf16[128,128]{1,0:T(8,128)(2,1)S(1)}, bf16[128,128]{1,0:T(8,128)(2,1)S(1)}, u32[]{:S(2)}, u32[]{:S(2)}) collective-permute-start(bf16[128,128]{1,0:T(8,128)(2,1)S(1)} %get-tuple-element.34), channel_id=1, source_target_pairs={{0,32},{4,36},{8,40},{12,44},{16,48},{20,52},{24,56},{28,60},{32,6... | collective-permute-start | bytes 98312 | tf_op jit(solution)/shard_map/ppermute | solution.py:437
  45.2 7.0 %copy-start.7 = (s32[32,10]{0,1:T(8,128)S(1)}, s32[32,10]{0,1:T(8,128)}, u32[]{:S(2)}) copy-start(s32[32,10]{0,1:T(8,128)} %param.31) | copy-start | bytes 3844
  45.2 7.0 %copy-start.8 = (f32[32,10]{0,1:T(8,128)S(1)}, f32[32,10]{0,1:T(8,128)}, u32[]{:S(2)}) copy-start(f32[32,10]{0,1:T(8,128)} %param.32) | copy-start | bytes 3844
  45.2 11.5 %copy-start.3 = (bf16[32,2048]{1,0:T(8,128)(2,1)S(1)}, bf16[32,2048]{1,0:T(8,128)(2,1)}, u32[]{:S(2)}) copy-start(bf16[32,2048]{1,0:T(8,128)(2,1)} %res_ref.1) | copy-start | bytes 393220
  45.2 11.5 %copy-start.4 = (f32[2048]{0:T(1024)S(1)}, f32[2048]{0:T(1024)}, u32[]{:S(2)}) copy-start(f32[2048]{0:T(1024)} %param.30) | copy-start | bytes 24580
  46.4 6.7 %collective-permute-start.2 = (bf16[32,2048]{1,0:T(8,128)(2,1)S(1)}, bf16[32,2048]{1,0:T(8,128)(2,1)S(1)}, u32[]{:S(2)}, u32[]{:S(2)}) collective-permute-start(bf16[32,2048]{1,0:T(8,128)(2,1)S(1)} %get-tuple-element.45), channel_id=1, source_target_pairs={{0,1},{1,2},{2,3},{3,0},{4,5},{5,6},{6,7},{7,4},{8,9},{9,10},{10,1... | collective-permute-start | bytes 393224 | tf_op jit(solution)/shard_map/ppermute | solution.py:456
  48.1 8.4 %collective-permute-start.3 = (bf16[32,2048]{1,0:T(8,128)(2,1)S(1)}, bf16[32,2048]{1,0:T(8,128)(2,1)S(1)}, u32[]{:S(2)}, u32[]{:S(2)}) collective-permute-start(bf16[32,2048]{1,0:T(8,128)(2,1)S(1)} %get-tuple-element.46), channel_id=1, source_target_pairs={{0,2},{1,3},{2,0},{3,1},{4,6},{5,7},{6,4},{7,5},{8,10},{9,11},{10,... | collective-permute-start | bytes 393224 | tf_op jit(solution)/shard_map/ppermute | solution.py:456
  51.4 5.3 %collective-permute-start.4 = (bf16[32,2048]{1,0:T(8,128)(2,1)S(1)}, bf16[32,2048]{1,0:T(8,128)(2,1)S(1)}, u32[]{:S(2)}, u32[]{:S(2)}) collective-permute-start(bf16[32,2048]{1,0:T(8,128)(2,1)S(1)} %get-tuple-element.47), channel_id=1, source_target_pairs={{0,3},{1,0},{2,1},{3,2},{4,7},{5,4},{6,5},{7,6},{8,11},{9,8},{10,9... | collective-permute-start | bytes 393224 | tf_op jit(solution)/shard_map/ppermute | solution.py:456
  57.9 39.4 %copy-start.1 = (bf16[2,512,2048]{2,1,0:T(8,128)(2,1)S(1)}, bf16[2,512,2048]{2,1,0:T(8,128)(2,1)}, u32[]{:S(2)}) copy-start(bf16[2,512,2048]{2,1,0:T(8,128)(2,1)} %down_ref.1) | copy-start | bytes 12582916
  104.3 3.7 %copy-start.5 = (f32[2048]{0:T(1024)S(1)}, f32[2048]{0:T(1024)}, u32[]{:S(2)}) copy-start(f32[2048]{0:T(1024)} %param.37) | copy-start | bytes 24580
  104.3 34.4 %all-to-all-start.3 = ((bf16[128,8,1024]{2,1,0:T(8,128)(2,1)}), bf16[128,8,1024]{2,1,0:T(8,128)(2,1)S(1)}, u32[]{:S(2)}, u32[]{:S(2)}) async-start(bf16[128,8,1024]{2,1,0:T(8,128)(2,1)} %bitcast.22), calls=%async_computation.3 | async-start | bytes 4194304 | tf_op jit(solution)/shard_map/all_to_all | solution.py:500

commit v3 on v2

--- a/solution.py
+++ b/solution.py
@@ -74,8 +74,24 @@
     return dotb(jnp.concatenate([ah, al, ah], axis=ca), jnp.concatenate([bh, bh, bl], axis=cb), ca, cb)
 
 
-def prep_kernel(q_hbm, k_hbm, v_hbm, cqk_hbm, cv_hbm, decay_hbm, beta_hbm, doc_hbm, conv_ref, edge_ref, within_ref, sys_ref, cols_ref, x_ref, cqk_ref, cv_ref, db_ref, doc_ref, sem):
-    kw = q_hbm.shape[1]
+def rim_kernel(qk_hbm, v_hbm, rim_ref, qk_ref, v_ref, sem):
+    tail = pl.ds(L - 8, 8)
+    copies = [
+        pltpu.make_async_copy(qk_hbm.at[tail], qk_ref, sem.at[0]),
+        pltpu.make_async_copy(v_hbm.at[tail], v_ref, sem.at[1]),
+    ]
+    for copy in copies:
+        copy.start()
+    for copy in copies:
+        copy.wait()
+    kw = qk_ref.shape[2]
+    for z in range(2):
+        rim_ref[:, z * kw : (z + 1) * kw] = qk_ref[:, z, :]
+    rim_ref[:, 2 * kw :] = v_ref[...]
+
+
+def prep_kernel(qk_hbm, v_hbm, cqk_hbm, cv_hbm, decay_hbm, beta_hbm, doc_hbm, conv_ref, edge_ref, within_ref, sys_ref, cols_ref, qk_ref, v_ref, cqk_ref, cv_ref, db_ref, doc_ref, sem):
+    kw = qk_hbm.shape[2]
     vw = v_hbm.shape[1]
     pairs = (
         (doc_hbm, doc_ref),
@@ -83,9 +99,8 @@
         (beta_hbm, db_ref.at[1]),
         (cqk_hbm, cqk_ref),
         (cv_hbm, cv_ref),
-        (q_hbm, x_ref.at[:, :kw]),
-        (k_hbm, x_ref.at[:, kw : 2 * kw]),
-        (v_hbm, x_ref.at[:, 2 * kw :]),
+        (qk_hbm, qk_ref),
+        (v_hbm, v_ref),
     )
     copies = [pltpu.make_async_copy(src, dst, sem.at[i]) for i, (src, dst) in enumerate(pairs)]
     for copy in copies:
@@ -140,7 +155,7 @@
         else:
             half, off = None, start - 2 * kw
         at, here = slice(off, off + step), slice(start, start + step)
-        x = x_ref[:, here].astype(F32)
+        x = (v_ref[:, at] if half is None else qk_ref[:, half, at]).astype(F32)
         row = iota((8, step), 0)
         total = taps(3, at, half) * x
         for s in (1, 2, 3):
@@ -274,11 +289,16 @@
     rank = (col // 2) % 2
     named = jnp.zeros((tokens, slots), F32)
     weight = jnp.zeros((tokens, slots), F32)
-    for k in range(ids_ref.shape[1]):
-        hit = expert == ids_ref[:, k : k + 1]
+    ti, tj = iota((tokens, tokens), 0), iota((tokens, tokens), 1)
+    same = (ti == tj).astype(F32)
+    ids = dotf(same, ids_ref[...].astype(F32), 1, 1)
+    weights = dotf(same, wt_ref[...], 1, 1)
+    expert = expert.astype(F32)
+    for k in range(ids_ref.shape[0]):
+        hit = expert == ids[:, k : k + 1]
         named = jnp.where(hit, 1.0, named)
-        weight = jnp.where(hit, wt_ref[:, k : k + 1], weight)
-    before = (iota((tokens, tokens), 0) > iota((tokens, tokens), 1)).astype(BF16)
+        weight = jnp.where(hit, weights[:, k : k + 1], weight)
+    before = (ti > tj).astype(BF16)
     earlier = dotb(before, named.astype(BF16))
     chosen = jnp.where(earlier == rank.astype(F32), named, 0.0)
     weight = chosen * weight
@@ -304,10 +324,19 @@
     out_ref[...] = jax.nn.sigmoid(score) * dotb(act, sdown_ref[...])
 
 
-def expert_kernel(recv_ref, gu_hbm, down_ref, out_hbm, gu_ref, flat_ref, x_ref, out_ref, gu_sem, sem):
-    loads = [pltpu.make_async_copy(gu_hbm.at[e, z], gu_ref.at[e, z], gu_sem.at[2 * e + z]) for e in range(2) for z in range(2)]
-    for load in loads:
-        load.start()
+def fetch_kernel(gu_hbm, down_hbm, gu_ref, down_ref, sem):
+    copies = [
+        pltpu.make_async_copy(src.at[e], dst.at[e], sem.at[2 * i + e])
+        for i, (src, dst) in enumerate(((gu_hbm, gu_ref), (down_hbm, down_ref)))
+        for e in range(2)
+    ]
+    for copy in copies:
+        copy.start()
+    for copy in copies:
+        copy.wait()
+
+
+def expert_kernel(recv_ref, gu_ref, down_ref, out_hbm, flat_ref, x_ref, out_ref, sem):
     rows, half = recv_ref.shape
     srcs = rows // 8
     flat = functools.partial(pl.ds, size=srcs, stride=8)
@@ -324,10 +353,7 @@
     acts = []
     for e in range(2):
         x = x_ref[e]
-        loads[2 * e].wait()
-        gate = silu(dotb(x, gu_ref[e, 0]))
-        loads[2 * e + 1].wait()
-        acts.append((gate * dotb(x, gu_ref[e, 1])).astype(BF16))
+        acts.append((silu(dotb(x, gu_ref[e, 0])) * dotb(x, gu_ref[e, 1])).astype(BF16))
     wide = 2 * lanes
     copies = []
     for p in range(half // wide):
@@ -380,11 +406,18 @@
 ):
     seq_n, exp_n = lax.axis_size("seq"), lax.axis_size("exp")
     runs = [[g * RUN + i for i in range(RUN)] for g in range(seq_n // RUN)]
-    q, k = qk_proj[:, 0], qk_proj[:, 1]
-    rim = jnp.concatenate([q[L - 8 :], k[L - 8 :], v_proj[L - 8 :]], axis=1)
+    kw, vw = qk_proj.shape[2], v_proj.shape[1]
+    wide = 2 * kw + vw
+    rim = call(
+        rim_kernel,
+        (near((8, wide), BF16),),
+        qk_proj, v_proj,
+        hbm=(0, 1),
+        scratch=[pltpu.VMEM((8, 2, kw), BF16), pltpu.VMEM((8, vw), BF16), pltpu.SemaphoreType.DMA((2,))],
+        name="rim",
+    )
     halo = lax.ppermute(rim, "seq", [(i, i + 1) for i in range(seq_n - 1)])
 
-    wide = 2 * q.shape[1] + v_proj.shape[1]
     conv, edge, within, system, cols = call(
         prep_kernel,
         (
@@ -394,15 +427,16 @@
             near((HEADS, L, L), F32),
             near((L, L), F32),
         ),
-        q, k, v_proj, conv_qk, conv_v, decay_log, beta_gate, doc_ids.reshape(seq_n, L),
-        hbm=range(8),
+        qk_proj, v_proj, conv_qk, conv_v, decay_log, beta_gate, doc_ids.reshape(seq_n, L),
+        hbm=range(7),
         scratch=[
-            pltpu.VMEM((L, wide), BF16),
+            pltpu.VMEM((L, 2, kw), BF16),
+            pltpu.VMEM((L, vw), BF16),
             pltpu.VMEM(conv_qk.shape, F32),
             pltpu.VMEM(conv_v.shape, F32),
             pltpu.VMEM((2, HEADS, L), F32),
             pltpu.VMEM((seq_n, L), jnp.int32),
-            pltpu.SemaphoreType.DMA((8,)),
+            pltpu.SemaphoreType.DMA((7,)),
         ],
         flops=10**8,
         name="prep",
@@ -454,13 +488,22 @@
     got = {}
     for s in (2, 1, 3):
         got[s] = lax.ppermute(sends[s - 1], "exp", [(i, (i + s) % exp_n) for i in range(exp_n)])
+    gu_near, down_near = call(
+        fetch_kernel,
+        (near(expert_gate_up.shape, BF16), near(expert_down.shape, BF16)),
+        expert_gate_up, expert_down,
+        hbm=(0, 1),
+        scratch=[pltpu.SemaphoreType.DMA((4,))],
+        name="fetch",
+    )
+    own, gu_near, down_near = lax.optimization_barrier((own, gu_near, down_near))
     devices = seq_n * exp_n
     slots = devices * 8
     half = model // 2
     hidden_mid, normed, send, pick = call(
         route_kernel,
         (free((rows, model), BF16), piece, near((slots, half), BF16), near((4 * rows, slots), BF16)),
-        own, got[1], got[2], got[3], residual, post_gain.reshape(1, model), route_ids, route_weight,
+        own, got[1], got[2], got[3], residual, post_gain.reshape(1, model), route_ids.T, route_weight.T,
         flops=2 * 10**8,
         name="route",
     )
@@ -469,15 +512,11 @@
     made = call(
         expert_kernel,
         (far((slots, half), BF16),),
-        recv.reshape(slots, half), expert_gate_up, expert_down,
-        hbm=(1,),
-        vmem=(2,),
+        recv.reshape(slots, half), gu_near, down_near,
         scratch=[
-            pltpu.VMEM(expert_gate_up.shape, BF16),
             pltpu.VMEM((half // 128, slots, 128), F32),
             pltpu.VMEM((2, 2 * devices, model), BF16),
             pltpu.VMEM((slots, half), BF16),
-            pltpu.SemaphoreType.DMA((4,)),
             pltpu.SemaphoreType.DMA((half // 256,)),
         ],
         flops=4 * 10**9,

time: 141 us -> 136 us (0.965)
  Pallas kernels: 22.3 us -> 26.7 us
  waiting for transfers between devices: 32 us -> 27.7 us
  local copies, waits for them, and re-layouts: 4 us -> 0.04 us
    pallas_call x10 -> x12, Pallas kernels: 22.3 us -> 26.7 us  [call(): pl.pallas_call(body, out_shape=[place(o.shape, o.dtype) if place else o f...]
    ppermute x3, waiting for transfers between devices: 4.38 us -> 0.01 us  [shards(): lax.ppermute(sends[s - 1], 'exp', [(i, (i + s) % exp_n) for i in range(ex...]
    slice x4 -> x0, local copies, waits for them, and re-layouts: 3.04 us -> none  [the longest x3 1.56 us: shards(): rim = jnp.concatenate([q[L - 8:], k[L - 8:], v_proj[L - 8:]], axis=1)]
  transfers between devices with their start and end apart: 6 -> 6, of which waited for: 5 -> 2; matrix products, arithmetic and copies ran while one was open for 2% -> 0% of each run, Pallas kernels for 5% -> 9%
where the time goes in v3:
time: 136 us
  blocking collectives  63.4 us (47%)
  waiting for transfers between devices  27.7 us (20%)
  Pallas kernels  26.7 us (20%)
  starting transfers between devices  17.2 us (13%)
    all_to_all x1, blocking collectives, shards(): lax.all_to_all(send.reshape(devices, 8, half), axes, split_axis=0, concat...  39.1 us
    all_to_all x1, waiting for transfers between devices, shards(): lax.all_to_all(made.reshape(devices, 8, half), axes, split_axis=0, concat...  27.1 us
    pallas_call x12, Pallas kernels, call(): pl.pallas_call(body, out_shape=[place(o.shape, o.dtype) if place else o f...  26.7 us
    all_to_all x1, blocking collectives, shards(): lax.all_to_all(maps, 'seq', split_axis=0, concat_axis=0, tiled=True, axis...  13.5 us
    all_to_all x1, blocking collectives, shards(): lax.all_to_all(starts, 'seq', split_axis=0, concat_axis=0, tiled=True, ax...  10.8 us
    ppermute x3, starting transfers between devices, shards(): lax.ppermute(sends[s - 1], 'exp', [(i, (i + s) % exp_n) for i in range(ex...  5.82 us
    ppermute x1, starting transfers between devices, shards(): halo = lax.ppermute(rim, 'seq', [(i, i + 1) for i in range(seq_n - 1)])  4.5 us
    all_to_all x1, starting transfers between devices, shards(): lax.all_to_all(made.reshape(devices, 8, half), axes, split_axis=0, concat...  3.7 us
  transfers between devices with their start and end apart: 6, of which 2 were waited for; matrix products, arithmetic and copies ran while one was open for 0% of the time, Pallas kernels for 9%

profile of v3, /device:TPU:1, one launch (start us, length us, event | category | flops | bytes accessed | tf_op | source)
XLA Modules:
  0.0 135.9 jit_solution(16019741550913783189)
XLA Ops:
  0.6 0.8 rim.1
  1.4 4.5 %collective-permute-start = (bf16[8,2048]{1,0:T(8,128)(2,1)S(1)}, bf16[8,2048]{1,0:T(8,128)(2,1)S(1)}, u32[]{:S(2)}, u32[]{:S(2)}) collective-permute-start(bf16[8,2048]{1,0:T(8,128)(2,1)S(1)} %rim.1), channel_id=1, source_target_pairs={{0,4},{4,8},{8,12},{12,16},{16,20},{20,24},{24,28},{28,32},{32,36}... | collective-permute-start | bytes 98312 | tf_op jit(solution)/shard_map/ppermute | solution.py:419
  5.9 3.0 %prep.1 = (f32[128,2048]{1,0:T(8,128)S(1)}, f32[16,2048]{1,0:T(8,128)S(1)}, f32[8,128,128]{2,1,0:T(8,128)S(1)}, f32[8,128,128]{2,1,0:T(8,128)S(1)}, f32[128,128]{1,0:T(8,128)S(1)}) custom-call(bf16[128,2,512]{2,1,0:T(2,128)(2,1)} %qk_hbm.3, bf16[128,1024]{1,0:T(8,128)(2,1)} %v_hbm.3, f32[4,2,512]{2,1,0:T(2,128)} %cqk_hbm.1, f32[4,1024]{1,0:T(4,128)} %cv_hbm.1, ...), custom_call_target="tpu_custom_call" | custom-call | flops 100000000 | bytes 581632 | tf_op jit(solution)/shard_map/prep/pallas_call | solution.py:42
  8.9 0.0 collective-permute-done.halo_ref
  8.9 3.7 %maps.1 = (bf16[8,256,128]{2,1,0:T(8,128)(2,1)S(1)}, f32[8,128,128]{2,1,0:T(8,128)S(1)}, f32[8,128,256]{2,1,0:T(8,128)S(1)}, f32[8,128,128]{2,1,0:T(8,128)S(1)}) custom-call(f32[128,2048]{1,0:T(8,128)S(1)} %get-tuple-element.33.conv_ref, f32[16,2048]{1,0:T(8,128)S(1)} %get-tuple-element.34.edge_ref, bf16[8,2048]{1,0:T(8,128)(2,1)S(1)} %collective-permute-done.halo_ref, ...), custom_call_target="tpu_custom_call" | custom-call | flops 2000000000 | bytes 2326528 | tf_op jit(solution)/shard_map/maps/pallas_call | solution.py:42
  12.6 0.0 copy-start
  12.6 0.0 copy-start.1
  12.6 0.0 copy-start.7
  12.6 13.5 %all_to_all.20.maps_ref = bf16[8,256,128]{2,1,0:T(8,128)(2,1)S(1)} all-to-all(bf16[8,256,128]{2,1,0:T(8,128)(2,1)S(1)} %get-tuple-element.38), channel_id=1, replica_groups={{0,4,8,12,16,20,24,28},{32,36,40,44,48,52,56,60},{64,68,72,76,80,84,88,..., dimensions={0} | all-to-all | bytes 1048576 | tf_op jit(solution)/shard_map/all_to_all | solution.py:456
  26.2 1.2 chain.1
  27.3 3.2 %collective-permute-start.1 = (bf16[128,128]{1,0:T(8,128)(2,1)S(1)}, bf16[128,128]{1,0:T(8,128)(2,1)S(1)}, u32[]{:S(2)}, u32[]{:S(2)}) collective-permute-start(bf16[128,128]{1,0:T(8,128)(2,1)S(1)} %get-tuple-element.39), channel_id=1, source_target_pairs={{0,32},{4,36},{8,40},{12,44},{16,48},{20,52},{24,56},{28,60},{32,6... | collective-permute-start | bytes 98312 | tf_op jit(solution)/shard_map/ppermute | solution.py:471
  30.5 0.5 local_out.1
  31.0 0.5 collective-permute-done.1.end_ref
  31.5 0.3 starts.1
  31.8 10.8 %all_to_all.21.start_ref = bf16[8,128,128]{2,1,0:T(8,128)(2,1)S(1)} all-to-all(bf16[8,128,128]{2,1,0:T(8,128)(2,1)S(1)} %starts.1), channel_id=1, replica_groups={{0,4,8,12,16,20,24,28},{32,36,40,44,48,52,56,60},{64,68,72,76,80,84,88,..., dimensions={0} | all-to-all | bytes 524288 | tf_op jit(solution)/shard_map/all_to_all | solution.py:474
  42.6 0.0 copy-done
  42.6 1.1 project.1
  43.8 1.7 %collective-permute-start.2 = (bf16[32,2048]{1,0:T(8,128)(2,1)S(1)}, bf16[32,2048]{1,0:T(8,128)(2,1)S(1)}, u32[]{:S(2)}, u32[]{:S(2)}) collective-permute-start(bf16[32,2048]{1,0:T(8,128)(2,1)S(1)} %get-tuple-element.53), channel_id=1, source_target_pairs={{0,1},{1,2},{2,3},{3,0},{4,5},{5,6},{6,7},{7,4},{8,9},{9,10},{10,1... | collective-permute-start | bytes 393224 | tf_op jit(solution)/shard_map/ppermute | solution.py:490
  45.5 3.3 %collective-permute-start.3 = (bf16[32,2048]{1,0:T(8,128)(2,1)S(1)}, bf16[32,2048]{1,0:T(8,128)(2,1)S(1)}, u32[]{:S(2)}, u32[]{:S(2)}) collective-permute-start(bf16[32,2048]{1,0:T(8,128)(2,1)S(1)} %get-tuple-element.54), channel_id=1, source_target_pairs={{0,2},{1,3},{2,0},{3,1},{4,6},{5,7},{6,4},{7,5},{8,10},{9,11},{10,... | collective-permute-start | bytes 393224 | tf_op jit(solution)/shard_map/ppermute | solution.py:490
  48.8 0.8 collective-permute-start.4
  49.6 4.7 %fetch.1 = (bf16[2,2,2048,512]{3,2,1,0:T(8,128)(2,1)S(1)}, bf16[2,512,2048]{2,1,0:T(8,128)(2,1)S(1)}) custom-call(bf16[2,2,2048,512]{3,2,1,0:T(8,128)(2,1)} %gu_hbm.1, bf16[2,512,2048]{2,1,0:T(8,128)(2,1)} %down_hbm.1), custom_call_target="tpu_custom_call" | custom-call | bytes 12582912 | tf_op jit(solution)/shard_map/fetch/pallas_call | solution.py:42
  54.3 0.0 collective-permute-done.2.r1_ref
  54.3 0.0 collective-permute-done.3.r2_ref
  54.3 0.0 collective-permute-done.4.r3_ref
  54.4 1.3 route.1
  55.7 39.1 %all_to_all.22 = bf16[128,8,1024]{2,1,0:T(8,128)(2,1)S(1)} all-to-all(bf16[128,8,1024]{2,1,0:T(8,128)(2,1)S(1)} %bitcast.12), channel_id=1, replica_groups=mesh['seq'=32,'exp'=4] {'seq','exp'}, dimensions={0} | all-to-all | bytes 4194304 | tf_op jit(solution)/shard_map/all_to_all | solution.py:511
  94.8 5.6 %experts.1 = bf16[1024,1024]{1,0:T(8,128)(2,1)} custom-call(bf16[1024,1024]{1,0:T(8,128)(2,1)S(1)} %bitcast.11, bf16[2,2,2048,512]{3,2,1,0:T(8,128)(2,1)S(1)} %get-tuple-element.58.gu_ref, bf16[2,512,2048]{2,1,0:T(8,128)(2,1)S(1)} %get-tuple-element.59.down_ref), custom_call_target="tpu_custom_call" | custom-call | flops 4000000000 | bytes 14680064 | tf_op jit(solution)/shard_map/experts/pallas_call | solution.py:42
  100.4 0.0 copy-start.6
  100.4 3.7 %all-to-all-start.3 = ((bf16[128,8,1024]{2,1,0:T(8,128)(2,1)}), bf16[128,8,1024]{2,1,0:T(8,128)(2,1)S(1)}, u32[]{:S(2)}, u32[]{:S(2)}) async-start(bf16[128,8,1024]{2,1,0:T(8,128)(2,1)} %bitcast.18), calls=%async_computation.3 | async-start | bytes 4194304 | tf_op jit(solution)/shard_map/all_to_all | solution.py:539
  104.1 3.5 %shared.1.shared_ref = f32[32,2048]{1,0:T(8,128)S(1)} custom-call(bf16[32,2048]{1,0:T(8,128)(2,1)S(1)} %get-tuple-element.63.norm_ref, f32[1,2048]{1,0:T(1,128)S(1)} %bitcast.16, bf16[2,2048,512]{2,1,0:T(8,128)(2,1)} %sgu_hbm.1, bf16[512,2048]{1,0:T(8,128)(2,1)} %sdown_hbm.1), custom_call_target="tpu_custom_call" | custom-call | flops 200000000 | bytes 6430720 | tf_op jit(solution)/shard_map/shared/pallas_call | solution.py:42
  107.7 27.1 %all-to-all-done.3 = bf16[128,8,1024]{2,1,0:T(8,128)(2,1)S(1)} async-done(((bf16[128,8,1024]{2,1,0:T(8,128)(2,1)}), bf16[128,8,1024]{2,1,0:T(8,128)(2,1)S(1)}, u32[]{:S(2)}, u32[]{:S(2)}) %all-to-all-start.3) | async-done | bytes 2097184 | tf_op jit(solution)/shard_map/all_to_all | solution.py:539
  134.8 1.1 combine.1
  (11 shorter events, 0.0 us)
Async XLA Ops:
  1.4 7.5 %collective-permute-start = (bf16[8,2048]{1,0:T(8,128)(2,1)S(1)}, bf16[8,2048]{1,0:T(8,128)(2,1)S(1)}, u32[]{:S(2)}, u32[]{:S(2)}) collective-permute-start(bf16[8,2048]{1,0:T(8,128)(2,1)S(1)} %rim.1), channel_id=1, source_target_pairs={{0,4},{4,8},{8,12},{12,16},{16,20},{20,24},{24,28},{28,32},{32,36}... | collective-permute-start | bytes 98312 | tf_op jit(solution)/shard_map/ppermute | solution.py:419
  12.6 30.0 %copy-start = (bf16[1024,2048]{1,0:T(8,128)(2,1)S(1)}, bf16[1024,2048]{1,0:T(8,128)(2,1)}, u32[]{:S(2)}) copy-start(bf16[1024,2048]{1,0:T(8,128)(2,1)} %w_ref.1) | copy-start | bytes 12582916
  12.6 30.0 %copy-start.1 = (bf16[128,1024]{1,0:T(8,128)(2,1)S(1)}, bf16[128,1024]{1,0:T(8,128)(2,1)}, u32[]{:S(2)}) copy-start(bf16[128,1024]{1,0:T(8,128)(2,1)} %z_ref.1) | copy-start | bytes 786436
  12.6 30.0 %copy-start.7 = (f32[128]{0:T(128)S(1)}, f32[128]{0:T(128)}, u32[]{:S(2)}) copy-start(f32[128]{0:T(128)} %param.27) | copy-start | bytes 1540
  27.3 4.2 %collective-permute-start.1 = (bf16[128,128]{1,0:T(8,128)(2,1)S(1)}, bf16[128,128]{1,0:T(8,128)(2,1)S(1)}, u32[]{:S(2)}, u32[]{:S(2)}) collective-permute-start(bf16[128,128]{1,0:T(8,128)(2,1)S(1)} %get-tuple-element.39), channel_id=1, source_target_pairs={{0,32},{4,36},{8,40},{12,44},{16,48},{20,52},{24,56},{28,60},{32,6... | collective-permute-start | bytes 98312 | tf_op jit(solution)/shard_map/ppermute | solution.py:471
  43.8 10.5 %collective-permute-start.2 = (bf16[32,2048]{1,0:T(8,128)(2,1)S(1)}, bf16[32,2048]{1,0:T(8,128)(2,1)S(1)}, u32[]{:S(2)}, u32[]{:S(2)}) collective-permute-start(bf16[32,2048]{1,0:T(8,128)(2,1)S(1)} %get-tuple-element.53), channel_id=1, source_target_pairs={{0,1},{1,2},{2,3},{3,0},{4,5},{5,6},{6,7},{7,4},{8,9},{9,10},{10,1... | collective-permute-start | bytes 393224 | tf_op jit(solution)/shard_map/ppermute | solution.py:490
  45.5 8.8 %collective-permute-start.3 = (bf16[32,2048]{1,0:T(8,128)(2,1)S(1)}, bf16[32,2048]{1,0:T(8,128)(2,1)S(1)}, u32[]{:S(2)}, u32[]{:S(2)}) collective-permute-start(bf16[32,2048]{1,0:T(8,128)(2,1)S(1)} %get-tuple-element.54), channel_id=1, source_target_pairs={{0,2},{1,3},{2,0},{3,1},{4,6},{5,7},{6,4},{7,5},{8,10},{9,11},{10,... | collective-permute-start | bytes 393224 | tf_op jit(solution)/shard_map/ppermute | solution.py:490
  48.8 5.6 %copy-start.2 = (bf16[32,2048]{1,0:T(8,128)(2,1)S(1)}, bf16[32,2048]{1,0:T(8,128)(2,1)}, u32[]{:S(2)}) copy-start(bf16[32,2048]{1,0:T(8,128)(2,1)} %res_ref.1) | copy-start | bytes 393220
  48.8 5.6 %copy-start.3 = (f32[2048]{0:T(1024)S(1)}, f32[2048]{0:T(1024)}, u32[]{:S(2)}) copy-start(f32[2048]{0:T(1024)} %param.30) | copy-start | bytes 24580
  48.8 5.6 %copy-start.4 = (s32[32,10]{0,1:T(8,128)S(1)}, s32[32,10]{0,1:T(8,128)}, u32[]{:S(2)}) copy-start(s32[32,10]{0,1:T(8,128)} %param.31) | copy-start | bytes 3844
  48.8 5.6 %copy-start.5 = (f32[32,10]{0,1:T(8,128)S(1)}, f32[32,10]{0,1:T(8,128)}, u32[]{:S(2)}) copy-start(f32[32,10]{0,1:T(8,128)} %param.32) | copy-start | bytes 3844
  48.8 5.5 %collective-permute-start.4 = (bf16[32,2048]{1,0:T(8,128)(2,1)S(1)}, bf16[32,2048]{1,0:T(8,128)(2,1)S(1)}, u32[]{:S(2)}, u32[]{:S(2)}) collective-permute-start(bf16[32,2048]{1,0:T(8,128)(2,1)S(1)} %get-tuple-element.55), channel_id=1, source_target_pairs={{0,3},{1,0},{2,1},{3,2},{4,7},{5,4},{6,5},{7,6},{8,11},{9,8},{10,9... | collective-permute-start | bytes 393224 | tf_op jit(solution)/shard_map/ppermute | solution.py:490
  100.4 3.7 %copy-start.6 = (f32[2048]{0:T(1024)S(1)}, f32[2048]{0:T(1024)}, u32[]{:S(2)}) copy-start(f32[2048]{0:T(1024)} %param.37) | copy-start | bytes 24580
  100.4 34.4 %all-to-all-start.3 = ((bf16[128,8,1024]{2,1,0:T(8,128)(2,1)}), bf16[128,8,1024]{2,1,0:T(8,128)(2,1)S(1)}, u32[]{:S(2)}, u32[]{:S(2)}) async-start(bf16[128,8,1024]{2,1,0:T(8,128)(2,1)} %bitcast.18), calls=%async_computation.3 | async-start | bytes 4194304 | tf_op jit(solution)/shard_map/all_to_all | solution.py:539

commit v4 on v3

--- a/solution.py
+++ b/solution.py
@@ -2,6 +2,7 @@
 
 import jax
 import jax.numpy as jnp
+import numpy as np
 from jax import lax
 from jax.experimental import pallas as pl
 from jax.experimental.pallas import tpu as pltpu
@@ -74,39 +75,26 @@
     return dotb(jnp.concatenate([ah, al, ah], axis=ca), jnp.concatenate([bh, bh, bl], axis=cb), ca, cb)
 
 
-def rim_kernel(qk_hbm, v_hbm, rim_ref, qk_ref, v_ref, sem):
-    tail = pl.ds(L - 8, 8)
-    copies = [
-        pltpu.make_async_copy(qk_hbm.at[tail], qk_ref, sem.at[0]),
-        pltpu.make_async_copy(v_hbm.at[tail], v_ref, sem.at[1]),
-    ]
+def rim_kernel(*refs):
+    n = (len(refs) - 2) // 2
+    sources, rim_ref, near_refs, sem = refs[:n], refs[n], refs[n + 1 : -1], refs[-1]
+    copies = [pltpu.make_async_copy(src, dst, sem.at[i]) for i, (src, dst) in enumerate(zip(sources, near_refs))]
     for copy in copies:
         copy.start()
-    for copy in copies:
-        copy.wait()
+    copies[0].wait()
+    copies[1].wait()
+    qk_ref, v_ref = near_refs[:2]
     kw = qk_ref.shape[2]
     for z in range(2):
-        rim_ref[:, z * kw : (z + 1) * kw] = qk_ref[:, z, :]
-    rim_ref[:, 2 * kw :] = v_ref[...]
-
-
-def prep_kernel(qk_hbm, v_hbm, cqk_hbm, cv_hbm, decay_hbm, beta_hbm, doc_hbm, conv_ref, edge_ref, within_ref, sys_ref, cols_ref, qk_ref, v_ref, cqk_ref, cv_ref, db_ref, doc_ref, sem):
-    kw = qk_hbm.shape[2]
-    vw = v_hbm.shape[1]
-    pairs = (
-        (doc_hbm, doc_ref),
-        (decay_hbm, db_ref.at[0]),
-        (beta_hbm, db_ref.at[1]),
-        (cqk_hbm, cqk_ref),
-        (cv_hbm, cv_ref),
-        (qk_hbm, qk_ref),
-        (v_hbm, v_ref),
-    )
-    copies = [pltpu.make_async_copy(src, dst, sem.at[i]) for i, (src, dst) in enumerate(pairs)]
-    for copy in copies:
-        copy.start()
-    for copy in copies[:3]:
+        rim_ref[:, z * kw : (z + 1) * kw] = qk_ref[L - 8 :, z, :]
+    rim_ref[:, 2 * kw :] = v_ref[L - 8 :]
+    for copy in copies[2:]:
         copy.wait()
+
+
+def prep_kernel(qk_ref, v_ref, cqk_ref, cv_ref, decay_ref, beta_ref, doc_ref, conv_ref, edge_ref, within_ref, sys_ref, cols_ref):
+    kw = qk_ref.shape[2]
+    vw = v_ref.shape[1]
     me = lax.axis_index("seq")
     cur = doc_ref[pl.ds(me, 1), :]
     prev = doc_ref[pl.ds(jnp.maximum(me - 1, 0), 1), :]
@@ -115,7 +103,7 @@
     prev8 = jnp.broadcast_to(prev, (8, L)).astype(F32)
     lane8 = iota((8, L), 1)
     row8 = iota((8, L), 0)
-    cum = db_ref[0]
+    cum = decay_ref[...]
     for step in (1, 2, 4, 8, 16, 32, 64):
         cum = cum + jnp.where(lane8 >= step, pltpu.roll(cum, step, 1), 0.0)
     flags = (cur8 == prev8[:, L - 1 :]).astype(F32)
@@ -128,7 +116,7 @@
     end_same = cur8 == cur8[:, last:]
     carried = jnp.exp(cum) * (cur8 == prev8[:, last:]).astype(F32)
     ends = jnp.where(end_same, jnp.exp(jnp.where(end_same, cum[:, last:] - cum, 0.0)), 0.0)
-    rows = jnp.concatenate([cum, db_ref[1], flags, carried, ends, jnp.zeros((L - 40, L), F32)], axis=0)
+    rows = jnp.concatenate([cum, beta_ref[...], flags, carried, ends, jnp.zeros((L - 40, L), F32)], axis=0)
     cols = rows.T
     cols_ref[...] = cols
     doc_col = cols[:, 20:21]
@@ -140,8 +128,6 @@
         within = jnp.where(keep, jnp.exp(jnp.where(keep, spread, 0.0)), 0.0)
         within_ref[h] = within
         sys_ref[h] = jnp.where(strict, cols[:, 8 + h : 9 + h] * within, 0.0)
-    for copy in copies[3:]:
-        copy.wait()
 
     def taps(i, at, half):
         if half is None:
@@ -274,7 +260,7 @@
         ref[...] = part_ref[pl.ds(pl.multiple_of(to * n, n), n)].astype(BF16)
 
 
-def route_kernel(own_ref, r1_ref, r2_ref, r3_ref, res_ref, gain_ref, ids_ref, wt_ref, mid_ref, norm_ref, send_ref, pick_ref):
+def route_kernel(own_ref, r1_ref, r2_ref, r3_ref, res_ref, gain_ref, ids_ref, wt_ref, to_ref, mid_ref, norm_ref, send_ref, pick_ref):
     hidden = own_ref[...] + r1_ref[...].astype(F32) + r2_ref[...].astype(F32) + r3_ref[...].astype(F32)
     hidden = res_ref[...].astype(F32) + hidden
     mid_ref[...] = hidden.astype(BF16)
@@ -285,7 +271,6 @@
     half = width // 2
     slots = send_ref.shape[0]
     col = iota((tokens, slots), 1)
-    expert = col // 4
     rank = (col // 2) % 2
     named = jnp.zeros((tokens, slots), F32)
     weight = jnp.zeros((tokens, slots), F32)
@@ -293,7 +278,7 @@
     same = (ti == tj).astype(F32)
     ids = dotf(same, ids_ref[...].astype(F32), 1, 1)
     weights = dotf(same, wt_ref[...], 1, 1)
-    expert = expert.astype(F32)
+    expert = to_ref[...].astype(F32)
     for k in range(ids_ref.shape[0]):
         hit = expert == ids[:, k : k + 1]
         named = jnp.where(hit, 1.0, named)
@@ -336,37 +321,54 @@
         copy.wait()
 
 
-def expert_kernel(recv_ref, gu_ref, down_ref, out_hbm, flat_ref, x_ref, out_ref, sem):
+def expert_kernel(recv_ref, gu_ref, down_ref, out_hbm, flat_ref, made_ref, x0_ref, x1_ref, out_ref, sem):
     rows, half = recv_ref.shape
     srcs = rows // 8
     flat = functools.partial(pl.ds, size=srcs, stride=8)
-    lanes = 128
+    lanes, wide = 128, 256
+    x_refs = (x0_ref, x1_ref)
+
+    def gather(e, c):
+        for r in range(2):
+            for b in range(2):
+                to = slice(b * half + c * lanes, b * half + (c + 1) * lanes)
+                x_refs[e][r * srcs : (r + 1) * srcs, to] = flat_ref[c, flat(4 * e + 2 * r + b), :].astype(BF16)
+
+    def down(e, act, p):
+        for b in range(2):
+            y = dotb(act, down_ref[e, :, b * half + p * wide : b * half + (p + 1) * wide])
+            for r in range(2):
+                for c in range(2):
+                    made_ref[2 * p + c, flat(4 * e + 2 * r + b), :] = y[r * srcs : (r + 1) * srcs, c * lanes : (c + 1) * lanes]
+
+    def hidden(e, n):
+        at = slice(n * wide, (n + 1) * wide)
+        x = x_refs[e][...]
+        return (silu(dotb(x, gu_ref[e, 0, :, at])) * dotb(x, gu_ref[e, 1, :, at])).astype(BF16)
+
     for c in range(half // lanes):
-        at = slice(c * lanes, (c + 1) * lanes)
-        flat_ref[c] = recv_ref[:, at].astype(F32)
-        for e in range(2):
-            for r in range(2):
-                for b in range(2):
-                    x_ref[e, r * srcs : (r + 1) * srcs, b * half + c * lanes : b * half + (c + 1) * lanes] = flat_ref[
-                        c, flat(4 * e + 2 * r + b), :
-                    ].astype(BF16)
+        flat_ref[c] = recv_ref[:, c * lanes : (c + 1) * lanes].astype(F32)
+        gather(0, c)
+    parts = gu_ref.shape[3] // wide
+    per = half // lanes // parts
     acts = []
-    for e in range(2):
-        x = x_ref[e]
-        acts.append((silu(dotb(x, gu_ref[e, 0])) * dotb(x, gu_ref[e, 1])).astype(BF16))
-    wide = 2 * lanes
+    for n in range(parts):
+        acts.append(hidden(0, n))
+        for c in range(n * per, (n + 1) * per):
+            gather(1, c)
+    first = jnp.concatenate(acts, axis=1)
+    acts = []
+    share = half // wide // parts
+    for n in range(parts):
+        acts.append(hidden(1, n))
+        for p in range(n * share, (n + 1) * share):
+            down(0, first, p)
+    second = jnp.concatenate(acts, axis=1)
     copies = []
     for p in range(half // wide):
-        for e in range(2):
-            for b in range(2):
-                y = dotb(acts[e], down_ref[e, :, b * half + p * wide : b * half + (p + 1) * wide])
-                for r in range(2):
-                    for c in range(2):
-                        flat_ref[2 * p + c, flat(4 * e + 2 * r + b), :] = y[
-                            r * srcs : (r + 1) * srcs, c * lanes : (c + 1) * lanes
-                        ]
+        down(1, second, p)
         for c in (2 * p, 2 * p + 1):
-            out_ref[:, c * lanes : (c + 1) * lanes] = flat_ref[c].astype(BF16)
+            out_ref[:, c * lanes : (c + 1) * lanes] = made_ref[c].astype(BF16)
         at = slice(p * wide, (p + 1) * wide)
         copies.append(pltpu.make_async_copy(out_ref.at[:, at], out_hbm.at[:, at], sem.at[p]))
         copies[-1].start()
@@ -381,6 +383,10 @@
     got = got[: 2 * n] + got[2 * n :]
     out_ref[:, :half] = (got[:n] + shared_ref[:, :half]).astype(BF16)
     out_ref[:, half:] = (got[n:] + shared_ref[:, half:]).astype(BF16)
+
+
+def exchange_order(seq_n, exp_n):
+    return [s * exp_n + e for c in range(2) for s in range(c, seq_n, 2) for e in range(exp_n)]
 
 
 def shards(
@@ -408,12 +414,13 @@
     runs = [[g * RUN + i for i in range(RUN)] for g in range(seq_n // RUN)]
     kw, vw = qk_proj.shape[2], v_proj.shape[1]
     wide = 2 * kw + vw
-    rim = call(
+    raw = (qk_proj, v_proj, conv_qk, conv_v, decay_log, beta_gate, doc_ids.reshape(seq_n, L))
+    rim, *held = call(
         rim_kernel,
-        (near((8, wide), BF16),),
-        qk_proj, v_proj,
-        hbm=(0, 1),
-        scratch=[pltpu.VMEM((8, 2, kw), BF16), pltpu.VMEM((8, vw), BF16), pltpu.SemaphoreType.DMA((2,))],
+        (near((8, wide), BF16), *(near(a.shape, a.dtype) for a in raw)),
+        *raw,
+        hbm=range(len(raw)),
+        scratch=[pltpu.SemaphoreType.DMA((len(raw),))],
         name="rim",
     )
     halo = lax.ppermute(rim, "seq", [(i, i + 1) for i in range(seq_n - 1)])
@@ -427,17 +434,7 @@
             near((HEADS, L, L), F32),
             near((L, L), F32),
         ),
-        qk_proj, v_proj, conv_qk, conv_v, decay_log, beta_gate, doc_ids.reshape(seq_n, L),
-        hbm=range(7),
-        scratch=[
-            pltpu.VMEM((L, 2, kw), BF16),
-            pltpu.VMEM((L, vw), BF16),
-            pltpu.VMEM(conv_qk.shape, F32),
-            pltpu.VMEM(conv_v.shape, F32),
-            pltpu.VMEM((2, HEADS, L), F32),
-            pltpu.VMEM((seq_n, L), jnp.int32),
-            pltpu.SemaphoreType.DMA((7,)),
-        ],
+        *held,
         flops=10**8,
         name="prep",
     )
@@ -500,22 +497,27 @@
     devices = seq_n * exp_n
     slots = devices * 8
     half = model // 2
+    order = exchange_order(seq_n, exp_n)
+    experts_at = np.repeat(2 * np.asarray(order, np.int32), 8).reshape(1, slots)
+    experts_at = experts_at + (np.arange(slots, dtype=np.int32) // 4 % 2)
     hidden_mid, normed, send, pick = call(
         route_kernel,
         (free((rows, model), BF16), piece, near((slots, half), BF16), near((4 * rows, slots), BF16)),
-        own, got[1], got[2], got[3], residual, post_gain.reshape(1, model), route_ids.T, route_weight.T,
+        own, got[1], got[2], got[3], residual, post_gain.reshape(1, model), route_ids.T, route_weight.T, jnp.asarray(experts_at),
         flops=2 * 10**8,
         name="route",
     )
     axes = ("seq", "exp")
-    recv = lax.all_to_all(send.reshape(devices, 8, half), axes, split_axis=0, concat_axis=0, tiled=True)
+    recv = lax.all_to_all(send.reshape(devices, 8, half), axes, split_axis=0, concat_axis=0, tiled=True, axis_index_groups=[order])
     made = call(
         expert_kernel,
         (far((slots, half), BF16),),
         recv.reshape(slots, half), gu_near, down_near,
         scratch=[
             pltpu.VMEM((half // 128, slots, 128), F32),
-            pltpu.VMEM((2, 2 * devices, model), BF16),
+            pltpu.VMEM((half // 128, slots, 128), F32),
+            pltpu.VMEM((2 * devices, model), BF16),
+            pltpu.VMEM((2 * devices, model), BF16),
             pltpu.VMEM((slots, half), BF16),
             pltpu.SemaphoreType.DMA((half // 256,)),
         ],
@@ -536,7 +538,7 @@
         flops=2 * 10**8,
         name="shared",
     )
-    back = lax.all_to_all(made.reshape(devices, 8, half), axes, split_axis=0, concat_axis=0, tiled=True)
+    back = lax.all_to_all(made.reshape(devices, 8, half), axes, split_axis=0, concat_axis=0, tiled=True, axis_index_groups=[order])
     moe_out = call(
         combine_kernel,
         (free((rows, model), BF16),),

time: 136 us -> 135 us (level)
  starting transfers between devices: 17.2 us -> 20.4 us
  waiting for transfers between devices: 27.7 us -> 25.5 us
  blocking collectives: 63.4 us -> 61.9 us
    all_to_all x1, starting transfers between devices: 3.7 us -> 6.53 us  [shards(): lax.all_to_all(made.reshape(devices, 8, half), axes, split_axis=0, concat...]
    all_to_all x1, waiting for transfers between devices: 27.1 us -> 25 us  [shards(): lax.all_to_all(made.reshape(devices, 8, half), axes, split_axis=0, concat...]
    all_to_all x1, blocking collectives: 39.1 us -> 37.1 us  [shards(): lax.all_to_all(send.reshape(devices, 8, half), axes, split_axis=0, concat...]
  transfers between devices with their start and end apart: 6 -> 6, of which waited for: 2 -> 2; matrix products, arithmetic and copies ran while one was open for 0% -> 0% of each run, Pallas kernels for 9% -> 8%
where the time goes in v4:
time: 135 us
  blocking collectives  61.9 us (46%)
  Pallas kernels  26 us (19%)
  waiting for transfers between devices  25.5 us (19%)
  starting transfers between devices  20.4 us (15%)
    all_to_all x1, blocking collectives, shards(): lax.all_to_all(send.reshape(devices, 8, half), axes, split_axis=0, concat...  37.1 us
    pallas_call x12, Pallas kernels, call(): pl.pallas_call(body, out_shape=[place(o.shape, o.dtype) if place else o f...  26 us
    all_to_all x1, waiting for transfers between devices, shards(): lax.all_to_all(made.reshape(devices, 8, half), axes, split_axis=0, concat...  25 us
    all_to_all x1, blocking collectives, shards(): lax.all_to_all(maps, 'seq', split_axis=0, concat_axis=0, tiled=True, axis...  14 us
    all_to_all x1, blocking collectives, shards(): lax.all_to_all(starts, 'seq', split_axis=0, concat_axis=0, tiled=True, ax...  10.8 us
    all_to_all x1, starting transfers between devices, shards(): lax.all_to_all(made.reshape(devices, 8, half), axes, split_axis=0, concat...  6.53 us
    ppermute x3, starting transfers between devices, shards(): lax.ppermute(sends[s - 1], 'exp', [(i, (i + s) % exp_n) for i in range(ex...  5.81 us
    ppermute x1, starting transfers between devices, shards(): halo = lax.ppermute(rim, 'seq', [(i, i + 1) for i in range(seq_n - 1)])  4.5 us
  transfers between devices with their start and end apart: 6, of which 2 were waited for; matrix products, arithmetic and copies ran while one was open for 0% of the time, Pallas kernels for 8%

profile of v4, /device:TPU:1, one launch (start us, length us, event | category | flops | bytes accessed | tf_op | source)
XLA Modules:
  0.0 134.8 jit_solution(9567209580598418130)
XLA Ops:
  0.6 1.1 rim.1
  1.8 4.5 %collective-permute-start = (bf16[8,2048]{1,0:T(8,128)(2,1)S(1)}, bf16[8,2048]{1,0:T(8,128)(2,1)S(1)}, u32[]{:S(2)}, u32[]{:S(2)}) collective-permute-start(bf16[8,2048]{1,0:T(8,128)(2,1)S(1)} %get-tuple-element.50), channel_id=1, source_target_pairs={{0,4},{4,8},{8,12},{12,16},{16,20},{20,24},{24,28},{28,32},{32,36}... | collective-permute-start | bytes 98312 | tf_op jit(solution)/shard_map/ppermute | solution.py:426
  6.3 1.9 %prep.1 = (f32[128,2048]{1,0:T(8,128)S(1)}, f32[16,2048]{1,0:T(8,128)S(1)}, f32[8,128,128]{2,1,0:T(8,128)S(1)}, f32[8,128,128]{2,1,0:T(8,128)S(1)}, f32[128,128]{1,0:T(8,128)S(1)}) custom-call(bf16[128,2,512]{2,1,0:T(2,128)(2,1)S(1)} %get-tuple-element.41.qk_ref, bf16[128,1024]{1,0:T(8,128)(2,1)S(1)} %get-tuple-element.42.v_ref, ...), custom_call_target="tpu_custom_call" | custom-call | flops 100000000 | bytes 581632 | tf_op jit(solution)/shard_map/prep/pallas_call | solution.py:43
  8.2 0.0 collective-permute-done.halo_ref
  8.2 3.7 %maps.1 = (bf16[8,256,128]{2,1,0:T(8,128)(2,1)S(1)}, f32[8,128,128]{2,1,0:T(8,128)S(1)}, f32[8,128,256]{2,1,0:T(8,128)S(1)}, f32[8,128,128]{2,1,0:T(8,128)S(1)}) custom-call(f32[128,2048]{1,0:T(8,128)S(1)} %get-tuple-element.48.conv_ref, f32[16,2048]{1,0:T(8,128)S(1)} %get-tuple-element.49.edge_ref, bf16[8,2048]{1,0:T(8,128)(2,1)S(1)} %collective-permute-done.halo_ref, ...), custom_call_target="tpu_custom_call" | custom-call | flops 2000000000 | bytes 2326528 | tf_op jit(solution)/shard_map/maps/pallas_call | solution.py:43
  11.9 0.0 copy-start
  11.9 0.0 copy-start.1
  11.9 0.0 copy-start.8
  12.0 14.0 %all_to_all.20.maps_ref = bf16[8,256,128]{2,1,0:T(8,128)(2,1)S(1)} all-to-all(bf16[8,256,128]{2,1,0:T(8,128)(2,1)S(1)} %get-tuple-element.54), channel_id=1, replica_groups={{0,4,8,12,16,20,24,28},{32,36,40,44,48,52,56,60},{64,68,72,76,80,84,88,..., dimensions={0} | all-to-all | bytes 1048576 | tf_op jit(solution)/shard_map/all_to_all | solution.py:453
  25.9 1.2 chain.1
  27.1 3.6 %collective-permute-start.1 = (bf16[128,128]{1,0:T(8,128)(2,1)S(1)}, bf16[128,128]{1,0:T(8,128)(2,1)S(1)}, u32[]{:S(2)}, u32[]{:S(2)}) collective-permute-start(bf16[128,128]{1,0:T(8,128)(2,1)S(1)} %get-tuple-element.55), channel_id=1, source_target_pairs={{0,32},{4,36},{8,40},{12,44},{16,48},{20,52},{24,56},{28,60},{32,6... | collective-permute-start | bytes 98312 | tf_op jit(solution)/shard_map/ppermute | solution.py:468
  30.7 0.5 local_out.1
  31.2 0.5 collective-permute-done.1.end_ref
  31.7 0.3 starts.1
  32.0 10.8 %all_to_all.21.start_ref = bf16[8,128,128]{2,1,0:T(8,128)(2,1)S(1)} all-to-all(bf16[8,128,128]{2,1,0:T(8,128)(2,1)S(1)} %starts.1), channel_id=1, replica_groups={{0,4,8,12,16,20,24,28},{32,36,40,44,48,52,56,60},{64,68,72,76,80,84,88,..., dimensions={0} | all-to-all | bytes 524288 | tf_op jit(solution)/shard_map/all_to_all | solution.py:471
  42.8 1.1 project.1
  44.0 1.7 %collective-permute-start.2 = (bf16[32,2048]{1,0:T(8,128)(2,1)S(1)}, bf16[32,2048]{1,0:T(8,128)(2,1)S(1)}, u32[]{:S(2)}, u32[]{:S(2)}) collective-permute-start(bf16[32,2048]{1,0:T(8,128)(2,1)S(1)} %get-tuple-element.69), channel_id=1, source_target_pairs={{0,1},{1,2},{2,3},{3,0},{4,5},{5,6},{6,7},{7,4},{8,9},{9,10},{10,1... | collective-permute-start | bytes 393224 | tf_op jit(solution)/shard_map/ppermute | solution.py:487
  45.7 3.3 %collective-permute-start.3 = (bf16[32,2048]{1,0:T(8,128)(2,1)S(1)}, bf16[32,2048]{1,0:T(8,128)(2,1)S(1)}, u32[]{:S(2)}, u32[]{:S(2)}) collective-permute-start(bf16[32,2048]{1,0:T(8,128)(2,1)S(1)} %get-tuple-element.70), channel_id=1, source_target_pairs={{0,2},{1,3},{2,0},{3,1},{4,6},{5,7},{6,4},{7,5},{8,10},{9,11},{10,... | collective-permute-start | bytes 393224 | tf_op jit(solution)/shard_map/ppermute | solution.py:487
  49.0 0.0 copy-start.7
  49.0 0.8 collective-permute-start.4
  49.8 4.7 %fetch.1 = (bf16[2,2,2048,512]{3,2,1,0:T(8,128)(2,1)S(1)}, bf16[2,512,2048]{2,1,0:T(8,128)(2,1)S(1)}) custom-call(bf16[2,2,2048,512]{3,2,1,0:T(8,128)(2,1)} %gu_hbm.1, bf16[2,512,2048]{2,1,0:T(8,128)(2,1)} %down_hbm.1), custom_call_target="tpu_custom_call" | custom-call | bytes 12582912 | tf_op jit(solution)/shard_map/fetch/pallas_call | solution.py:43
  54.5 0.0 collective-permute-done.2.r1_ref
  54.5 0.0 collective-permute-done.3.r2_ref
  54.5 0.0 collective-permute-done.4.r3_ref
  54.6 1.3 route.1
  55.9 37.1 %all_to_all.22 = bf16[128,8,1024]{2,1,0:T(8,128)(2,1)S(1)} all-to-all(bf16[128,8,1024]{2,1,0:T(8,128)(2,1)S(1)} %bitcast.12), channel_id=1, replica_groups={{0,1,2,3,8,9,10,11,16,17,18,19,24,25,26,27,32,33,34,35,40,41,42,43,48,4..., dimensions={0} | all-to-all | bytes 4194304 | tf_op jit(solution)/shard_map/all_to_all | solution.py:511
  93.0 5.6 %experts.1 = bf16[1024,1024]{1,0:T(8,128)(2,1)} custom-call(bf16[1024,1024]{1,0:T(8,128)(2,1)S(1)} %bitcast.11, bf16[2,2,2048,512]{3,2,1,0:T(8,128)(2,1)S(1)} %get-tuple-element.74.gu_ref, bf16[2,512,2048]{2,1,0:T(8,128)(2,1)S(1)} %get-tuple-element.75.down_ref), custom_call_target="tpu_custom_call" | custom-call | flops 4000000000 | bytes 14680064 | tf_op jit(solution)/shard_map/experts/pallas_call | solution.py:43
  98.6 0.0 copy-start.6
  98.6 6.5 %all-to-all-start.3 = ((bf16[128,8,1024]{2,1,0:T(8,128)(2,1)}), bf16[128,8,1024]{2,1,0:T(8,128)(2,1)S(1)}, u32[]{:S(2)}, u32[]{:S(2)}) async-start(bf16[128,8,1024]{2,1,0:T(8,128)(2,1)} %bitcast.18), calls=%async_computation.3 | async-start | bytes 4194304 | tf_op jit(solution)/shard_map/all_to_all | solution.py:541
  105.2 3.5 %shared.1.shared_ref = f32[32,2048]{1,0:T(8,128)S(1)} custom-call(bf16[32,2048]{1,0:T(8,128)(2,1)S(1)} %get-tuple-element.79.norm_ref, f32[1,2048]{1,0:T(1,128)S(1)} %bitcast.16, bf16[2,2048,512]{2,1,0:T(8,128)(2,1)} %sgu_hbm.1, bf16[512,2048]{1,0:T(8,128)(2,1)} %sdown_hbm.1), custom_call_target="tpu_custom_call" | custom-call | flops 200000000 | bytes 6430720 | tf_op jit(solution)/shard_map/shared/pallas_call | solution.py:43
  108.7 25.0 %all-to-all-done.3 = bf16[128,8,1024]{2,1,0:T(8,128)(2,1)S(1)} async-done(((bf16[128,8,1024]{2,1,0:T(8,128)(2,1)}), bf16[128,8,1024]{2,1,0:T(8,128)(2,1)S(1)}, u32[]{:S(2)}, u32[]{:S(2)}) %all-to-all-start.3) | async-done | bytes 2097184 | tf_op jit(solution)/shard_map/all_to_all | solution.py:541
  133.7 1.1 combine.1
  (13 shorter events, 0.0 us)
Async XLA Ops:
  1.8 6.4 %collective-permute-start = (bf16[8,2048]{1,0:T(8,128)(2,1)S(1)}, bf16[8,2048]{1,0:T(8,128)(2,1)S(1)}, u32[]{:S(2)}, u32[]{:S(2)}) collective-permute-start(bf16[8,2048]{1,0:T(8,128)(2,1)S(1)} %get-tuple-element.50), channel_id=1, source_target_pairs={{0,4},{4,8},{8,12},{12,16},{16,20},{20,24},{24,28},{28,32},{32,36}... | collective-permute-start | bytes 98312 | tf_op jit(solution)/shard_map/ppermute | solution.py:426
  11.9 30.9 %copy-start = (bf16[1024,2048]{1,0:T(8,128)(2,1)S(1)}, bf16[1024,2048]{1,0:T(8,128)(2,1)}, u32[]{:S(2)}) copy-start(bf16[1024,2048]{1,0:T(8,128)(2,1)} %w_ref.1) | copy-start | bytes 12582916
  11.9 30.9 %copy-start.1 = (bf16[128,1024]{1,0:T(8,128)(2,1)S(1)}, bf16[128,1024]{1,0:T(8,128)(2,1)}, u32[]{:S(2)}) copy-start(bf16[128,1024]{1,0:T(8,128)(2,1)} %z_ref.1) | copy-start | bytes 786436
  11.9 30.9 %copy-start.8 = (f32[128]{0:T(128)S(1)}, f32[128]{0:T(128)}, u32[]{:S(2)}) copy-start(f32[128]{0:T(128)} %param.28) | copy-start | bytes 1540
  27.1 4.6 %collective-permute-start.1 = (bf16[128,128]{1,0:T(8,128)(2,1)S(1)}, bf16[128,128]{1,0:T(8,128)(2,1)S(1)}, u32[]{:S(2)}, u32[]{:S(2)}) collective-permute-start(bf16[128,128]{1,0:T(8,128)(2,1)S(1)} %get-tuple-element.55), channel_id=1, source_target_pairs={{0,32},{4,36},{8,40},{12,44},{16,48},{20,52},{24,56},{28,60},{32,6... | collective-permute-start | bytes 98312 | tf_op jit(solution)/shard_map/ppermute | solution.py:468
  44.0 10.5 %collective-permute-start.2 = (bf16[32,2048]{1,0:T(8,128)(2,1)S(1)}, bf16[32,2048]{1,0:T(8,128)(2,1)S(1)}, u32[]{:S(2)}, u32[]{:S(2)}) collective-permute-start(bf16[32,2048]{1,0:T(8,128)(2,1)S(1)} %get-tuple-element.69), channel_id=1, source_target_pairs={{0,1},{1,2},{2,3},{3,0},{4,5},{5,6},{6,7},{7,4},{8,9},{9,10},{10,1... | collective-permute-start | bytes 393224 | tf_op jit(solution)/shard_map/ppermute | solution.py:487
  45.7 8.8 %collective-permute-start.3 = (bf16[32,2048]{1,0:T(8,128)(2,1)S(1)}, bf16[32,2048]{1,0:T(8,128)(2,1)S(1)}, u32[]{:S(2)}, u32[]{:S(2)}) collective-permute-start(bf16[32,2048]{1,0:T(8,128)(2,1)S(1)} %get-tuple-element.70), channel_id=1, source_target_pairs={{0,2},{1,3},{2,0},{3,1},{4,6},{5,7},{6,4},{7,5},{8,10},{9,11},{10,... | collective-permute-start | bytes 393224 | tf_op jit(solution)/shard_map/ppermute | solution.py:487
  49.0 5.6 %copy-start.2 = (bf16[32,2048]{1,0:T(8,128)(2,1)S(1)}, bf16[32,2048]{1,0:T(8,128)(2,1)}, u32[]{:S(2)}) copy-start(bf16[32,2048]{1,0:T(8,128)(2,1)} %res_ref.1) | copy-start | bytes 393220
  49.0 5.6 %copy-start.3 = (f32[2048]{0:T(1024)S(1)}, f32[2048]{0:T(1024)}, u32[]{:S(2)}) copy-start(f32[2048]{0:T(1024)} %param.31) | copy-start | bytes 24580
  49.0 5.6 %copy-start.4 = (s32[32,10]{0,1:T(8,128)S(1)}, s32[32,10]{0,1:T(8,128)}, u32[]{:S(2)}) copy-start(s32[32,10]{0,1:T(8,128)} %param.32) | copy-start | bytes 3844
  49.0 5.6 %copy-start.5 = (f32[32,10]{0,1:T(8,128)S(1)}, f32[32,10]{0,1:T(8,128)}, u32[]{:S(2)}) copy-start(f32[32,10]{0,1:T(8,128)} %param.33) | copy-start | bytes 3844
  49.0 5.6 %copy-start.7 = (s32[1,1024]{1,0:T(1,128)S(1)}, s32[1,1024]{1,0:T(1,128)}, u32[]{:S(2)}) copy-start(s32[1,1024]{1,0:T(1,128)} %constant.2.clone.to_ref) | copy-start | bytes 12292
  49.0 5.5 %collective-permute-start.4 = (bf16[32,2048]{1,0:T(8,128)(2,1)S(1)}, bf16[32,2048]{1,0:T(8,128)(2,1)S(1)}, u32[]{:S(2)}, u32[]{:S(2)}) collective-permute-start(bf16[32,2048]{1,0:T(8,128)(2,1)S(1)} %get-tuple-element.71), channel_id=1, source_target_pairs={{0,3},{1,0},{2,1},{3,2},{4,7},{5,4},{6,5},{7,6},{8,11},{9,8},{10,9... | collective-permute-start | bytes 393224 | tf_op jit(solution)/shard_map/ppermute | solution.py:487
  98.6 6.5 %copy-start.6 = (f32[2048]{0:T(1024)S(1)}, f32[2048]{0:T(1024)}, u32[]{:S(2)}) copy-start(f32[2048]{0:T(1024)} %param.38) | copy-start | bytes 24580
  98.6 35.1 %all-to-all-start.3 = ((bf16[128,8,1024]{2,1,0:T(8,128)(2,1)}), bf16[128,8,1024]{2,1,0:T(8,128)(2,1)S(1)}, u32[]{:S(2)}, u32[]{:S(2)}) async-start(bf16[128,8,1024]{2,1,0:T(8,128)(2,1)} %bitcast.18), calls=%async_computation.3 | async-start | bytes 4194304 | tf_op jit(solution)/shard_map/all_to_all | solution.py:541

commit v5 on v4

--- a/solution.py
+++ b/solution.py
@@ -15,6 +15,7 @@
 HD = 128
 HEADS = 8
 RUN = 8
+RUN_ORDER = (0, 2, 4, 6, 1, 3, 5, 7)
 VMEM_CAP = 28 * 1024 * 1024
 
 
@@ -75,26 +76,39 @@
     return dotb(jnp.concatenate([ah, al, ah], axis=ca), jnp.concatenate([bh, bh, bl], axis=cb), ca, cb)
 
 
-def rim_kernel(*refs):
-    n = (len(refs) - 2) // 2
-    sources, rim_ref, near_refs, sem = refs[:n], refs[n], refs[n + 1 : -1], refs[-1]
-    copies = [pltpu.make_async_copy(src, dst, sem.at[i]) for i, (src, dst) in enumerate(zip(sources, near_refs))]
+def rim_kernel(qk_hbm, v_hbm, rim_ref, qk_ref, v_ref, sem):
+    tail = pl.ds(L - 8, 8)
+    copies = [
+        pltpu.make_async_copy(qk_hbm.at[tail], qk_ref, sem.at[0]),
+        pltpu.make_async_copy(v_hbm.at[tail], v_ref, sem.at[1]),
+    ]
     for copy in copies:
         copy.start()
-    copies[0].wait()
-    copies[1].wait()
-    qk_ref, v_ref = near_refs[:2]
+    for copy in copies:
+        copy.wait()
     kw = qk_ref.shape[2]
     for z in range(2):
-        rim_ref[:, z * kw : (z + 1) * kw] = qk_ref[L - 8 :, z, :]
-    rim_ref[:, 2 * kw :] = v_ref[L - 8 :]
-    for copy in copies[2:]:
+        rim_ref[:, z * kw : (z + 1) * kw] = qk_ref[:, z, :]
+    rim_ref[:, 2 * kw :] = v_ref[...]
+
+
+def prep_kernel(qk_hbm, v_hbm, cqk_hbm, cv_hbm, decay_hbm, beta_hbm, doc_hbm, conv_ref, edge_ref, within_ref, sys_ref, cols_ref, qk_ref, v_ref, cqk_ref, cv_ref, db_ref, doc_ref, sem):
+    kw = qk_hbm.shape[2]
+    vw = v_hbm.shape[1]
+    pairs = (
+        (doc_hbm, doc_ref),
+        (decay_hbm, db_ref.at[0]),
+        (beta_hbm, db_ref.at[1]),
+        (cqk_hbm, cqk_ref),
+        (cv_hbm, cv_ref),
+        (qk_hbm, qk_ref),
+        (v_hbm, v_ref),
+    )
+    copies = [pltpu.make_async_copy(src, dst, sem.at[i]) for i, (src, dst) in enumerate(pairs)]
+    for copy in copies:
+        copy.start()
+    for copy in copies[:3]:
         copy.wait()
-
-
-def prep_kernel(qk_ref, v_ref, cqk_ref, cv_ref, decay_ref, beta_ref, doc_ref, conv_ref, edge_ref, within_ref, sys_ref, cols_ref):
-    kw = qk_ref.shape[2]
-    vw = v_ref.shape[1]
     me = lax.axis_index("seq")
     cur = doc_ref[pl.ds(me, 1), :]
     prev = doc_ref[pl.ds(jnp.maximum(me - 1, 0), 1), :]
@@ -103,7 +117,7 @@
     prev8 = jnp.broadcast_to(prev, (8, L)).astype(F32)
     lane8 = iota((8, L), 1)
     row8 = iota((8, L), 0)
-    cum = decay_ref[...]
+    cum = db_ref[0]
     for step in (1, 2, 4, 8, 16, 32, 64):
         cum = cum + jnp.where(lane8 >= step, pltpu.roll(cum, step, 1), 0.0)
     flags = (cur8 == prev8[:, L - 1 :]).astype(F32)
@@ -116,7 +130,7 @@
     end_same = cur8 == cur8[:, last:]
     carried = jnp.exp(cum) * (cur8 == prev8[:, last:]).astype(F32)
     ends = jnp.where(end_same, jnp.exp(jnp.where(end_same, cum[:, last:] - cum, 0.0)), 0.0)
-    rows = jnp.concatenate([cum, beta_ref[...], flags, carried, ends, jnp.zeros((L - 40, L), F32)], axis=0)
+    rows = jnp.concatenate([cum, db_ref[1], flags, carried, ends, jnp.zeros((L - 40, L), F32)], axis=0)
     cols = rows.T
     cols_ref[...] = cols
     doc_col = cols[:, 20:21]
@@ -128,6 +142,8 @@
         within = jnp.where(keep, jnp.exp(jnp.where(keep, spread, 0.0)), 0.0)
         within_ref[h] = within
         sys_ref[h] = jnp.where(strict, cols[:, 8 + h : 9 + h] * within, 0.0)
+    for copy in copies[3:]:
+        copy.wait()
 
     def taps(i, at, half):
         if half is None:
@@ -222,8 +238,9 @@
     state = jnp.concatenate([jnp.zeros((HD, HD), F32), (ri == ci).astype(F32)], axis=1)
     for i in range(RUN):
         pq_ref[i] = state
-        trans = maps_ref[i, :HD]
-        offset = maps_ref[i, HD:].astype(F32)
+        at = RUN_ORDER.index(i)
+        trans = maps_ref[at, :HD]
+        offset = maps_ref[at, HD:].astype(F32)
         if i == 0:
             state = jnp.concatenate([offset, trans.astype(F32)], axis=1)
             continue
@@ -239,7 +256,7 @@
     for i in range(RUN):
         hi, lo = split(pq_ref[i, :, HD:])
         moved = dotb(jnp.concatenate([hi, lo], axis=1), ends)
-        start_ref[i] = (pq_ref[i, :, :HD] + moved).astype(BF16)
+        start_ref[RUN_ORDER.index(i)] = (pq_ref[i, :, :HD] + moved).astype(BF16)
 
 
 def project_kernel(out_ref, qe_ref, start_ref, z_ref, gain_ref, w_ref, own_ref, s1_ref, s2_ref, s3_ref, part_ref):
@@ -411,16 +428,15 @@
     shared_gate,
 ):
     seq_n, exp_n = lax.axis_size("seq"), lax.axis_size("exp")
-    runs = [[g * RUN + i for i in range(RUN)] for g in range(seq_n // RUN)]
+    runs = [[g * RUN + i for i in RUN_ORDER] for g in range(seq_n // RUN)]
     kw, vw = qk_proj.shape[2], v_proj.shape[1]
     wide = 2 * kw + vw
-    raw = (qk_proj, v_proj, conv_qk, conv_v, decay_log, beta_gate, doc_ids.reshape(seq_n, L))
-    rim, *held = call(
+    rim = call(
         rim_kernel,
-        (near((8, wide), BF16), *(near(a.shape, a.dtype) for a in raw)),
-        *raw,
-        hbm=range(len(raw)),
-        scratch=[pltpu.SemaphoreType.DMA((len(raw),))],
+        (near((8, wide), BF16),),
+        qk_proj, v_proj,
+        hbm=(0, 1),
+        scratch=[pltpu.VMEM((8, 2, kw), BF16), pltpu.VMEM((8, vw), BF16), pltpu.SemaphoreType.DMA((2,))],
         name="rim",
     )
     halo = lax.ppermute(rim, "seq", [(i, i + 1) for i in range(seq_n - 1)])
@@ -434,7 +450,17 @@
             near((HEADS, L, L), F32),
             near((L, L), F32),
         ),
-        *held,
+        qk_proj, v_proj, conv_qk, conv_v, decay_log, beta_gate, doc_ids.reshape(seq_n, L),
+        hbm=range(7),
+        scratch=[
+            pltpu.VMEM((L, 2, kw), BF16),
+            pltpu.VMEM((L, vw), BF16),
+            pltpu.VMEM(conv_qk.shape, F32),
+            pltpu.VMEM(conv_v.shape, F32),
+            pltpu.VMEM((2, HEADS, L), F32),
+            pltpu.VMEM((seq_n, L), jnp.int32),
+            pltpu.SemaphoreType.DMA((7,)),
+        ],
         flops=10**8,
         name="prep",
     )

time: 135 us -> 135 us (level)
  transfers between devices with their start and end apart: 6 -> 6, of which waited for: 2 -> 3; matrix products, arithmetic and copies ran while one was open for 0% -> 0% of each run, Pallas kernels for 8% -> 9%
where the time goes in v5:
time: 135 us; the launch traced here: 134 us
  blocking collectives  60.7 us (45%)
  Pallas kernels  26.7 us (20%)
  waiting for transfers between devices  26.1 us (19%)
  starting transfers between devices  20.1 us (15%)
    all_to_all x1, blocking collectives, shards(): lax.all_to_all(send.reshape(devices, 8, half), axes, split_axis=0, concat...  36.6 us
    pallas_call x12, Pallas kernels, call(): pl.pallas_call(body, out_shape=[place(o.shape, o.dtype) if place else o f...  26.7 us
    all_to_all x1, waiting for transfers between devices, shards(): lax.all_to_all(made.reshape(devices, 8, half), axes, split_axis=0, concat...  25 us
    all_to_all x1, blocking collectives, shards(): lax.all_to_all(maps, 'seq', split_axis=0, concat_axis=0, tiled=True, axis...  13.5 us
    all_to_all x1, blocking collectives, shards(): lax.all_to_all(starts, 'seq', split_axis=0, concat_axis=0, tiled=True, ax...  10.6 us
    all_to_all x1, starting transfers between devices, shards(): lax.all_to_all(made.reshape(devices, 8, half), axes, split_axis=0, concat...  6.52 us
    ppermute x3, starting transfers between devices, shards(): lax.ppermute(sends[s - 1], 'exp', [(i, (i + s) % exp_n) for i in range(ex...  5.82 us
    ppermute x1, starting transfers between devices, shards(): halo = lax.ppermute(rim, 'seq', [(i, i + 1) for i in range(seq_n - 1)])  4.5 us
  transfers between devices with their start and end apart: 6, of which 3 were waited for; matrix products, arithmetic and copies ran while one was open for 0% of the time, Pallas kernels for 9%

profile of v5, /device:TPU:1, one launch (start us, length us, event | category | flops | bytes accessed | tf_op | source)
XLA Modules:
  0.0 134.4 jit_solution(13488444451665997315)
XLA Ops:
  0.6 0.8 rim.1
  1.4 4.5 %collective-permute-start = (bf16[8,2048]{1,0:T(8,128)(2,1)S(1)}, bf16[8,2048]{1,0:T(8,128)(2,1)S(1)}, u32[]{:S(2)}, u32[]{:S(2)}) collective-permute-start(bf16[8,2048]{1,0:T(8,128)(2,1)S(1)} %rim.1), channel_id=1, source_target_pairs={{0,4},{4,8},{8,12},{12,16},{16,20},{20,24},{24,28},{28,32},{32,36}... | collective-permute-start | bytes 98312 | tf_op jit(solution)/shard_map/ppermute | solution.py:442
  5.9 3.0 %prep.1 = (f32[128,2048]{1,0:T(8,128)S(1)}, f32[16,2048]{1,0:T(8,128)S(1)}, f32[8,128,128]{2,1,0:T(8,128)S(1)}, f32[8,128,128]{2,1,0:T(8,128)S(1)}, f32[128,128]{1,0:T(8,128)S(1)}) custom-call(bf16[128,2,512]{2,1,0:T(2,128)(2,1)} %qk_hbm.3, bf16[128,1024]{1,0:T(8,128)(2,1)} %v_hbm.3, f32[4,2,512]{2,1,0:T(2,128)} %cqk_hbm.1, f32[4,1024]{1,0:T(4,128)} %cv_hbm.1, ...), custom_call_target="tpu_custom_call" | custom-call | flops 100000000 | bytes 581632 | tf_op jit(solution)/shard_map/prep/pallas_call | solution.py:44
  8.9 0.0 collective-permute-done.halo_ref
  8.9 3.7 %maps.1 = (bf16[8,256,128]{2,1,0:T(8,128)(2,1)S(1)}, f32[8,128,128]{2,1,0:T(8,128)S(1)}, f32[8,128,256]{2,1,0:T(8,128)S(1)}, f32[8,128,128]{2,1,0:T(8,128)S(1)}) custom-call(f32[128,2048]{1,0:T(8,128)S(1)} %get-tuple-element.33.conv_ref, f32[16,2048]{1,0:T(8,128)S(1)} %get-tuple-element.34.edge_ref, bf16[8,2048]{1,0:T(8,128)(2,1)S(1)} %collective-permute-done.halo_ref, ...), custom_call_target="tpu_custom_call" | custom-call | flops 2000000000 | bytes 2326528 | tf_op jit(solution)/shard_map/maps/pallas_call | solution.py:44
  12.6 0.0 copy-start
  12.6 0.0 copy-start.1
  12.6 0.0 copy-start.8
  12.6 13.5 %all_to_all.20.maps_ref = bf16[8,256,128]{2,1,0:T(8,128)(2,1)S(1)} all-to-all(bf16[8,256,128]{2,1,0:T(8,128)(2,1)S(1)} %get-tuple-element.38), channel_id=1, replica_groups={{0,8,16,24,4,12,20,28},{32,40,48,56,36,44,52,60},{64,72,80,88,68,76,84,..., dimensions={0} | all-to-all | bytes 1048576 | tf_op jit(solution)/shard_map/all_to_all | solution.py:479
  26.2 1.2 chain.1
  27.3 3.2 %collective-permute-start.1 = (bf16[128,128]{1,0:T(8,128)(2,1)S(1)}, bf16[128,128]{1,0:T(8,128)(2,1)S(1)}, u32[]{:S(2)}, u32[]{:S(2)}) collective-permute-start(bf16[128,128]{1,0:T(8,128)(2,1)S(1)} %get-tuple-element.39), channel_id=1, source_target_pairs={{0,32},{4,36},{8,40},{12,44},{16,48},{20,52},{24,56},{28,60},{32,6... | collective-permute-start | bytes 98312 | tf_op jit(solution)/shard_map/ppermute | solution.py:494
  30.6 0.5 local_out.1
  31.0 0.5 collective-permute-done.1.end_ref
  31.6 0.3 starts.1
  31.9 10.6 %all_to_all.21.start_ref = bf16[8,128,128]{2,1,0:T(8,128)(2,1)S(1)} all-to-all(bf16[8,128,128]{2,1,0:T(8,128)(2,1)S(1)} %starts.1), channel_id=1, replica_groups={{0,8,16,24,4,12,20,28},{32,40,48,56,36,44,52,60},{64,72,80,88,68,76,84,..., dimensions={0} | all-to-all | bytes 524288 | tf_op jit(solution)/shard_map/all_to_all | solution.py:497
  42.5 1.1 project.1
  43.6 1.7 %collective-permute-start.2 = (bf16[32,2048]{1,0:T(8,128)(2,1)S(1)}, bf16[32,2048]{1,0:T(8,128)(2,1)S(1)}, u32[]{:S(2)}, u32[]{:S(2)}) collective-permute-start(bf16[32,2048]{1,0:T(8,128)(2,1)S(1)} %get-tuple-element.53), channel_id=1, source_target_pairs={{0,1},{1,2},{2,3},{3,0},{4,5},{5,6},{6,7},{7,4},{8,9},{9,10},{10,1... | collective-permute-start | bytes 393224 | tf_op jit(solution)/shard_map/ppermute | solution.py:513
  45.3 3.3 %collective-permute-start.3 = (bf16[32,2048]{1,0:T(8,128)(2,1)S(1)}, bf16[32,2048]{1,0:T(8,128)(2,1)S(1)}, u32[]{:S(2)}, u32[]{:S(2)}) collective-permute-start(bf16[32,2048]{1,0:T(8,128)(2,1)S(1)} %get-tuple-element.54), channel_id=1, source_target_pairs={{0,2},{1,3},{2,0},{3,1},{4,6},{5,7},{6,4},{7,5},{8,10},{9,11},{10,... | collective-permute-start | bytes 393224 | tf_op jit(solution)/shard_map/ppermute | solution.py:513
  48.6 0.0 copy-start.7
  48.6 0.8 collective-permute-start.4
  49.5 4.7 %fetch.1 = (bf16[2,2,2048,512]{3,2,1,0:T(8,128)(2,1)S(1)}, bf16[2,512,2048]{2,1,0:T(8,128)(2,1)S(1)}) custom-call(bf16[2,2,2048,512]{3,2,1,0:T(8,128)(2,1)} %gu_hbm.1, bf16[2,512,2048]{2,1,0:T(8,128)(2,1)} %down_hbm.1), custom_call_target="tpu_custom_call" | custom-call | bytes 12582912 | tf_op jit(solution)/shard_map/fetch/pallas_call | solution.py:44
  54.2 0.0 collective-permute-done.2.r1_ref
  54.2 0.5 collective-permute-done.3.r2_ref
  54.7 0.0 collective-permute-done.4.r3_ref
  54.7 1.3 route.1
  56.0 36.6 %all_to_all.22 = bf16[128,8,1024]{2,1,0:T(8,128)(2,1)S(1)} all-to-all(bf16[128,8,1024]{2,1,0:T(8,128)(2,1)S(1)} %bitcast.12), channel_id=1, replica_groups={{0,1,2,3,8,9,10,11,16,17,18,19,24,25,26,27,32,33,34,35,40,41,42,43,48,4..., dimensions={0} | all-to-all | bytes 4194304 | tf_op jit(solution)/shard_map/all_to_all | solution.py:537
  92.6 5.6 %experts.1 = bf16[1024,1024]{1,0:T(8,128)(2,1)} custom-call(bf16[1024,1024]{1,0:T(8,128)(2,1)S(1)} %bitcast.11, bf16[2,2,2048,512]{3,2,1,0:T(8,128)(2,1)S(1)} %get-tuple-element.58.gu_ref, bf16[2,512,2048]{2,1,0:T(8,128)(2,1)S(1)} %get-tuple-element.59.down_ref), custom_call_target="tpu_custom_call" | custom-call | flops 4000000000 | bytes 14680064 | tf_op jit(solution)/shard_map/experts/pallas_call | solution.py:44
  98.2 0.0 copy-start.6
  98.2 6.5 %all-to-all-start.3 = ((bf16[128,8,1024]{2,1,0:T(8,128)(2,1)}), bf16[128,8,1024]{2,1,0:T(8,128)(2,1)S(1)}, u32[]{:S(2)}, u32[]{:S(2)}) async-start(bf16[128,8,1024]{2,1,0:T(8,128)(2,1)} %bitcast.18), calls=%async_computation.3 | async-start | bytes 4194304 | tf_op jit(solution)/shard_map/all_to_all | solution.py:567
  104.7 3.5 %shared.1.shared_ref = f32[32,2048]{1,0:T(8,128)S(1)} custom-call(bf16[32,2048]{1,0:T(8,128)(2,1)S(1)} %get-tuple-element.63.norm_ref, f32[1,2048]{1,0:T(1,128)S(1)} %bitcast.16, bf16[2,2048,512]{2,1,0:T(8,128)(2,1)} %sgu_hbm.1, bf16[512,2048]{1,0:T(8,128)(2,1)} %sdown_hbm.1), custom_call_target="tpu_custom_call" | custom-call | flops 200000000 | bytes 6430720 | tf_op jit(solution)/shard_map/shared/pallas_call | solution.py:44
  108.3 25.0 %all-to-all-done.3 = bf16[128,8,1024]{2,1,0:T(8,128)(2,1)S(1)} async-done(((bf16[128,8,1024]{2,1,0:T(8,128)(2,1)}), bf16[128,8,1024]{2,1,0:T(8,128)(2,1)S(1)}, u32[]{:S(2)}, u32[]{:S(2)}) %all-to-all-start.3) | async-done | bytes 2097184 | tf_op jit(solution)/shard_map/all_to_all | solution.py:567
  133.3 1.1 combine.1
  (13 shorter events, 0.0 us)
Async XLA Ops:
  1.4 7.5 %collective-permute-start = (bf16[8,2048]{1,0:T(8,128)(2,1)S(1)}, bf16[8,2048]{1,0:T(8,128)(2,1)S(1)}, u32[]{:S(2)}, u32[]{:S(2)}) collective-permute-start(bf16[8,2048]{1,0:T(8,128)(2,1)S(1)} %rim.1), channel_id=1, source_target_pairs={{0,4},{4,8},{8,12},{12,16},{16,20},{20,24},{24,28},{28,32},{32,36}... | collective-permute-start | bytes 98312 | tf_op jit(solution)/shard_map/ppermute | solution.py:442
  12.6 29.9 %copy-start = (bf16[1024,2048]{1,0:T(8,128)(2,1)S(1)}, bf16[1024,2048]{1,0:T(8,128)(2,1)}, u32[]{:S(2)}) copy-start(bf16[1024,2048]{1,0:T(8,128)(2,1)} %w_ref.1) | copy-start | bytes 12582916
  12.6 29.9 %copy-start.1 = (bf16[128,1024]{1,0:T(8,128)(2,1)S(1)}, bf16[128,1024]{1,0:T(8,128)(2,1)}, u32[]{:S(2)}) copy-start(bf16[128,1024]{1,0:T(8,128)(2,1)} %z_ref.1) | copy-start | bytes 786436
  12.6 29.9 %copy-start.8 = (f32[128]{0:T(128)S(1)}, f32[128]{0:T(128)}, u32[]{:S(2)}) copy-start(f32[128]{0:T(128)} %param.28) | copy-start | bytes 1540
  27.3 4.2 %collective-permute-start.1 = (bf16[128,128]{1,0:T(8,128)(2,1)S(1)}, bf16[128,128]{1,0:T(8,128)(2,1)S(1)}, u32[]{:S(2)}, u32[]{:S(2)}) collective-permute-start(bf16[128,128]{1,0:T(8,128)(2,1)S(1)} %get-tuple-element.39), channel_id=1, source_target_pairs={{0,32},{4,36},{8,40},{12,44},{16,48},{20,52},{24,56},{28,60},{32,6... | collective-permute-start | bytes 98312 | tf_op jit(solution)/shard_map/ppermute | solution.py:494
  43.6 10.6 %collective-permute-start.2 = (bf16[32,2048]{1,0:T(8,128)(2,1)S(1)}, bf16[32,2048]{1,0:T(8,128)(2,1)S(1)}, u32[]{:S(2)}, u32[]{:S(2)}) collective-permute-start(bf16[32,2048]{1,0:T(8,128)(2,1)S(1)} %get-tuple-element.53), channel_id=1, source_target_pairs={{0,1},{1,2},{2,3},{3,0},{4,5},{5,6},{6,7},{7,4},{8,9},{9,10},{10,1... | collective-permute-start | bytes 393224 | tf_op jit(solution)/shard_map/ppermute | solution.py:513
  45.3 9.4 %collective-permute-start.3 = (bf16[32,2048]{1,0:T(8,128)(2,1)S(1)}, bf16[32,2048]{1,0:T(8,128)(2,1)S(1)}, u32[]{:S(2)}, u32[]{:S(2)}) collective-permute-start(bf16[32,2048]{1,0:T(8,128)(2,1)S(1)} %get-tuple-element.54), channel_id=1, source_target_pairs={{0,2},{1,3},{2,0},{3,1},{4,6},{5,7},{6,4},{7,5},{8,10},{9,11},{10,... | collective-permute-start | bytes 393224 | tf_op jit(solution)/shard_map/ppermute | solution.py:513
  48.6 6.1 %copy-start.2 = (bf16[32,2048]{1,0:T(8,128)(2,1)S(1)}, bf16[32,2048]{1,0:T(8,128)(2,1)}, u32[]{:S(2)}) copy-start(bf16[32,2048]{1,0:T(8,128)(2,1)} %res_ref.1) | copy-start | bytes 393220
  48.6 6.1 %copy-start.3 = (f32[2048]{0:T(1024)S(1)}, f32[2048]{0:T(1024)}, u32[]{:S(2)}) copy-start(f32[2048]{0:T(1024)} %param.31) | copy-start | bytes 24580
  48.6 6.1 %copy-start.4 = (s32[32,10]{0,1:T(8,128)S(1)}, s32[32,10]{0,1:T(8,128)}, u32[]{:S(2)}) copy-start(s32[32,10]{0,1:T(8,128)} %param.32) | copy-start | bytes 3844
  48.6 6.1 %copy-start.5 = (f32[32,10]{0,1:T(8,128)S(1)}, f32[32,10]{0,1:T(8,128)}, u32[]{:S(2)}) copy-start(f32[32,10]{0,1:T(8,128)} %param.33) | copy-start | bytes 3844
  48.6 6.1 %copy-start.7 = (s32[1,1024]{1,0:T(1,128)S(1)}, s32[1,1024]{1,0:T(1,128)}, u32[]{:S(2)}) copy-start(s32[1,1024]{1,0:T(1,128)} %constant.2.clone.to_ref) | copy-start | bytes 12292
  48.6 6.0 %collective-permute-start.4 = (bf16[32,2048]{1,0:T(8,128)(2,1)S(1)}, bf16[32,2048]{1,0:T(8,128)(2,1)S(1)}, u32[]{:S(2)}, u32[]{:S(2)}) collective-permute-start(bf16[32,2048]{1,0:T(8,128)(2,1)S(1)} %get-tuple-element.55), channel_id=1, source_target_pairs={{0,3},{1,0},{2,1},{3,2},{4,7},{5,4},{6,5},{7,6},{8,11},{9,8},{10,9... | collective-permute-start | bytes 393224 | tf_op jit(solution)/shard_map/ppermute | solution.py:513
  98.2 6.5 %copy-start.6 = (f32[2048]{0:T(1024)S(1)}, f32[2048]{0:T(1024)}, u32[]{:S(2)}) copy-start(f32[2048]{0:T(1024)} %param.38) | copy-start | bytes 24580
  98.2 35.1 %all-to-all-start.3 = ((bf16[128,8,1024]{2,1,0:T(8,128)(2,1)}), bf16[128,8,1024]{2,1,0:T(8,128)(2,1)S(1)}, u32[]{:S(2)}, u32[]{:S(2)}) async-start(bf16[128,8,1024]{2,1,0:T(8,128)(2,1)} %bitcast.18), calls=%async_computation.3 | async-start | bytes 4194304 | tf_op jit(solution)/shard_map/all_to_all | solution.py:567

commit v6 on v5

--- a/solution.py
+++ b/solution.py
@@ -219,7 +219,7 @@
         uw_ref[h] = uw
         sc_ref[h] = qk[h // 2] * within_ref[h]
         cq_ref[h] = carried * q_heads[h // 2]
-        ends = dot3(cols[:, 32 + h : 33 + h] * kj, uw, 0, 0)
+        ends = dotb((cols[:, 32 + h : 33 + h] * kj).astype(BF16), uw.astype(BF16), 0, 0)
         maps_ref[h, :L] = (carried[L - 1 :] * eye - ends[:, HD:]).astype(BF16)
         maps_ref[h, L:] = ends[:, :HD].astype(BF16)
 

time: 135 us -> 136 us (level)
  no operation moved by 1% of the time
where the time goes in v6:
time: 136 us; the launch traced here: 135 us
  blocking collectives  60.7 us (45%)
  Pallas kernels  27.5 us (20%)
  waiting for transfers between devices  26.1 us (19%)
  starting transfers between devices  20 us (15%)
    all_to_all x1, blocking collectives, shards(): lax.all_to_all(send.reshape(devices, 8, half), axes, split_axis=0, concat...  36.6 us
    pallas_call x12, Pallas kernels, call(): pl.pallas_call(body, out_shape=[place(o.shape, o.dtype) if place else o f...  27.5 us
    all_to_all x1, waiting for transfers between devices, shards(): lax.all_to_all(made.reshape(devices, 8, half), axes, split_axis=0, concat...  25 us
    all_to_all x1, blocking collectives, shards(): lax.all_to_all(maps, 'seq', split_axis=0, concat_axis=0, tiled=True, axis...  13.5 us
    all_to_all x1, blocking collectives, shards(): lax.all_to_all(starts, 'seq', split_axis=0, concat_axis=0, tiled=True, ax...  10.6 us
    all_to_all x1, starting transfers between devices, shards(): lax.all_to_all(made.reshape(devices, 8, half), axes, split_axis=0, concat...  6.52 us
    ppermute x3, starting transfers between devices, shards(): lax.ppermute(sends[s - 1], 'exp', [(i, (i + s) % exp_n) for i in range(ex...  5.8 us
    ppermute x1, starting transfers between devices, shards(): halo = lax.ppermute(rim, 'seq', [(i, i + 1) for i in range(seq_n - 1)])  4.5 us
  transfers between devices with their start and end apart: 6, of which 3 were waited for; matrix products, arithmetic and copies ran while one was open for 0% of the time, Pallas kernels for 9%

profile of v6, /device:TPU:1, one launch (start us, length us, event | category | flops | bytes accessed | tf_op | source)
XLA Modules:
  0.0 135.1 jit_solution(1545866742234223608)
XLA Ops:
  0.6 0.8 rim.1
  1.4 4.5 %collective-permute-start = (bf16[8,2048]{1,0:T(8,128)(2,1)S(1)}, bf16[8,2048]{1,0:T(8,128)(2,1)S(1)}, u32[]{:S(2)}, u32[]{:S(2)}) collective-permute-start(bf16[8,2048]{1,0:T(8,128)(2,1)S(1)} %rim.1), channel_id=1, source_target_pairs={{0,4},{4,8},{8,12},{12,16},{16,20},{20,24},{24,28},{28,32},{32,36}... | collective-permute-start | bytes 98312 | tf_op jit(solution)/shard_map/ppermute | solution.py:442
  5.9 3.0 %prep.1 = (f32[128,2048]{1,0:T(8,128)S(1)}, f32[16,2048]{1,0:T(8,128)S(1)}, f32[8,128,128]{2,1,0:T(8,128)S(1)}, f32[8,128,128]{2,1,0:T(8,128)S(1)}, f32[128,128]{1,0:T(8,128)S(1)}) custom-call(bf16[128,2,512]{2,1,0:T(2,128)(2,1)} %qk_hbm.3, bf16[128,1024]{1,0:T(8,128)(2,1)} %v_hbm.3, f32[4,2,512]{2,1,0:T(2,128)} %cqk_hbm.1, f32[4,1024]{1,0:T(4,128)} %cv_hbm.1, ...), custom_call_target="tpu_custom_call" | custom-call | flops 100000000 | bytes 581632 | tf_op jit(solution)/shard_map/prep/pallas_call | solution.py:44
  8.9 0.0 collective-permute-done.halo_ref
  8.9 4.4 %maps.1 = (bf16[8,256,128]{2,1,0:T(8,128)(2,1)S(1)}, f32[8,128,128]{2,1,0:T(8,128)S(1)}, f32[8,128,256]{2,1,0:T(8,128)S(1)}, f32[8,128,128]{2,1,0:T(8,128)S(1)}) custom-call(f32[128,2048]{1,0:T(8,128)S(1)} %get-tuple-element.33.conv_ref, f32[16,2048]{1,0:T(8,128)S(1)} %get-tuple-element.34.edge_ref, bf16[8,2048]{1,0:T(8,128)(2,1)S(1)} %collective-permute-done.halo_ref, ...), custom_call_target="tpu_custom_call" | custom-call | flops 2000000000 | bytes 2326528 | tf_op jit(solution)/shard_map/maps/pallas_call | solution.py:44
  13.4 0.0 copy-start
  13.4 0.0 copy-start.1
  13.4 0.0 copy-start.8
  13.4 13.5 %all_to_all.20.maps_ref = bf16[8,256,128]{2,1,0:T(8,128)(2,1)S(1)} all-to-all(bf16[8,256,128]{2,1,0:T(8,128)(2,1)S(1)} %get-tuple-element.38), channel_id=1, replica_groups={{0,8,16,24,4,12,20,28},{32,40,48,56,36,44,52,60},{64,72,80,88,68,76,84,..., dimensions={0} | all-to-all | bytes 1048576 | tf_op jit(solution)/shard_map/all_to_all | solution.py:479
  26.9 1.2 chain.1
  28.1 3.2 %collective-permute-start.1 = (bf16[128,128]{1,0:T(8,128)(2,1)S(1)}, bf16[128,128]{1,0:T(8,128)(2,1)S(1)}, u32[]{:S(2)}, u32[]{:S(2)}) collective-permute-start(bf16[128,128]{1,0:T(8,128)(2,1)S(1)} %get-tuple-element.39), channel_id=1, source_target_pairs={{0,32},{4,36},{8,40},{12,44},{16,48},{20,52},{24,56},{28,60},{32,6... | collective-permute-start | bytes 98312 | tf_op jit(solution)/shard_map/ppermute | solution.py:494
  31.3 0.5 local_out.1
  31.8 0.5 collective-permute-done.1.end_ref
  32.3 0.3 starts.1
  32.6 10.6 %all_to_all.21.start_ref = bf16[8,128,128]{2,1,0:T(8,128)(2,1)S(1)} all-to-all(bf16[8,128,128]{2,1,0:T(8,128)(2,1)S(1)} %starts.1), channel_id=1, replica_groups={{0,8,16,24,4,12,20,28},{32,40,48,56,36,44,52,60},{64,72,80,88,68,76,84,..., dimensions={0} | all-to-all | bytes 524288 | tf_op jit(solution)/shard_map/all_to_all | solution.py:497
  43.2 1.1 project.1
  44.4 1.7 %collective-permute-start.2 = (bf16[32,2048]{1,0:T(8,128)(2,1)S(1)}, bf16[32,2048]{1,0:T(8,128)(2,1)S(1)}, u32[]{:S(2)}, u32[]{:S(2)}) collective-permute-start(bf16[32,2048]{1,0:T(8,128)(2,1)S(1)} %get-tuple-element.53), channel_id=1, source_target_pairs={{0,1},{1,2},{2,3},{3,0},{4,5},{5,6},{6,7},{7,4},{8,9},{9,10},{10,1... | collective-permute-start | bytes 393224 | tf_op jit(solution)/shard_map/ppermute | solution.py:513
  46.1 3.3 %collective-permute-start.3 = (bf16[32,2048]{1,0:T(8,128)(2,1)S(1)}, bf16[32,2048]{1,0:T(8,128)(2,1)S(1)}, u32[]{:S(2)}, u32[]{:S(2)}) collective-permute-start(bf16[32,2048]{1,0:T(8,128)(2,1)S(1)} %get-tuple-element.54), channel_id=1, source_target_pairs={{0,2},{1,3},{2,0},{3,1},{4,6},{5,7},{6,4},{7,5},{8,10},{9,11},{10,... | collective-permute-start | bytes 393224 | tf_op jit(solution)/shard_map/ppermute | solution.py:513
  49.4 0.0 copy-start.7
  49.4 0.8 collective-permute-start.4
  50.2 4.7 %fetch.1 = (bf16[2,2,2048,512]{3,2,1,0:T(8,128)(2,1)S(1)}, bf16[2,512,2048]{2,1,0:T(8,128)(2,1)S(1)}) custom-call(bf16[2,2,2048,512]{3,2,1,0:T(8,128)(2,1)} %gu_hbm.1, bf16[2,512,2048]{2,1,0:T(8,128)(2,1)} %down_hbm.1), custom_call_target="tpu_custom_call" | custom-call | bytes 12582912 | tf_op jit(solution)/shard_map/fetch/pallas_call | solution.py:44
  54.9 0.0 collective-permute-done.2.r1_ref
  54.9 0.5 collective-permute-done.3.r2_ref
  55.4 0.0 collective-permute-done.4.r3_ref
  55.5 1.3 route.1
  56.8 36.6 %all_to_all.22 = bf16[128,8,1024]{2,1,0:T(8,128)(2,1)S(1)} all-to-all(bf16[128,8,1024]{2,1,0:T(8,128)(2,1)S(1)} %bitcast.12), channel_id=1, replica_groups={{0,1,2,3,8,9,10,11,16,17,18,19,24,25,26,27,32,33,34,35,40,41,42,43,48,4..., dimensions={0} | all-to-all | bytes 4194304 | tf_op jit(solution)/shard_map/all_to_all | solution.py:537
  93.3 5.6 %experts.1 = bf16[1024,1024]{1,0:T(8,128)(2,1)} custom-call(bf16[1024,1024]{1,0:T(8,128)(2,1)S(1)} %bitcast.11, bf16[2,2,2048,512]{3,2,1,0:T(8,128)(2,1)S(1)} %get-tuple-element.58.gu_ref, bf16[2,512,2048]{2,1,0:T(8,128)(2,1)S(1)} %get-tuple-element.59.down_ref), custom_call_target="tpu_custom_call" | custom-call | flops 4000000000 | bytes 14680064 | tf_op jit(solution)/shard_map/experts/pallas_call | solution.py:44
  98.9 0.0 copy-start.6
  99.0 6.5 %all-to-all-start.3 = ((bf16[128,8,1024]{2,1,0:T(8,128)(2,1)}), bf16[128,8,1024]{2,1,0:T(8,128)(2,1)S(1)}, u32[]{:S(2)}, u32[]{:S(2)}) async-start(bf16[128,8,1024]{2,1,0:T(8,128)(2,1)} %bitcast.18), calls=%async_computation.3 | async-start | bytes 4194304 | tf_op jit(solution)/shard_map/all_to_all | solution.py:567
  105.5 3.5 %shared.1.shared_ref = f32[32,2048]{1,0:T(8,128)S(1)} custom-call(bf16[32,2048]{1,0:T(8,128)(2,1)S(1)} %get-tuple-element.63.norm_ref, f32[1,2048]{1,0:T(1,128)S(1)} %bitcast.16, bf16[2,2048,512]{2,1,0:T(8,128)(2,1)} %sgu_hbm.1, bf16[512,2048]{1,0:T(8,128)(2,1)} %sdown_hbm.1), custom_call_target="tpu_custom_call" | custom-call | flops 200000000 | bytes 6430720 | tf_op jit(solution)/shard_map/shared/pallas_call | solution.py:44
  109.0 25.0 %all-to-all-done.3 = bf16[128,8,1024]{2,1,0:T(8,128)(2,1)S(1)} async-done(((bf16[128,8,1024]{2,1,0:T(8,128)(2,1)}), bf16[128,8,1024]{2,1,0:T(8,128)(2,1)S(1)}, u32[]{:S(2)}, u32[]{:S(2)}) %all-to-all-start.3) | async-done | bytes 2097184 | tf_op jit(solution)/shard_map/all_to_all | solution.py:567
  134.0 1.1 combine.1
  (13 shorter events, 0.0 us)
Async XLA Ops:
  1.4 7.5 %collective-permute-start = (bf16[8,2048]{1,0:T(8,128)(2,1)S(1)}, bf16[8,2048]{1,0:T(8,128)(2,1)S(1)}, u32[]{:S(2)}, u32[]{:S(2)}) collective-permute-start(bf16[8,2048]{1,0:T(8,128)(2,1)S(1)} %rim.1), channel_id=1, source_target_pairs={{0,4},{4,8},{8,12},{12,16},{16,20},{20,24},{24,28},{28,32},{32,36}... | collective-permute-start | bytes 98312 | tf_op jit(solution)/shard_map/ppermute | solution.py:442
  13.4 29.9 %copy-start = (bf16[1024,2048]{1,0:T(8,128)(2,1)S(1)}, bf16[1024,2048]{1,0:T(8,128)(2,1)}, u32[]{:S(2)}) copy-start(bf16[1024,2048]{1,0:T(8,128)(2,1)} %w_ref.1) | copy-start | bytes 12582916
  13.4 29.9 %copy-start.1 = (bf16[128,1024]{1,0:T(8,128)(2,1)S(1)}, bf16[128,1024]{1,0:T(8,128)(2,1)}, u32[]{:S(2)}) copy-start(bf16[128,1024]{1,0:T(8,128)(2,1)} %z_ref.1) | copy-start | bytes 786436
  13.4 29.8 %copy-start.8 = (f32[128]{0:T(128)S(1)}, f32[128]{0:T(128)}, u32[]{:S(2)}) copy-start(f32[128]{0:T(128)} %param.28) | copy-start | bytes 1540
  28.1 4.2 %collective-permute-start.1 = (bf16[128,128]{1,0:T(8,128)(2,1)S(1)}, bf16[128,128]{1,0:T(8,128)(2,1)S(1)}, u32[]{:S(2)}, u32[]{:S(2)}) collective-permute-start(bf16[128,128]{1,0:T(8,128)(2,1)S(1)} %get-tuple-element.39), channel_id=1, source_target_pairs={{0,32},{4,36},{8,40},{12,44},{16,48},{20,52},{24,56},{28,60},{32,6... | collective-permute-start | bytes 98312 | tf_op jit(solution)/shard_map/ppermute | solution.py:494
  44.4 10.5 %collective-permute-start.2 = (bf16[32,2048]{1,0:T(8,128)(2,1)S(1)}, bf16[32,2048]{1,0:T(8,128)(2,1)S(1)}, u32[]{:S(2)}, u32[]{:S(2)}) collective-permute-start(bf16[32,2048]{1,0:T(8,128)(2,1)S(1)} %get-tuple-element.53), channel_id=1, source_target_pairs={{0,1},{1,2},{2,3},{3,0},{4,5},{5,6},{6,7},{7,4},{8,9},{9,10},{10,1... | collective-permute-start | bytes 393224 | tf_op jit(solution)/shard_map/ppermute | solution.py:513
  46.1 9.4 %collective-permute-start.3 = (bf16[32,2048]{1,0:T(8,128)(2,1)S(1)}, bf16[32,2048]{1,0:T(8,128)(2,1)S(1)}, u32[]{:S(2)}, u32[]{:S(2)}) collective-permute-start(bf16[32,2048]{1,0:T(8,128)(2,1)S(1)} %get-tuple-element.54), channel_id=1, source_target_pairs={{0,2},{1,3},{2,0},{3,1},{4,6},{5,7},{6,4},{7,5},{8,10},{9,11},{10,... | collective-permute-start | bytes 393224 | tf_op jit(solution)/shard_map/ppermute | solution.py:513
  49.4 6.1 %copy-start.2 = (bf16[32,2048]{1,0:T(8,128)(2,1)S(1)}, bf16[32,2048]{1,0:T(8,128)(2,1)}, u32[]{:S(2)}) copy-start(bf16[32,2048]{1,0:T(8,128)(2,1)} %res_ref.1) | copy-start | bytes 393220
  49.4 6.1 %copy-start.3 = (f32[2048]{0:T(1024)S(1)}, f32[2048]{0:T(1024)}, u32[]{:S(2)}) copy-start(f32[2048]{0:T(1024)} %param.31) | copy-start | bytes 24580
  49.4 6.1 %copy-start.4 = (s32[32,10]{0,1:T(8,128)S(1)}, s32[32,10]{0,1:T(8,128)}, u32[]{:S(2)}) copy-start(s32[32,10]{0,1:T(8,128)} %param.32) | copy-start | bytes 3844
  49.4 6.1 %copy-start.5 = (f32[32,10]{0,1:T(8,128)S(1)}, f32[32,10]{0,1:T(8,128)}, u32[]{:S(2)}) copy-start(f32[32,10]{0,1:T(8,128)} %param.33) | copy-start | bytes 3844
  49.4 6.1 %copy-start.7 = (s32[1,1024]{1,0:T(1,128)S(1)}, s32[1,1024]{1,0:T(1,128)}, u32[]{:S(2)}) copy-start(s32[1,1024]{1,0:T(1,128)} %constant.2.clone.to_ref) | copy-start | bytes 12292
  49.4 6.0 %collective-permute-start.4 = (bf16[32,2048]{1,0:T(8,128)(2,1)S(1)}, bf16[32,2048]{1,0:T(8,128)(2,1)S(1)}, u32[]{:S(2)}, u32[]{:S(2)}) collective-permute-start(bf16[32,2048]{1,0:T(8,128)(2,1)S(1)} %get-tuple-element.55), channel_id=1, source_target_pairs={{0,3},{1,0},{2,1},{3,2},{4,7},{5,4},{6,5},{7,6},{8,11},{9,8},{10,9... | collective-permute-start | bytes 393224 | tf_op jit(solution)/shard_map/ppermute | solution.py:513
  98.9 6.5 %copy-start.6 = (f32[2048]{0:T(1024)S(1)}, f32[2048]{0:T(1024)}, u32[]{:S(2)}) copy-start(f32[2048]{0:T(1024)} %param.38) | copy-start | bytes 24580
  99.0 35.1 %all-to-all-start.3 = ((bf16[128,8,1024]{2,1,0:T(8,128)(2,1)}), bf16[128,8,1024]{2,1,0:T(8,128)(2,1)S(1)}, u32[]{:S(2)}, u32[]{:S(2)}) async-start(bf16[128,8,1024]{2,1,0:T(8,128)(2,1)} %bitcast.18), calls=%async_computation.3 | async-start | bytes 4194304 | tf_op jit(solution)/shard_map/all_to_all | solution.py:567
